TPU v7x, 256 devices: a whole 4x4x8 slice. The times are simulated.
256 devices in a mesh: region: 16 (over z, core), layer: 16 (over x, y).
Axes of the slice: x: 4, y: 4, z: 8, core: 2. Of those that a mesh axis runs over, the one named last changes fastest.
Arguments:
- right_side: float32 [64, 1048576], P(None, ('region', 'layer')), may hold values from -72 to 72
- block_entries: float32 [16384, 7, 4096], P(('region', 'layer')), may hold values from -0.01875 to 2.01875, as said below
- neighbours: int32 [16384, 6], P(('region', 'layer')), may hold values from 0 to 95
- face_rows: int32 [1024, 8], P(('region', 'layer')), may hold values from 0 to 63
- die_owner: int32 [131072, 1], P(('region', 'layer')), may hold values from 0 to 15; in each aligned block of 512 rows (0 to 511, 512 to 1023, ...) at most 128 rows name the same one
- die_node: int32 [131072], P(('region', 'layer')), may hold values from 0 to 4095
Outputs:
- solution_field: float32 [64, 1048576], P(None, ('region', 'layer'))
- residual: float32 [64, 1048576], P(None, ('region', 'layer'))
- mech_temps: float32 [4096, 8192], P(('region', 'layer'))
Inputs may be any that keep to these rules, and one draw needn't show every extreme that they name: `block_entries`: dense blocks of the conduction operator: the diagonal block of each block row carries the node's own coupling on its diagonal. `die_owner`: among the 512 rows of one device, at most 128 name the same owner, and in some devices exactly 128 do.
All inputs are finite; a program needn't handle non-finite values.
Results may differ from a plain program's by a relative error of at most 0.0003.
Values sent between devices are 32-bit elements; how exact they have to be, the bound alone decides.
No kernel may reach another device: no remote copies, remote signals or barrier semaphores. Data moves between devices by JAX's collectives and lax.ppermute only.
A program may use at most 128 MiB of HBM per device.

v0:
```python
import jax
import jax.numpy as jnp
from jax import lax
from jax.sharding import PartitionSpec as P

BLOCK = 64
RHS = 64
COUPLED = 7
BLK_DEV = 64
SLOTS = 128
FACES = 8


def partner(shard, axis, bit):
    return lax.ppermute(shard, axis, [(i, i ^ 1 << bit) for i in range(lax.axis_size(axis))])


def with_halo(cells, sides, width):
    for axis, dim in sides:
        count = lax.axis_size(axis)
        ends = count - 1
        head = lax.slice_in_dim(cells, 0, width, axis=dim)
        tail = lax.slice_in_dim(cells, cells.shape[dim] - width, cells.shape[dim], axis=dim)
        cells = jnp.concatenate(
            [
                lax.ppermute(tail, axis, [(i, (i + 1) % count) for i in range(ends)]),
                cells,
                lax.ppermute(head, axis, [((i + 1) % count, i) for i in range(ends)]),
            ],
            axis=dim,
        )
    return cells


def exact_dot(left, right):
    return jnp.dot(left, right, precision=lax.Precision.HIGHEST, preferred_element_type=jnp.float32)


def chol_solve(matrix, target):
    lower_factor = jnp.linalg.cholesky(matrix)
    halfway = lax.linalg.triangular_solve(lower_factor, target, left_side=True, lower=True)
    return lax.linalg.triangular_solve(
        lower_factor, halfway, left_side=True, lower=True, transpose_a=True
    )


def place_rows(values_rows, owners, owner_count):
    owner_hits = (owners[:, None] == jnp.arange(owner_count, dtype=jnp.int32)[None, :]).astype(
        jnp.int32
    )
    earlier_hits = jnp.cumsum(owner_hits, axis=0, dtype=jnp.int32) - owner_hits
    rank_index = jnp.sum(earlier_hits * owner_hits, axis=1, dtype=jnp.int32)
    slot_index = owners * SLOTS + rank_index
    empty_rows = jnp.zeros((owner_count * SLOTS, values_rows.shape[1]), values_rows.dtype)
    return (
        empty_rows.at[slot_index]
        .set(values_rows)
        .reshape(owner_count, SLOTS * values_rows.shape[1])
    )


def on_device(right_side, block_entries, neighbours, face_rows, die_owner, die_node):
    tile_mats = block_entries.reshape(BLK_DEV, COUPLED, BLOCK, BLOCK)
    face_list = face_rows.reshape(-1)
    neighbour_list = neighbours.reshape(-1)
    owners = die_owner[:, 0]
    owner_count = lax.axis_size("layer")
    top_bit = lax.axis_size("region").bit_length() - 2

    def apply_op(field):
        tiles = field.reshape(RHS, BLK_DEV, BLOCK)
        outgoing = jnp.take(tiles, face_list, axis=1).reshape(RHS, 4, FACES * BLOCK)
        near_rows = partner(outgoing[:, 0], "region", 0)
        far_rows = partner(outgoing[:, 1], "region", top_bit)
        stacked = jnp.stack([outgoing[:, 3], outgoing[:, 2]], axis=1)
        layered = with_halo(stacked, (("layer", 1),), 1)
        received = jnp.stack([near_rows, far_rows, layered[:, 0], layered[:, 3]], axis=1)
        extended = jnp.concatenate([tiles, received.reshape(RHS, 4 * FACES, BLOCK)], axis=1)
        picked = jnp.take(extended, neighbour_list, axis=1).reshape(
            RHS, BLK_DEV, COUPLED - 1, BLOCK
        )
        columns = jnp.concatenate([tiles[:, :, None, :], picked], axis=2)
        product = jnp.einsum("snkb,nkab->sna", columns, tile_mats, precision=lax.Precision.HIGHEST)
        return product.reshape(RHS, BLK_DEV * BLOCK)

    norm_zero = lax.psum(exact_dot(right_side, right_side.T), ("region", "layer"))
    image_zero = apply_op(right_side)
    curve_zero = lax.psum(exact_dot(right_side, image_zero.T), ("region", "layer"))
    alpha_first = chol_solve(0.5 * (curve_zero + curve_zero.T), norm_zero)
    iterate_one = exact_dot(alpha_first.T, right_side)
    resid_one = right_side - exact_dot(alpha_first.T, image_zero)
    norm_one = lax.psum(exact_dot(resid_one, resid_one.T), ("region", "layer"))
    beta_step = chol_solve(norm_zero, norm_one)
    direction = resid_one + exact_dot(beta_step.T, right_side)
    image_one = apply_op(direction)
    curve_one = lax.psum(exact_dot(direction, image_one.T), ("region", "layer"))
    alpha_second = chol_solve(0.5 * (curve_one + curve_one.T), norm_one)
    solution_field = iterate_one + exact_dot(alpha_second.T, direction)
    residual = resid_one - exact_dot(alpha_second.T, image_one)
    outgoing_rows = place_rows(jnp.take(solution_field, die_node, axis=1).T, owners, owner_count)
    mech_temps = lax.all_to_all(outgoing_rows, "layer", split_axis=0, concat_axis=0, tiled=True)
    return (solution_field, residual, mech_temps)


def solution(mesh):
    in_specs = (
        P(None, ("region", "layer")),
        P(("region", "layer"), None, None),
        P(("region", "layer"), None),
        P(("region", "layer"), None),
        P(("region", "layer"), None),
        P(("region", "layer")),
    )
    out_specs = (
        P(None, ("region", "layer")),
        P(None, ("region", "layer")),
        P(("region", "layer"), None),
    )
    return jax.shard_map(
        on_device, mesh=mesh, in_specs=in_specs, out_specs=out_specs, check_vma=False
    )
```

profile of v0, /device:TPU:8, one launch (start us, length us, event | category | flops | bytes accessed | tf_op | source)
XLA Modules:
  0.0 480.5 jit_solution(8176909102505080614)
XLA Ops:
  1.4 3.1 reshape.98
  4.6 2.9 copy.80
  7.5 1.7 gather_fusion
  12.1 2.4 reshape.100
  14.4 3.1 fusion.53
  18.3 7.2 %collective-permute-start.1 = (f32[64,512]{1,0:T(8,128)}, f32[64,512]{1,0:T(8,128)}, u32[]{:S(2)}, u32[]{:S(2)}) collective-permute-start(f32[64,512]{1,0:T(8,128)} %bitcast.131), channel_id=1, source_target_pairs={{0,128},{16,144},{32,160},{48,176},{64,192},{80,208},{96,224},{112... | collective-permute-start | bytes 393224 | tf_op jit(solution)/shard_map/ppermute | solution.py:15
  25.5 3.5 collective-permute-start.2
  28.9 3.2 collective-permute-start.3
  35.0 2.2 broadcast_in_dim_reshape.6
  37.2 12.7 %reshape.104 = f32[64,7,64,64]{3,2,0,1:T(8,128)} reshape(f32[64,7,4096]{2,0,1:T(8,128)} %param.16) | data formatting | bytes 14680064 | tf_op jit(solution)/shard_map/reshape | solution.py:63
  49.8 4.1 copy.82
  57.5 2.0 pad_maximum_fusion
  59.5 5.9 %gather_fusion.1 = f32[384,64,64]{2,1,0:T(8,128)} fusion(f32[64,96,64]{2,0,1:T(8,128)S(1)} %pad_maximum_fusion, s32[1024]{0:T(1024)S(1)} %pad_clamp_fusion.1), kind=kCustom, calls=%fused_computation.1.clone | custom fusion | bytes 12584448 | tf_op jit(solution)/shard_map/jit(_take)/gather | solution.py:79
  65.4 10.7 %broadcast_select_fusion.1 = f32[384,64,64]{2,1,0:T(8,128)} fusion(f32[384,64,64]{2,1,0:T(8,128)} %gather_fusion.1, pred[384]{0:T(512)(128)(4,1)S(1)} %compare_and_fusion), kind=kLoop, calls=%fused_computation.17 | loop fusion | flops 1572864 | bytes 12583296 | tf_op jit(solution)/shard_map/jit(_take)/select_n | solution.py:79
  76.1 21.7 %fusion.15 = f32[64,64,64]{2,0,1:T(8,128)S(1)} fusion(f32[64,7,64,64]{3,2,0,1:T(8,128)} %reshape.104, f32[64,64,6,64]{3,0,2,1:T(8,128)} %bitcast.134, f32[64,64,1,64]{3,0,2,1:T(8,128)S(1)} %copy-done.8), kind=kOutput, calls=%fused_computation.25 | convolution fusion | flops 1411121152 | bytes 15728640 | tf_op jit(solution)/shard_map/snkb,nkab->sna/dot_general | solution.py:83
  97.8 2.5 copy.84
  100.3 2.1 reshape.105
  103.5 75.3 %all-reduce = (f32[64,64]{0,1:T(8,128)S(1)}, f32[64,64]{1,0:T(8,128)S(1)}) all-reduce(f32[64,64]{0,1:T(8,128)S(1)} %fusion.54, f32[64,64]{1,0:T(8,128)S(1)} %convolution_bitcast_fusion), channel_id=1, replica_groups=mesh['region'=16,'layer'=16] {'region','layer'}, use_global_device_ids=true, to_apply=%region_3.7 | all-reduce | flops 8192 | bytes 65536 | tf_op jit(solution)/shard_map/psum | solution.py:86
  178.9 5.8 %cholesky.70 = f32[64,64]{1,0:T(8,128)S(1)} custom-call(f32[64,64]{1,0:T(8,128)S(1)} %fusion.41), custom_call_target="Cholesky" | custom-call | tf_op jit(solution)/shard_map/jit(cholesky)/cholesky | solution.py:40
  186.1 4.9 %custom-call.15 = f32[1,64,64]{1,2,0:T(8,128)S(1)} custom-call(f32[1,64,64]{2,1,0:T(8,128)S(1)} %fusion.26), custom_call_target="InvertDiagBlocksLowerTriangular" | custom-call | tf_op jit(solution)/shard_map/triangular_solve/custom-call.2 | solution.py:42
  191.2 5.8 %cholesky.59 = f32[64,64]{1,0:T(8,128)S(1)} custom-call(f32[64,64]{1,0:T(8,128)S(1)} %fusion.46), custom_call_target="Cholesky" | custom-call | tf_op jit(solution)/shard_map/jit(cholesky)/cholesky | solution.py:40
  198.4 4.9 %custom-call.13 = f32[1,64,64]{1,2,0:T(8,128)S(1)} custom-call(f32[1,64,64]{2,1,0:T(8,128)S(1)} %fusion.25), custom_call_target="InvertDiagBlocksLowerTriangular" | custom-call | tf_op jit(solution)/shard_map/triangular_solve/custom-call.2 | solution.py:42
  205.7 74.6 %psum.30 = f32[64,64]{1,0:T(8,128)S(1)} all-reduce(f32[64,64]{1,0:T(8,128)S(1)} %fusion.56), channel_id=1, replica_groups=mesh['region'=16,'layer'=16] {'region','layer'}, use_global_device_ids=true, to_apply=%region_4.0 | all-reduce | flops 4096 | bytes 32768 | tf_op jit(solution)/shard_map/psum | solution.py:92
  281.9 2.2 reshape.106
  284.0 4.1 copy.94
  288.2 3.2 gather_fusion.2
  294.5 2.4 fusion.52
  297.0 2.6 collective-permute-start.5
  299.6 2.2 collective-permute-start.6
  301.8 4.1 collective-permute-start.7
  306.0 2.0 fusion.55
  308.0 2.2 broadcast_in_dim_reshape.7
  310.2 4.1 copy.96
  316.0 2.0 pad_maximum_fusion.1
  318.0 6.0 %gather_fusion.3 = f32[384,64,64]{2,1,0:T(8,128)} fusion(f32[64,96,64]{2,0,1:T(8,128)S(1)} %pad_maximum_fusion.1, s32[1024]{0:T(1024)S(1)} %pad_clamp_fusion.1), kind=kCustom, calls=%fused_computation.3.clone | custom fusion | bytes 12584448 | tf_op jit(solution)/shard_map/jit(_take)/gather | solution.py:79
  324.1 10.7 %broadcast_select_fusion = f32[384,64,64]{2,1,0:T(8,128)} fusion(f32[384,64,64]{2,1,0:T(8,128)} %gather_fusion.3, pred[384]{0:T(512)(128)(4,1)S(1)} %compare_and_fusion), kind=kLoop, calls=%fused_computation.16 | loop fusion | flops 1572864 | bytes 12583296 | tf_op jit(solution)/shard_map/jit(_take)/select_n | solution.py:79
  334.7 21.5 %fusion.10 = f32[64,64,64]{2,0,1:T(8,128)S(1)} fusion(f32[64,7,64,64]{3,2,0,1:T(8,128)} %reshape.104, f32[64,64,6,64]{3,0,2,1:T(8,128)} %bitcast.133, f32[64,64,1,64]{3,0,2,1:T(8,128)S(1)} %copy-done.7), kind=kOutput, calls=%fused_computation.24 | convolution fusion | flops 1411121152 | bytes 15728640 | tf_op jit(solution)/shard_map/snkb,nkab->sna/dot_general | solution.py:83
  356.2 2.6 copy.98
  358.8 2.1 reshape.110
  361.9 76.6 %psum.31 = f32[64,64]{1,0:T(8,128)S(1)} all-reduce(f32[64,64]{1,0:T(8,128)S(1)} %fusion.57), channel_id=1, replica_groups=mesh['region'=16,'layer'=16] {'region','layer'}, use_global_device_ids=true, to_apply=%region_5.0 | all-reduce | flops 4096 | bytes 32768 | tf_op jit(solution)/shard_map/psum | solution.py:96
  438.8 5.8 %cholesky.81 = f32[64,64]{1,0:T(8,128)S(1)} custom-call(f32[64,64]{1,0:T(8,128)S(1)} %fusion.35), custom_call_target="Cholesky" | custom-call | tf_op jit(solution)/shard_map/jit(cholesky)/cholesky | solution.py:40
  446.0 4.9 %custom-call.17 = f32[1,64,64]{1,2,0:T(8,128)S(1)} custom-call(f32[1,64,64]{2,1,0:T(8,128)S(1)} %fusion.27), custom_call_target="InvertDiagBlocksLowerTriangular" | custom-call | tf_op jit(solution)/shard_map/triangular_solve/custom-call.2 | solution.py:42
  451.3 3.2 convolution_add_fusion
  454.5 3.2 copy.102
  457.7 5.0 %scatter_custom_fusion = f32[2048,64]{1,0:T(8,128)S(1)} fusion(s32[512]{0:T(512)S(1)} %bitcast.142, f32[]{:T(128)} %constant.75.clone.1, f32[]{:T(128)} %constant.81.clone.1, pred[512]{0:T(512)(128)(4,1)S(1)} %compare_and_fusion.2, f32[64,4096]{0,1:T(8,128)} %copy.102, s32[1024]{0:T(1024)S(1)} %pad_clamp_fusion), kind=kCustom, calls=%fused_computation.32 | custom fusion | flops 32768 | bytes 1577480 | tf_op jit(solution)/shard_map/scatter | solution.py:57
  464.1 4.9 %all-to-all-start = ((f32[16,1,8192]{2,1,0:T(1,128)}), f32[16,1,8192]{2,1,0:T(1,128)S(1)}, u32[]{:S(2)}, u32[]{:S(2)}) async-start(f32[16,1,8192]{2,1,0:T(1,128)} %all_to_all.11), calls=%async_computation | async-start | bytes 1048576 | tf_op jit(solution)/shard_map/all_to_all | solution.py:101
  469.0 2.0 convolution_subtract_fusion
  471.0 8.1 %all-to-all-done = f32[16,1,8192]{2,1,0:T(1,128)S(1)} async-done(((f32[16,1,8192]{2,1,0:T(1,128)}), f32[16,1,8192]{2,1,0:T(1,128)S(1)}, u32[]{:S(2)}, u32[]{:S(2)}) %all-to-all-start) | async-done | bytes 524320 | tf_op jit(solution)/shard_map/all_to_all | solution.py:101
  (105 shorter events, 28.9 us)
Async XLA Ops:
  4.5 27.6 %copy-start.11 = (s32[64,6]{0,1:T(8,128)S(1)}, s32[64,6]{0,1:T(8,128)}, u32[]{:S(2)}) copy-start(s32[64,6]{0,1:T(8,128)} %param.17) | copy-start | bytes 4612
  4.6 27.8 %copy-start = (f32[64,4096]{1,0:T(8,128)S(1)}, f32[64,4096]{1,0:T(8,128)}, u32[]{:S(2)}) copy-start(f32[64,4096]{1,0:T(8,128)} %param.15) | copy-start | bytes 3145732
  4.6 28.8 %copy-start.10 = (s32[512]{0:T(512)S(1)}, s32[512]{0:T(512)}, u32[]{:S(2)}) copy-start(s32[512]{0:T(512)} %param.20) | copy-start | bytes 6148
  4.6 28.9 %copy-start.9 = (s32[512,1]{0,1:T(1,128)S(1)}, s32[512,1]{0,1:T(1,128)}, u32[]{:S(2)}) copy-start(s32[512,1]{0,1:T(1,128)} %param.19) | copy-start | bytes 6148
  7.5 29.7 %copy-start.6 = (f32[64,64,64]{2,0,1:T(8,128)}, f32[64,64,64]{2,0,1:T(8,128)S(1)}, u32[]{:S(2)}) copy-start(f32[64,64,64]{2,0,1:T(8,128)S(1)} %copy.80) | copy-start | bytes 3145732
  17.5 36.4 %collective-permute-start = (f32[64,512]{1,0:T(8,128)S(1)}, f32[64,512]{1,0:T(8,128)S(1)}, u32[]{:S(2)}, u32[]{:S(2)}) collective-permute-start(f32[64,512]{1,0:T(8,128)S(1)} %bitcast.136), channel_id=1, source_target_pairs={{0,16},{16,0},{32,48},{48,32},{64,80},{80,64},{96,112},{112,96},{1... | collective-permute-start | bytes 393224 | tf_op jit(solution)/shard_map/ppermute | solution.py:15
  18.3 35.8 %collective-permute-start.1 = (f32[64,512]{1,0:T(8,128)}, f32[64,512]{1,0:T(8,128)}, u32[]{:S(2)}, u32[]{:S(2)}) collective-permute-start(f32[64,512]{1,0:T(8,128)} %bitcast.131), channel_id=1, source_target_pairs={{0,128},{16,144},{32,160},{48,176},{64,192},{80,208},{96,224},{112... | collective-permute-start | bytes 393224 | tf_op jit(solution)/shard_map/ppermute | solution.py:15
  25.5 29.6 %collective-permute-start.2 = (f32[64,1,512]{2,1,0:T(1,128)}, f32[64,1,512]{2,1,0:T(1,128)}, u32[]{:S(2)}, u32[]{:S(2)}) collective-permute-start(f32[64,1,512]{2,1,0:T(1,128)} %get-tuple-element.15), channel_id=1, source_target_pairs={{0,1},{1,2},{2,3},{3,4},{4,5},{5,6},{6,7},{7,8},{8,9},{9,10},{10,1... | collective-permute-start | bytes 393224 | tf_op jit(solution)/shard_map/ppermute | solution.py:26
  28.9 26.1 %collective-permute-start.3 = (f32[64,1,512]{2,1,0:T(1,128)}, f32[64,1,512]{2,1,0:T(1,128)}, u32[]{:S(2)}, u32[]{:S(2)}) collective-permute-start(f32[64,1,512]{2,1,0:T(1,128)} %get-tuple-element.16), channel_id=1, source_target_pairs={{1,0},{2,1},{3,2},{4,3},{5,4},{6,5},{7,6},{8,7},{9,8},{10,9},{11,1... | collective-permute-start | bytes 393224 | tf_op jit(solution)/shard_map/ppermute | solution.py:28
  65.4 10.7 %copy-start.8 = (f32[64,64,1,64]{3,0,2,1:T(8,128)S(1)}, f32[64,64,1,64]{3,0,2,1:T(8,128)}, u32[]{:S(2)}) copy-start(f32[64,64,1,64]{3,0,2,1:T(8,128)} %copy.82) | copy-start | bytes 3145732
  97.8 4.7 copy-start.1
  204.8 86.6 %copy-start.4 = (f32[64,4096]{1,0:T(8,128)}, f32[64,4096]{1,0:T(8,128)S(1)}, u32[]{:S(2)}) copy-start(f32[64,4096]{1,0:T(8,128)S(1)} %convolution_subtract_fusion.1) | copy-start | bytes 3145732
  281.8 26.2 %copy-start.2 = (f32[64,4096]{1,0:T(8,128)}, f32[64,4096]{1,0:T(8,128)S(1)}, u32[]{:S(2)}) copy-start(f32[64,4096]{1,0:T(8,128)S(1)} %convolution_add_fusion.1) | copy-start | bytes 3145732
  296.9 17.4 %collective-permute-start.4 = (f32[64,512]{1,0:T(8,128)S(1)}, f32[64,512]{1,0:T(8,128)S(1)}, u32[]{:S(2)}, u32[]{:S(2)}) collective-permute-start(f32[64,512]{1,0:T(8,128)S(1)} %bitcast.137), channel_id=1, source_target_pairs={{0,16},{16,0},{32,48},{48,32},{64,80},{80,64},{96,112},{112,96},{1... | collective-permute-start | bytes 393224 | tf_op jit(solution)/shard_map/ppermute | solution.py:15
  297.0 17.4 %collective-permute-start.5 = (f32[64,512]{1,0:T(8,128)S(1)}, f32[64,512]{1,0:T(8,128)S(1)}, u32[]{:S(2)}, u32[]{:S(2)}) collective-permute-start(f32[64,512]{1,0:T(8,128)S(1)} %bitcast.138), channel_id=1, source_target_pairs={{0,128},{16,144},{32,160},{48,176},{64,192},{80,208},{96,224},{112... | collective-permute-start | bytes 393224 | tf_op jit(solution)/shard_map/ppermute | solution.py:15
  299.6 14.9 %collective-permute-start.6 = (f32[64,1,512]{2,1,0:T(1,128)S(1)}, f32[64,1,512]{2,1,0:T(1,128)S(1)}, u32[]{:S(2)}, u32[]{:S(2)}) collective-permute-start(f32[64,1,512]{2,1,0:T(1,128)S(1)} %get-tuple-element.11), channel_id=1, source_target_pairs={{0,1},{1,2},{2,3},{3,4},{4,5},{5,6},{6,7},{7,8},{8,9},{9,10},{10,1... | collective-permute-start | bytes 393224 | tf_op jit(solution)/shard_map/ppermute | solution.py:26
  301.8 12.7 %collective-permute-start.7 = (f32[64,1,512]{2,1,0:T(1,128)S(1)}, f32[64,1,512]{2,1,0:T(1,128)S(1)}, u32[]{:S(2)}, u32[]{:S(2)}) collective-permute-start(f32[64,1,512]{2,1,0:T(1,128)S(1)} %get-tuple-element.12), channel_id=1, source_target_pairs={{1,0},{2,1},{3,2},{4,3},{5,4},{6,5},{7,6},{8,7},{9,8},{10,9},{11,1... | collective-permute-start | bytes 393224 | tf_op jit(solution)/shard_map/ppermute | solution.py:28
  324.1 10.7 %copy-start.7 = (f32[64,64,1,64]{3,0,2,1:T(8,128)S(1)}, f32[64,64,1,64]{3,0,2,1:T(8,128)}, u32[]{:S(2)}) copy-start(f32[64,64,1,64]{3,0,2,1:T(8,128)} %copy.96) | copy-start | bytes 3145732
  356.2 4.7 copy-start.3
  360.9 108.1 %copy-start.5 = (f32[64,4096]{1,0:T(8,128)S(1)}, f32[64,4096]{1,0:T(8,128)}, u32[]{:S(2)}) copy-start(f32[64,4096]{1,0:T(8,128)} %copy-done.4) | copy-start | bytes 3145732
  464.1 15.0 %all-to-all-start = ((f32[16,1,8192]{2,1,0:T(1,128)}), f32[16,1,8192]{2,1,0:T(1,128)S(1)}, u32[]{:S(2)}, u32[]{:S(2)}) async-start(f32[16,1,8192]{2,1,0:T(1,128)} %all_to_all.11), calls=%async_computation | async-start | bytes 1048576 | tf_op jit(solution)/shard_map/all_to_all | solution.py:101
where the time goes:
time: 486 us; the launch traced here: 480 us
  blocking collectives  227 us (47%)
  local copies, waits for them, and re-layouts  86.1 us (18%)
  other arithmetic  72.6 us (15%)
  matrix products  57.6 us (12%)
  starting transfers between devices  27.9 us (6%)
  waiting for transfers between devices  8.13 us (2%)
    psum x1, blocking collectives, on_device(): curve_one = lax.psum(exact_dot(direction, image_one.T), ('region', 'layer'))  76.6 us
    psum x1, blocking collectives, on_device(): lax.psum(exact_dot(right_side, right_side.T), ('region', 'layer'))  75.3 us
    psum x1, blocking collectives, on_device(): norm_one = lax.psum(exact_dot(resid_one, resid_one.T), ('region', 'layer'))  74.6 us
    dot_general x2, matrix products, apply_op(): jnp.einsum('snkb,nkab->sna', columns, tile_mats, precision=lax.Precision....  43.2 us
    select_n x3, other arithmetic, apply_op(): jnp.take(extended, neighbour_list, axis=1)  21.3 us
    another operation x9, other arithmetic, chol_solve(): lower_factor = jnp.linalg.cholesky(matrix)  19.6 us
    another operation x6, other arithmetic, chol_solve(): lax.linalg.triangular_solve(lower_factor, halfway, left_side=True, lower=...  16.6 us
    dot_general x9, matrix products, exact_dot(): jnp.dot(left, right, precision=lax.Precision.HIGHEST, preferred_element_t...  13.2 us
  transfers between devices with their start and end apart: 9, of which 1 were waited for; matrix products, arithmetic and copies ran while one was open for 7% of the time, Pallas kernels for 0%

commit v1 on v0

v1 whole, which is shorter than its diff:
```python
import functools

import jax
import jax.numpy as jnp
from jax import lax
from jax.experimental import pallas as pl
from jax.experimental.pallas import tpu as pltpu
from jax.sharding import PartitionSpec as P

BLOCK = 64
RHS = 64
COUPLED = 7
BLK_DEV = 64
NODES_DEV = BLK_DEV * BLOCK
DIE_ROWS = 512
SLOTS = 128
FACES = 8
LANES = 128
STEP = 8
GRID = BLK_DEV // STEP
SHIFT = 1.5
BF16 = jnp.bfloat16
F32 = jnp.float32


def params(mib):
    return pltpu.CompilerParams(vmem_limit_bytes=mib * 1024 * 1024)


def cost(flops, moved):
    return pl.CostEstimate(flops=flops, bytes_accessed=moved, transcendentals=0)


def resident():
    return pl.BlockSpec(memory_space=pltpu.VMEM)


def smem():
    return pl.BlockSpec(memory_space=pltpu.SMEM)


def left_lanes(rows):
    return lax.broadcasted_iota(jnp.int32, (rows, LANES), 1) < RHS


def two_parts(doubled):
    lead = doubled.astype(BF16).astype(F32)
    return jnp.where(left_lanes(doubled.shape[0]), lead, doubled - lead).astype(BF16)


def emit_faces(face_rows, nodes_ref, face_refs):
    for side, face_ref in enumerate(face_refs):
        for face in range(FACES):
            start = pl.multiple_of(face_rows[side, face] * BLOCK, BLOCK)
            upper = nodes_ref[pl.ds(start, 32), :]
            lower = nodes_ref[pl.ds(start + 32, 32), :]
            face_ref[face * 32 : (face + 1) * 32, :] = jnp.where(left_lanes(32), upper, lower)


def field_kernel(face_rows, right_ref, parts_ref, nodes_ref, *face_refs):
    step = pl.program_id(0)
    for chunk in range(STEP * BLOCK // LANES):
        piece = right_ref[:, chunk * LANES : (chunk + 1) * LANES]
        doubled = jnp.concatenate([piece, piece], axis=0).T
        start = pl.multiple_of(step * STEP * BLOCK + chunk * LANES, LANES)
        nodes_ref[pl.ds(start, LANES), :] = doubled
        halves = two_parts(doubled)
        parts_ref[step * STEP + 2 * chunk] = halves[:BLOCK]
        parts_ref[step * STEP + 2 * chunk + 1] = halves[BLOCK:]

    @pl.when(step == GRID - 1)
    def _():
        emit_faces(face_rows, nodes_ref, face_refs)


def entries_kernel(raw_ref, mats_ref, rows_ref):
    step = pl.program_id(0)
    half = left_lanes(32)
    lane = lax.broadcasted_iota(jnp.int32, (32, LANES), 1)
    twice = 2 * lax.broadcasted_iota(jnp.int32, (32, LANES), 0)
    shift_even = jnp.where(lane == twice, SHIFT, 0.0)
    shift_odd = jnp.where(lane == twice + 1, SHIFT, 0.0)
    shift_odd = jnp.where(half, shift_odd, 0.0)
    shift_even = jnp.where(half, shift_even, 0.0)
    for k in range(COUPLED):
        for pair in range(32):
            rows_ref[pl.ds((k * 32 + pair) * STEP, STEP), :] = raw_ref[
                k, :, pair * LANES : (pair + 1) * LANES
            ]
    for item in range(STEP):
        for duo in range(4):
            first = rows_ref[pl.ds(2 * duo * 256 + item, 32, stride=STEP), :]
            if 2 * duo + 1 < COUPLED:
                second = rows_ref[pl.ds((2 * duo + 1) * 256 + item, 32, stride=STEP), :]
            else:
                second = jnp.zeros_like(first)
            even = jnp.where(half, first, pltpu.roll(second, RHS, 1))
            odd = jnp.where(half, pltpu.roll(first, RHS, 1), second)
            if duo == 0:
                even = even - shift_even
                odd = odd - shift_odd
            stacked = jnp.concatenate([even, odd], axis=0)
            lead = stacked.astype(BF16)
            rest = (stacked - lead.astype(F32)).astype(BF16)
            block = step * STEP + item
            mats_ref[block, :BLOCK, duo * LANES : (duo + 1) * LANES] = lead
            mats_ref[block, BLOCK:, duo * LANES : (duo + 1) * LANES] = rest


def fill_extended(parts_ref, received, extended_ref):
    extended_ref[:BLK_DEV] = parts_ref[...]
    half = left_lanes(32)
    for side, got_ref in enumerate(received):
        for face in range(FACES):
            packed = got_ref[face * 32 : (face + 1) * 32, :]
            turned = pltpu.roll(packed, RHS, 1)
            block = BLK_DEV + side * FACES + face
            extended_ref[block, :32] = two_parts(jnp.where(half, packed, turned))
            extended_ref[block, 32:] = two_parts(jnp.where(half, turned, packed))


def block_row(block, neighbours, mats_ref, extended_ref, nodes_ref):
    pieces = [extended_ref[block]]
    for k in range(COUPLED - 1):
        pieces.append(extended_ref[neighbours[k, block]])
    pieces.append(pieces[0])
    product = jnp.dot(
        mats_ref[block], jnp.concatenate(pieces, axis=0), preferred_element_type=F32
    )
    folded = product[:BLOCK] + product[BLOCK:]
    doubled = folded + pltpu.roll(folded, RHS, 1)
    start = pl.multiple_of(block * BLOCK, BLOCK)
    nodes_ref[pl.ds(start, 32, stride=2), :] = doubled[:32]
    nodes_ref[pl.ds(start + 1, 32, stride=2), :] = doubled[32:]
    return nodes_ref[pl.ds(start, BLOCK), :]


def first_kernel(
    neighbours, face_rows, mats_ref, parts_ref, own_ref, near, far, below, above,
    image_ref, both_ref, out0, out1, out2, out3, extended_ref, nodes_ref,
):
    fill_extended(parts_ref, (near, far, below, above), extended_ref)

    def group(step, carry):
        for item in range(STEP):
            block = step * STEP + item
            doubled = block_row(block, neighbours, mats_ref, extended_ref, nodes_ref)
            image_ref[block] = two_parts(doubled)
            rows = pl.ds(pl.multiple_of(block * BLOCK, BLOCK), BLOCK)
            both_ref[rows, :] = jnp.where(left_lanes(BLOCK), own_ref[rows, :], doubled)
        return carry

    lax.fori_loop(0, GRID, group, 0)
    emit_faces(face_rows, nodes_ref, (out0, out1, out2, out3))


def gram_of(left, right):
    return lax.dot_general(left, right, (((0,), (0,)), ((), ())), preferred_element_type=F32)


def quarter_sum(grid):
    tall = grid[:RHS] + grid[RHS:]
    return tall + pltpu.roll(tall, RHS, 1)


def rows_of(ref, step):
    first = pl.multiple_of(step * STEP, STEP)
    return ref[pl.ds(first, STEP)].reshape(STEP * BLOCK, LANES)


def gram_kernel(field_ref, image_ref, out_ref, wide_acc, acc_ref):
    wide_acc[...] = jnp.zeros_like(wide_acc)
    acc_ref[...] = jnp.zeros_like(acc_ref)

    def group(step, carry):
        field = rows_of(field_ref, step)
        image = rows_of(image_ref, step)
        wide_acc[...] += gram_of(field, jnp.concatenate([field, image], axis=1))
        acc_ref[...] += gram_of(image, image)
        return carry

    lax.fori_loop(0, GRID, group, 0)
    out_ref[:RHS, :] = quarter_sum(wide_acc[:, :LANES])
    out_ref[RHS:LANES, :] = quarter_sum(wide_acc[:, LANES:])
    out_ref[LANES:, :] = quarter_sum(acc_ref[...])


def second_kernel(
    neighbours, mats_ref, parts_ref, near, far, below, above, field_ref, gram_ref,
    image_ref, sums_ref, extended_ref, nodes_ref, acc_ref,
):
    fill_extended(parts_ref, (near, far, below, above), extended_ref)
    acc_ref[...] = jnp.zeros_like(acc_ref)

    def group(step, carry):
        for item in range(STEP):
            block = step * STEP + item
            doubled = block_row(block, neighbours, mats_ref, extended_ref, nodes_ref)
            image_ref[block] = two_parts(doubled)
        joined = jnp.concatenate([rows_of(field_ref, step), rows_of(parts_ref, step)], axis=1)
        acc_ref[...] += gram_of(joined, rows_of(image_ref, step))
        return carry

    lax.fori_loop(0, GRID, group, 0)
    pack_sums(
        gram_ref[:RHS, :],
        gram_ref[RHS:LANES, :],
        gram_ref[LANES:, :],
        quarter_sum(acc_ref[:LANES]),
        quarter_sum(acc_ref[LANES:]),
        sums_ref,
    )


def pack_sums(norm, curve, image_norm, far_field, far_image, sums_ref):
    half = left_lanes(RHS)
    row = lax.broadcasted_iota(jnp.int32, (RHS, LANES), 0)
    col = lax.broadcasted_iota(jnp.int32, (RHS, LANES), 1)
    col = jnp.where(half, col, col - RHS)
    upper = row <= col
    diagonal = jnp.sum(jnp.where(row == col, image_norm, 0.0), axis=0, keepdims=True)
    last = jnp.where(row == RHS - 2, diagonal[:, RHS - 1 : RHS], diagonal)
    square = far_image[:, :RHS]
    balanced = 0.5 * (square + square.T)
    balanced = jnp.concatenate([balanced, balanced], axis=1)
    packed = jnp.where(upper, balanced, last)
    sums_ref[:RHS, :] = jnp.where(half, jnp.where(upper, norm, image_norm), curve)
    sums_ref[RHS:, :] = jnp.where(half, far_field, packed)


def unpack_sums(sums_ref):
    pair = sums_ref[:RHS, :RHS]
    curve = sums_ref[:RHS, RHS:]
    far_field = sums_ref[RHS:, :RHS]
    packed = sums_ref[RHS:, RHS:]
    row = lax.broadcasted_iota(jnp.int32, (RHS, RHS), 0)
    col = lax.broadcasted_iota(jnp.int32, (RHS, RHS), 1)
    pair_t = pair.T
    packed_t = packed.T
    norm = jnp.where(row <= col, pair, pair_t)
    lanes = lax.broadcasted_iota(jnp.int32, (1, RHS), 1)
    diagonal = jnp.where(
        lanes == RHS - 1, packed[RHS - 2 : RHS - 1, :1], packed[RHS - 1 : RHS, :]
    )
    image_norm = jnp.where(row > col, pair, pair_t)
    image_norm = jnp.where(row == col, diagonal, image_norm)
    far_image = jnp.where(row <= col, packed, packed_t)
    return norm, curve, image_norm, far_field, far_image


def relay_kernel(owners, die_node, both_ref, out_ref, counts):
    out_ref[...] = jnp.zeros_like(out_ref)
    for owner in range(16):
        counts[owner] = owner * SLOTS

    def move(row, carry):
        owner = owners[row]
        slot = counts[owner]
        counts[owner] = slot + 1
        out_ref[pl.ds(slot, 1), :] = both_ref[pl.ds(die_node[row], 1), :]
        return carry

    lax.fori_loop(0, DIE_ROWS, move, 0, unroll=8)


def mul(left, right):
    return jnp.dot(left, right, precision=lax.Precision.HIGHEST, preferred_element_type=F32)


def mul_t(left, right):
    return lax.dot_general(
        left,
        right,
        (((1,), (1,)), ((), ())),
        precision=lax.Precision.HIGHEST,
        preferred_element_type=F32,
    )


def eliminate(systems):
    row_id = lax.broadcasted_iota(jnp.int32, (RHS, 1), 0)
    for k in range(RHS):
        done = []
        for system in systems:
            pivot = system[k : k + 1, :] * (1.0 / system[k : k + 1, k : k + 1])
            done.append(jnp.where(row_id == k, pivot, system - system[:, k : k + 1] * pivot))
        systems = done
    return [system[:, RHS:] for system in systems]


def wide(left, right):
    return jnp.concatenate([left, right], axis=1)


def solve_steps(sums_ref):
    norm_zero, cross, image_norm, far_field, far_image = unpack_sums(sums_ref)
    eye = (
        lax.broadcasted_iota(jnp.int32, (RHS, RHS), 0)
        == lax.broadcasted_iota(jnp.int32, (RHS, RHS), 1)
    ).astype(F32)
    curve_zero = 0.5 * (cross + cross.T) + SHIFT * norm_zero
    alpha, norm_inverse = eliminate([wide(curve_zero, norm_zero), wide(norm_zero, eye)])
    alpha_t = alpha.T
    gram = jnp.concatenate([wide(norm_zero, cross), wide(cross.T, image_norm)], axis=0)
    shifted = jnp.concatenate([wide(cross, far_field), wide(image_norm, far_image)], axis=0)
    start = eye - SHIFT * alpha_t
    resid = wide(start, -alpha_t)
    norm_one = mul_t(mul(resid, gram), resid)
    mixed = start + mul(norm_inverse, norm_one).T
    direction = wide(mixed, -alpha_t)
    curve_one = mul_t(mul(direction, shifted + SHIFT * gram), direction)
    (alpha_two,) = eliminate([wide(0.5 * (curve_one + curve_one.T), norm_one)])
    second = mul(alpha_two.T, wide(mixed, alpha_t))
    gain, drop = second[:, :RHS], second[:, RHS:]
    keep = alpha_t + gain
    return keep, drop, start - SHIFT * gain, keep - SHIFT * drop


def halves_of(value):
    lead = value.astype(BF16)
    return lead, (value - lead.astype(F32)).astype(BF16)


def final_kernel(
    sums_ref, field_ref, image_ref, far_ref, solution_ref, residual_ref, coef_ref, weights_ref
):
    step = pl.program_id(0)

    @pl.when(step == 0)
    def _():
        keep, drop, left_over, taken = solve_steps(sums_ref)
        top = [wide(keep, keep), wide(-drop, -drop), jnp.zeros((RHS, LANES), F32)]
        low = [wide(left_over, left_over), wide(-taken, -taken), wide(drop, drop)]
        rows = jnp.concatenate(
            [jnp.concatenate(top, axis=1), jnp.concatenate(low, axis=1)], axis=0
        )
        lead, rest = halves_of(rows)
        weights_ref[:LANES] = lead
        weights_ref[LANES:] = rest
        coef_ref[...] = jnp.concatenate([keep.T, -drop.T], axis=0)

    basis = jnp.concatenate(
        [rows_of(ref, step) for ref in (field_ref, image_ref, far_ref)], axis=1
    )
    mixed = lax.dot_general(
        weights_ref[...], basis, (((1,), (1,)), ((), ())), preferred_element_type=F32
    )
    mixed = mixed[:LANES] + mixed[LANES:]
    solution_ref[...] = mixed[:RHS]
    residual_ref[...] = mixed[RHS:]


def owner_kernel(coef_ref, got_ref, out_ref):
    coef = coef_ref[...]
    none = jnp.zeros_like(coef)
    square = jnp.concatenate([wide(coef, none), wide(none, coef)], axis=0)
    weights = jnp.concatenate(halves_of(square), axis=1)
    for pack in range(8):
        pieces = []
        for pair in range(8 * pack, 8 * pack + 8):
            pieces.append(
                wide(
                    got_ref[pl.ds(2 * pair, 16, stride=SLOTS), :],
                    got_ref[pl.ds(2 * pair + 1, 16, stride=SLOTS), :],
                )
            )
        rows = jnp.concatenate(pieces, axis=0)
        lead, rest = halves_of(rows)
        product = jnp.dot(
            jnp.concatenate([lead, rest], axis=0), weights, preferred_element_type=F32
        )
        product = product[:LANES] + product[LANES:]
        product = product[:, :LANES] + product[:, LANES:]
        for at in range(8):
            pair = 8 * pack + at
            out_ref[:, pair * LANES : (pair + 1) * LANES] = product[16 * at : 16 * at + 16]


def swap(shard, axis, bit):
    return lax.ppermute(shard, axis, [(i, i ^ bit) for i in range(lax.axis_size(axis))])


def exchange(faces):
    count = lax.axis_size("layer")
    top = lax.axis_size("region") // 2
    near = swap(faces[0], "region", 1)
    far = swap(faces[1], "region", top)
    below = lax.ppermute(faces[2], "layer", [(i, i + 1) for i in range(count - 1)])
    above = lax.ppermute(faces[3], "layer", [(i + 1, i) for i in range(count - 1)])
    return near, far, below, above


def total(local):
    layers = lax.axis_size("layer")
    regions = lax.axis_size("region")
    parts = local.reshape(layers, LANES // layers, LANES)
    mine = jnp.sum(lax.all_to_all(parts, "layer", 0, 0, tiled=True), axis=0)
    copies = jnp.broadcast_to(mine[None], (regions,) + mine.shape)
    mine = jnp.sum(lax.all_to_all(copies, "region", 0, 0, tiled=True), axis=0)
    copies = jnp.broadcast_to(mine[None], (layers,) + mine.shape)
    return lax.all_to_all(copies, "layer", 0, 0, tiled=True).reshape(LANES, LANES)


PARTS = jax.ShapeDtypeStruct((BLK_DEV, BLOCK, LANES), BF16)
NODE_ROWS = jax.ShapeDtypeStruct((NODES_DEV, LANES), F32)
FACE = jax.ShapeDtypeStruct((FACES * 32, LANES), F32)
FIELD = jax.ShapeDtypeStruct((RHS, NODES_DEV), F32)
FIELD_STEP = pl.BlockSpec((RHS, STEP * BLOCK), lambda i: (0, i))


def on_device(right_side, block_entries, neighbours, face_rows, die_owner, die_node):
    owners = die_owner[:, 0]
    neighbours = neighbours.T
    entries = jnp.transpose(block_entries, (1, 0, 2))
    outcome = pl.pallas_call(
        field_kernel,
        grid=(GRID,),
        in_specs=[smem(), FIELD_STEP],
        out_specs=[resident()] * 6,
        out_shape=[PARTS, NODE_ROWS] + [FACE] * 4,
        compiler_params=params(8),
        cost_estimate=cost(1_000_000, 5_000_000),
        name="field",
    )(face_rows, right_side)
    field, own_rows, faces = outcome[0], outcome[1], outcome[2:]
    received = exchange(faces)
    mats = pl.pallas_call(
        entries_kernel,
        grid=(GRID,),
        in_specs=[pl.BlockSpec((COUPLED, STEP, BLOCK * BLOCK), lambda i: (0, i, 0))],
        out_specs=resident(),
        out_shape=jax.ShapeDtypeStruct((BLK_DEV, 2 * BLOCK, 4 * LANES), BF16),
        scratch_shapes=[pltpu.VMEM((COUPLED * 32 * STEP, LANES), F32)],
        compiler_params=params(8),
        cost_estimate=cost(10_000_000, 16_000_000),
        name="entries",
    )(entries)
    apply_scratch = [
        pltpu.VMEM((BLK_DEV + 4 * FACES, BLOCK, LANES), BF16),
        pltpu.VMEM((NODES_DEV, LANES), F32),
    ]
    outcome = pl.pallas_call(
        first_kernel,
        in_specs=[smem(), smem()] + [resident()] * 7,
        out_specs=[resident()] * 6,
        out_shape=[PARTS, NODE_ROWS] + [FACE] * 4,
        scratch_shapes=apply_scratch,
        compiler_params=params(8),
        cost_estimate=cost(1_000_000_000, 16_000_000),
        name="first_image",
    )(neighbours, face_rows, mats, field, own_rows, *received)
    image, both_rows, faces = outcome[0], outcome[1], outcome[2:]
    received = exchange(faces)
    outgoing = pl.pallas_call(
        relay_kernel,
        in_specs=[smem(), smem(), resident()],
        out_specs=resident(),
        out_shape=jax.ShapeDtypeStruct((16 * SLOTS, LANES), F32),
        scratch_shapes=[pltpu.SMEM((16,), jnp.int32)],
        compiler_params=params(8),
        cost_estimate=cost(1_000_000, 10_000_000),
        name="relay_rows",
    )(owners, die_node, both_rows)
    relayed = lax.all_to_all(
        outgoing.reshape(16, SLOTS, LANES), "layer", 0, 0, tiled=True
    ).reshape(16 * SLOTS, LANES)
    grams = pl.pallas_call(
        gram_kernel,
        in_specs=[resident()] * 2,
        out_specs=resident(),
        out_shape=jax.ShapeDtypeStruct((3 * RHS, LANES), F32),
        scratch_shapes=[pltpu.VMEM((LANES, 2 * LANES), F32), pltpu.VMEM((LANES, LANES), F32)],
        compiler_params=params(8),
        cost_estimate=cost(500_000_000, 2_000_000),
        name="near_grams",
    )(field, image)
    far_image, sums = pl.pallas_call(
        second_kernel,
        in_specs=[smem()] + [resident()] * 8,
        out_specs=[resident()] * 2,
        out_shape=[PARTS, jax.ShapeDtypeStruct((LANES, LANES), F32)],
        scratch_shapes=apply_scratch + [pltpu.VMEM((2 * LANES, LANES), F32)],
        compiler_params=params(8),
        cost_estimate=cost(1_000_000_000, 14_000_000),
        name="second_image",
    )(neighbours, mats, image, *received, field, grams)
    sums = total(sums)
    solution_field, residual, coef = pl.pallas_call(
        final_kernel,
        grid=(GRID,),
        in_specs=[resident()] * 4,
        out_specs=[FIELD_STEP, FIELD_STEP, resident()],
        out_shape=[FIELD, FIELD, jax.ShapeDtypeStruct((LANES, RHS), F32)],
        scratch_shapes=[pltpu.VMEM((2 * LANES, 3 * LANES), BF16)],
        compiler_params=params(8),
        cost_estimate=cost(500_000_000, 8_000_000),
        name="final",
    )(sums, field, image, far_image)
    mech_temps = pl.pallas_call(
        owner_kernel,
        in_specs=[resident()] * 2,
        out_specs=resident(),
        out_shape=jax.ShapeDtypeStruct((16, SLOTS * RHS), F32),
        compiler_params=params(8),
        cost_estimate=cost(100_000_000, 2_000_000),
        name="owner_rows",
    )(coef, relayed)
    return solution_field, residual, mech_temps


def solution(mesh):
    in_specs = (
        P(None, ("region", "layer")),
        P(("region", "layer"), None, None),
        P(("region", "layer"), None),
        P(("region", "layer"), None),
        P(("region", "layer"), None),
        P(("region", "layer")),
    )
    out_specs = (
        P(None, ("region", "layer")),
        P(None, ("region", "layer")),
        P(("region", "layer"), None),
    )
    return jax.shard_map(
        on_device, mesh=mesh, in_specs=in_specs, out_specs=out_specs, check_vma=False
    )
```

time: 486 us -> 122 us (0.25)
  blocking collectives: 227 us -> 30.6 us
  local copies, waits for them, and re-layouts: 86.1 us -> 10.7 us
  other arithmetic: 72.6 us -> 0.04 us
  matrix products: 57.6 us -> 0 us
  Pallas kernels: 0 us -> 43.9 us
    psum x3 -> x0, blocking collectives: 227 us -> none  [the longest x1 76.6 us: on_device(): curve_one = lax.psum(exact_dot(direction, image_one.T), ('region', 'layer'))]
    dot_general x11 -> x0, matrix products: 56.4 us -> none  [the longest x2 43.2 us: apply_op(): jnp.einsum('snkb,nkab->sna', columns, tile_mats, precision=lax.Precision....]
    pallas_call x0 -> x8, Pallas kernels: none -> 43.9 us  [the longest x1 17.8 us: on_device(): pl.pallas_call(final_kernel, grid=(GRID,), in_specs=[resident()] * 4, out...]
    another operation x19 -> x0, other arithmetic: 39.4 us -> none  [the longest x9 19.6 us: chol_solve(): lower_factor = jnp.linalg.cholesky(matrix)]
    reshape x15 -> x0, local copies, waits for them, and re-layouts: 35.6 us -> none  [the longest x1 12.7 us: on_device(): tile_mats = block_entries.reshape(BLK_DEV, COUPLED, BLOCK, BLOCK)]
    all_to_all x0 -> x2, blocking collectives: none -> 30.6 us  [the longest x1 15.9 us: total(): mine = jnp.sum(lax.all_to_all(parts, 'layer', 0, 0, tiled=True), axis=0)]
    select_n x8 -> x0, other arithmetic: 24.1 us -> none  [the longest x3 21.3 us: apply_op(): jnp.take(extended, neighbour_list, axis=1)]
    gather x4 -> x0, local copies, waits for them, and re-layouts: 16.7 us -> none  [the longest x2 11.9 us: apply_op(): jnp.take(extended, neighbour_list, axis=1)]
  transfers between devices with their start and end apart: 9 -> 10, of which waited for: 1 -> 2; matrix products, arithmetic and copies ran while one was open for 7% -> 0% of each run, Pallas kernels for 0% -> 23%
where the time goes in v1:
time: 122 us; the launch traced here: 121 us
  Pallas kernels  43.9 us (36%)
  blocking collectives  30.6 us (25%)
  starting transfers between devices  30.4 us (25%)
  local copies, waits for them, and re-layouts  10.7 us (9%)
  waiting for transfers between devices  4.48 us (4%)
    pallas_call x1, Pallas kernels, on_device(): pl.pallas_call(final_kernel, grid=(GRID,), in_specs=[resident()] * 4, out...  17.8 us
    all_to_all x1, blocking collectives, total(): mine = jnp.sum(lax.all_to_all(parts, 'layer', 0, 0, tiled=True), axis=0)  15.9 us
    all_to_all x1, blocking collectives, total(): mine = jnp.sum(lax.all_to_all(copies, 'region', 0, 0, tiled=True), axis=0)  14.7 us
    unnamed x22, local copies, waits for them, and re-layouts  10.1 us
    ppermute x4, starting transfers between devices, swap(): lax.ppermute(shard, axis, [(i, i ^ bit) for i in range(lax.axis_size(axis...  7.42 us
    pallas_call x1, Pallas kernels, on_device(): pl.pallas_call(second_kernel, in_specs=[smem()] + [resident()] * 8, out_s...  7.23 us
    ppermute x2, starting transfers between devices, exchange(): lax.ppermute(faces[2], 'layer', [(i, i + 1) for i in range(count - 1)])  6.94 us
    all_to_all x1, starting transfers between devices, on_device(): lax.all_to_all(outgoing.reshape(16, SLOTS, LANES), 'layer', 0, 0, tiled=T...  6.53 us
  transfers between devices with their start and end apart: 10, of which 2 were waited for; matrix products, arithmetic and copies ran while one was open for 0% of the time, Pallas kernels for 23%

profile of v1, /device:TPU:8, one launch (start us, length us, event | category | flops | bytes accessed | tf_op | source)
XLA Modules:
  0.0 121.0 jit_solution(11557937192599861608)
XLA Ops:
  0.6 0.0 copy-start.5
  0.6 1.2 %copy-done.5 = f32[64,4096]{1,0:T(8,128)S(1)} copy-done((f32[64,4096]{1,0:T(8,128)S(1)}, f32[64,4096]{1,0:T(8,128)}, u32[]{:S(2)}) %copy-start.5) | copy-done | bytes 1048600
  1.9 0.0 copy-start.7
  1.9 0.7 copy-done.7
  2.5 2.0 %field.1 = (bf16[64,64,128]{2,1,0:T(8,128)(2,1)S(1)}, f32[4096,128]{1,0:T(8,128)S(1)}, f32[256,128]{1,0:T(8,128)S(1)}, f32[256,128]{1,0:T(8,128)S(1)}, f32[256,128]{1,0:T(8,128)S(1)}, /*index=5*/f32[256,128]{1,0:T(8,128)S(1)}) custom-call(s32[4,8]{1,0:T(4,128)S(1)} %copy-done.7, f32[64,4096]{1,0:T(8,128)S(1)} %copy-done.5), custom_call_target="tpu_custom_call" | custom-call | flops 1000000 | bytes 5000000 | tf_op jit(solution)/shard_map/field/pallas_call | solution.py:415
  4.5 0.1 collective-permute-start
  4.6 7.3 %collective-permute-start.1 = (f32[256,128]{1,0:T(8,128)S(1)}, f32[256,128]{1,0:T(8,128)S(1)}, u32[]{:S(2)}, u32[]{:S(2)}) collective-permute-start(f32[256,128]{1,0:T(8,128)S(1)} %get-tuple-element.23), channel_id=1, source_target_pairs={{0,128},{16,144},{32,160},{48,176},{64,192},{80,208},{96,224},{112... | collective-permute-start | bytes 393224 | tf_op jit(solution)/shard_map/ppermute | solution.py:380
  11.9 3.5 %collective-permute-start.2 = (f32[256,128]{1,0:T(8,128)S(1)}, f32[256,128]{1,0:T(8,128)S(1)}, u32[]{:S(2)}, u32[]{:S(2)}) collective-permute-start(f32[256,128]{1,0:T(8,128)S(1)} %get-tuple-element.24), channel_id=1, source_target_pairs={{0,1},{1,2},{2,3},{3,4},{4,5},{5,6},{6,7},{7,8},{8,9},{9,10},{10,1... | collective-permute-start | bytes 393224 | tf_op jit(solution)/shard_map/ppermute | solution.py:388
  15.4 2.4 %collective-permute-start.3 = (f32[256,128]{1,0:T(8,128)S(1)}, f32[256,128]{1,0:T(8,128)S(1)}, u32[]{:S(2)}, u32[]{:S(2)}) collective-permute-start(f32[256,128]{1,0:T(8,128)S(1)} %get-tuple-element.25), channel_id=1, source_target_pairs={{1,0},{2,1},{3,2},{4,3},{5,4},{6,5},{7,6},{8,7},{9,8},{10,9},{11,1... | collective-permute-start | bytes 393224 | tf_op jit(solution)/shard_map/ppermute | solution.py:389
  17.7 0.0 copy-start
  17.7 3.1 %copy-done = f32[64,7,4096]{2,0,1:T(8,128)S(1)} copy-done((f32[64,7,4096]{2,0,1:T(8,128)S(1)}, f32[64,7,4096]{2,0,1:T(8,128)}, u32[]{:S(2)}) %copy-start) | copy-done | bytes 7340056
  20.8 3.9 %entries.1.mats_ref = bf16[64,128,512]{2,1,0:T(8,128)(2,1)S(1)} custom-call(f32[7,64,4096]{2,1,0:T(8,128)S(1)} %bitcast.7), custom_call_target="tpu_custom_call" | custom-call | flops 10000000 | bytes 16000000 | tf_op jit(solution)/shard_map/entries/pallas_call | solution.py:427
  24.7 0.0 collective-permute-done.near
  24.7 0.0 collective-permute-done.1.far
  24.7 0.0 collective-permute-done.2.below
  24.7 0.0 collective-permute-done.3.above
  24.8 0.0 copy-done.6
  24.8 0.0 copy-done.8
  24.8 5.1 %first_image.1 = (bf16[64,64,128]{2,1,0:T(8,128)(2,1)S(1)}, f32[4096,128]{1,0:T(8,128)S(1)}, f32[256,128]{1,0:T(8,128)S(1)}, f32[256,128]{1,0:T(8,128)S(1)}, f32...) custom-call(s32[6,64]{1,0:T(8,128)S(1)} %bitcast.11, s32[4,8]{1,0:T(4,128)S(1)} %copy-done.8, ...), custom_call_target="tpu_custom_call" | custom-call | flops 1000000000 | bytes 16000000 | tf_op jit(solution)/shard_map/first_image/pallas_call | solution.py:442
  29.9 0.0 copy-start.1
  29.9 1.3 %copy-done.1 = f32[4096,128]{1,0:T(8,128)} copy-done((f32[4096,128]{1,0:T(8,128)}, f32[4096,128]{1,0:T(8,128)S(1)}, u32[]{:S(2)}) %copy-start.1) | copy-done | bytes 2097176
  31.3 0.0 collective-permute-start.4
  31.3 0.1 collective-permute-start.5
  31.3 3.5 %collective-permute-start.6 = (f32[256,128]{1,0:T(8,128)S(1)}, f32[256,128]{1,0:T(8,128)S(1)}, u32[]{:S(2)}, u32[]{:S(2)}) collective-permute-start(f32[256,128]{1,0:T(8,128)S(1)} %get-tuple-element.29), channel_id=1, source_target_pairs={{0,1},{1,2},{2,3},{3,4},{4,5},{5,6},{6,7},{7,8},{8,9},{9,10},{10,1... | collective-permute-start | bytes 393224 | tf_op jit(solution)/shard_map/ppermute | solution.py:388
  34.8 2.4 %collective-permute-start.7 = (f32[256,128]{1,0:T(8,128)S(1)}, f32[256,128]{1,0:T(8,128)S(1)}, u32[]{:S(2)}, u32[]{:S(2)}) collective-permute-start(f32[256,128]{1,0:T(8,128)S(1)} %get-tuple-element.30), channel_id=1, source_target_pairs={{1,0},{2,1},{3,2},{4,3},{5,4},{6,5},{7,6},{8,7},{9,8},{10,9},{11,1... | collective-permute-start | bytes 393224 | tf_op jit(solution)/shard_map/ppermute | solution.py:389
  37.2 2.3 %near_grams.1.gram_ref = f32[192,128]{1,0:T(8,128)S(1)} custom-call(bf16[64,64,128]{2,1,0:T(8,128)(2,1)S(1)} %get-tuple-element.20.parts_ref.field_ref, bf16[64,64,128]{2,1,0:T(8,128)(2,1)S(1)} %get-tuple-element.26.image_ref.parts_ref), custom_call_target="tpu_custom_call" | custom-call | flops 500000000 | bytes 2000000 | tf_op jit(solution)/shard_map/near_grams/pallas_call | solution.py:467
  39.5 0.0 collective-permute-done.4.near
  39.5 3.7 %collective-permute-done.5.far = f32[256,128]{1,0:T(8,128)S(1)} collective-permute-done((f32[256,128]{1,0:T(8,128)S(1)}, f32[256,128]{1,0:T(8,128)S(1)}, u32[]{:S(2)}, u32[]{:S(2)}) %collective-permute-start.5) | collective-permute-done | bytes 131104 | tf_op jit(solution)/shard_map/ppermute | solution.py:380
  43.2 0.0 collective-permute-done.6.below
  43.2 0.0 collective-permute-done.7.above
  43.2 7.2 %second_image.1 = (bf16[64,64,128]{2,1,0:T(8,128)(2,1)S(1)}, f32[128,128]{1,0:T(8,128)S(1)}) custom-call(s32[6,64]{1,0:T(8,128)S(1)} %bitcast.12, bf16[64,128,512]{2,1,0:T(8,128)(2,1)S(1)} %entries.1.mats_ref, bf16[64,64,128]{2,1,0:T(8,128)(2,1)S(1)} %get-tuple-element.26.image_ref.parts_ref, f32[256,128]{1,0:T(8,128)S(1)} %collective-permute-done.4.near, ...), custom_call_target="tpu_custom_call" | custom-call | flops 1000000000 | bytes 14000000 | tf_op jit(solution)/shard_map/second_image/pallas_call | solution.py:477
  50.5 0.0 copy-start.3
  50.5 1.0 copy-done.3
  51.4 15.9 %all_to_all.20 = f32[16,8,128]{2,1,0:T(8,128)S(1)} all-to-all(f32[16,8,128]{2,1,0:T(8,128)S(1)} %bitcast.10), channel_id=1, replica_groups=mesh['region'=16,'layer'=16] {'layer'}, dimensions={0} | all-to-all | bytes 131072 | tf_op jit(solution)/shard_map/all_to_all | solution.py:397
  67.3 14.7 %all_to_all.21 = f32[16,8,128]{2,1,0:T(8,128)S(1)} all-to-all(f32[16,8,128]{2,1,0:T(8,128)S(1)} %broadcast_in_dim.4), channel_id=1, replica_groups=mesh['region'=16,'layer'=16] {'region'}, dimensions={0} | all-to-all | bytes 131072 | tf_op jit(solution)/shard_map/all_to_all | solution.py:399
  82.0 0.6 broadcast_in_dim.5
  82.7 4.8 %all-to-all-start.2 = ((f32[16,8,128]{2,1,0:T(8,128)}), f32[16,8,128]{2,1,0:T(8,128)S(1)}, u32[]{:S(2)}, u32[]{:S(2)}) async-start(f32[16,8,128]{2,1,0:T(8,128)} %broadcast_in_dim.5), calls=%async_computation.2 | async-start | bytes 131072 | tf_op jit(solution)/shard_map/all_to_all | solution.py:401
  87.5 0.0 copy-done.9
  87.5 0.0 copy-done.10
  87.5 0.0 copy-start.2
  87.5 1.6 %copy-done.2 = f32[4096,128]{1,0:T(8,128)S(1)} copy-done((f32[4096,128]{1,0:T(8,128)S(1)}, f32[4096,128]{1,0:T(8,128)}, u32[]{:S(2)}) %copy-start.2) | copy-done | bytes 2097176
  89.1 4.0 %relay_rows.1 = f32[2048,128]{1,0:T(8,128)} custom-call(s32[512]{0:T(512)S(1)} %bitcast.13, s32[512]{0:T(512)S(1)} %copy-done.10, f32[4096,128]{1,0:T(8,128)S(1)} %copy-done.2), custom_call_target="tpu_custom_call" | custom-call | flops 1000000 | bytes 10000000 | tf_op jit(solution)/shard_map/relay_rows/pallas_call | solution.py:454
  93.1 0.7 all-to-all-done.2
  93.8 6.5 %all-to-all-start.3 = ((f32[16,128,128]{2,1,0:T(8,128)}), f32[16,128,128]{2,1,0:T(8,128)S(1)}, u32[]{:S(2)}, u32[]{:S(2)}) async-start(f32[16,128,128]{2,1,0:T(8,128)} %bitcast.5), calls=%async_computation.3 | async-start | bytes 2097152 | tf_op jit(solution)/shard_map/all_to_all | solution.py:464
  100.3 1.2 %copy-done.4 = bf16[64,64,128]{2,1,0:T(8,128)(2,1)S(1)} copy-done((bf16[64,64,128]{2,1,0:T(8,128)(2,1)S(1)}, bf16[64,64,128]{2,1,0:T(8,128)(2,1)}, u32[]{:S(2)}) %copy-start.4) | copy-done | bytes 1048600
  101.5 17.8 %final.1 = (f32[64,4096]{1,0:T(8,128)}, f32[64,4096]{1,0:T(8,128)}, f32[128,64]{1,0:T(8,128)S(1)}) custom-call(f32[128,128]{1,0:T(8,128)S(1)} %bitcast.9, bf16[64,64,128]{2,1,0:T(8,128)(2,1)S(1)} %get-tuple-element.20.parts_ref.field_ref, bf16[64,64,128]{2,1,0:T(8,128)(2,1)S(1)} %get-tuple-element.26.image_ref.parts_ref, bf16[64,64,128]{2,1,0:T(8,128)(2,1)S(1)} %copy-done.4), custom_call_target="tpu_custom_call" | custom-call | flops 500000000 | bytes 8000000 | tf_op jit(solution)/shard_map/final/pallas_call | solution.py:488
  119.3 0.0 all-to-all-done.3
  119.3 1.6 %owner_rows.1 = f32[16,8192]{1,0:T(8,128)} custom-call(f32[128,64]{1,0:T(8,128)S(1)} %get-tuple-element.35.coef_ref, f32[2048,128]{1,0:T(8,128)S(1)} %bitcast.8), custom_call_target="tpu_custom_call" | custom-call | flops 100000000 | bytes 2000000 | tf_op jit(solution)/shard_map/owner_rows/pallas_call | solution.py:499
  (8 shorter events, 0.1 us)
Async XLA Ops:
  0.6 1.2 %copy-start.5 = (f32[64,4096]{1,0:T(8,128)S(1)}, f32[64,4096]{1,0:T(8,128)}, u32[]{:S(2)}) copy-start(f32[64,4096]{1,0:T(8,128)} %right_ref.1) | copy-start | bytes 3145732
  1.9 0.7 copy-start.7
  4.5 20.2 %collective-permute-start = (f32[256,128]{1,0:T(8,128)S(1)}, f32[256,128]{1,0:T(8,128)S(1)}, u32[]{:S(2)}, u32[]{:S(2)}) collective-permute-start(f32[256,128]{1,0:T(8,128)S(1)} %get-tuple-element.22), channel_id=1, source_target_pairs={{0,16},{16,0},{32,48},{48,32},{64,80},{80,64},{96,112},{112,96},{1... | collective-permute-start | bytes 393224 | tf_op jit(solution)/shard_map/ppermute | solution.py:380
  4.6 20.1 %collective-permute-start.1 = (f32[256,128]{1,0:T(8,128)S(1)}, f32[256,128]{1,0:T(8,128)S(1)}, u32[]{:S(2)}, u32[]{:S(2)}) collective-permute-start(f32[256,128]{1,0:T(8,128)S(1)} %get-tuple-element.23), channel_id=1, source_target_pairs={{0,128},{16,144},{32,160},{48,176},{64,192},{80,208},{96,224},{112... | collective-permute-start | bytes 393224 | tf_op jit(solution)/shard_map/ppermute | solution.py:380
  11.9 12.9 %collective-permute-start.2 = (f32[256,128]{1,0:T(8,128)S(1)}, f32[256,128]{1,0:T(8,128)S(1)}, u32[]{:S(2)}, u32[]{:S(2)}) collective-permute-start(f32[256,128]{1,0:T(8,128)S(1)} %get-tuple-element.24), channel_id=1, source_target_pairs={{0,1},{1,2},{2,3},{3,4},{4,5},{5,6},{6,7},{7,8},{8,9},{9,10},{10,1... | collective-permute-start | bytes 393224 | tf_op jit(solution)/shard_map/ppermute | solution.py:388
  15.4 9.4 %collective-permute-start.3 = (f32[256,128]{1,0:T(8,128)S(1)}, f32[256,128]{1,0:T(8,128)S(1)}, u32[]{:S(2)}, u32[]{:S(2)}) collective-permute-start(f32[256,128]{1,0:T(8,128)S(1)} %get-tuple-element.25), channel_id=1, source_target_pairs={{1,0},{2,1},{3,2},{4,3},{5,4},{6,5},{7,6},{8,7},{9,8},{10,9},{11,1... | collective-permute-start | bytes 393224 | tf_op jit(solution)/shard_map/ppermute | solution.py:389
  17.7 3.1 %copy-start = (f32[64,7,4096]{2,0,1:T(8,128)S(1)}, f32[64,7,4096]{2,0,1:T(8,128)}, u32[]{:S(2)}) copy-start(f32[64,7,4096]{2,0,1:T(8,128)} %param.7) | copy-start | bytes 22020100
  20.8 3.9 %copy-start.6 = (s32[64,6]{0,1:T(8,128)S(1)}, s32[64,6]{0,1:T(8,128)}, u32[]{:S(2)}) copy-start(s32[64,6]{0,1:T(8,128)} %param.8) | copy-start | bytes 4612
  20.8 3.9 %copy-start.8 = (s32[4,8]{1,0:T(4,128)S(1)}, s32[4,8]{1,0:T(4,128)}, u32[]{:S(2)}) copy-start(s32[4,8]{1,0:T(4,128)} %face_rows.3) | copy-start | bytes 388
  29.9 1.3 %copy-start.1 = (f32[4096,128]{1,0:T(8,128)}, f32[4096,128]{1,0:T(8,128)S(1)}, u32[]{:S(2)}) copy-start(f32[4096,128]{1,0:T(8,128)S(1)} %get-tuple-element.36.both_ref) | copy-start | bytes 6291460
  31.3 56.2 %copy-start.9 = (s32[512,1]{0,1:T(1,128)S(1)}, s32[512,1]{0,1:T(1,128)}, u32[]{:S(2)}) copy-start(s32[512,1]{0,1:T(1,128)} %param.10) | copy-start | bytes 6148
  31.3 56.2 %copy-start.10 = (s32[512]{0:T(512)S(1)}, s32[512]{0:T(512)}, u32[]{:S(2)}) copy-start(s32[512]{0:T(512)} %die_node.1) | copy-start | bytes 6148
  31.3 8.2 %collective-permute-start.4 = (f32[256,128]{1,0:T(8,128)S(1)}, f32[256,128]{1,0:T(8,128)S(1)}, u32[]{:S(2)}, u32[]{:S(2)}) collective-permute-start(f32[256,128]{1,0:T(8,128)S(1)} %get-tuple-element.27), channel_id=1, source_target_pairs={{0,16},{16,0},{32,48},{48,32},{64,80},{80,64},{96,112},{112,96},{1... | collective-permute-start | bytes 393224 | tf_op jit(solution)/shard_map/ppermute | solution.py:380
  31.3 11.9 %collective-permute-start.5 = (f32[256,128]{1,0:T(8,128)S(1)}, f32[256,128]{1,0:T(8,128)S(1)}, u32[]{:S(2)}, u32[]{:S(2)}) collective-permute-start(f32[256,128]{1,0:T(8,128)S(1)} %get-tuple-element.28), channel_id=1, source_target_pairs={{0,128},{16,144},{32,160},{48,176},{64,192},{80,208},{96,224},{112... | collective-permute-start | bytes 393224 | tf_op jit(solution)/shard_map/ppermute | solution.py:380
  31.3 11.9 %collective-permute-start.6 = (f32[256,128]{1,0:T(8,128)S(1)}, f32[256,128]{1,0:T(8,128)S(1)}, u32[]{:S(2)}, u32[]{:S(2)}) collective-permute-start(f32[256,128]{1,0:T(8,128)S(1)} %get-tuple-element.29), channel_id=1, source_target_pairs={{0,1},{1,2},{2,3},{3,4},{4,5},{5,6},{6,7},{7,8},{8,9},{9,10},{10,1... | collective-permute-start | bytes 393224 | tf_op jit(solution)/shard_map/ppermute | solution.py:388
  34.8 8.4 %collective-permute-start.7 = (f32[256,128]{1,0:T(8,128)S(1)}, f32[256,128]{1,0:T(8,128)S(1)}, u32[]{:S(2)}, u32[]{:S(2)}) collective-permute-start(f32[256,128]{1,0:T(8,128)S(1)} %get-tuple-element.30), channel_id=1, source_target_pairs={{1,0},{2,1},{3,2},{4,3},{5,4},{6,5},{7,6},{8,7},{9,8},{10,9},{11,1... | collective-permute-start | bytes 393224 | tf_op jit(solution)/shard_map/ppermute | solution.py:389
  50.5 1.0 copy-start.3
  82.7 11.1 %all-to-all-start.2 = ((f32[16,8,128]{2,1,0:T(8,128)}), f32[16,8,128]{2,1,0:T(8,128)S(1)}, u32[]{:S(2)}, u32[]{:S(2)}) async-start(f32[16,8,128]{2,1,0:T(8,128)} %broadcast_in_dim.5), calls=%async_computation.2 | async-start | bytes 131072 | tf_op jit(solution)/shard_map/all_to_all | solution.py:401
  87.5 1.6 %copy-start.2 = (f32[4096,128]{1,0:T(8,128)S(1)}, f32[4096,128]{1,0:T(8,128)}, u32[]{:S(2)}) copy-start(f32[4096,128]{1,0:T(8,128)} %copy-done.1) | copy-start | bytes 6291460
  93.8 25.5 %all-to-all-start.3 = ((f32[16,128,128]{2,1,0:T(8,128)}), f32[16,128,128]{2,1,0:T(8,128)S(1)}, u32[]{:S(2)}, u32[]{:S(2)}) async-start(f32[16,128,128]{2,1,0:T(8,128)} %bitcast.5), calls=%async_computation.3 | async-start | bytes 2097152 | tf_op jit(solution)/shard_map/all_to_all | solution.py:464
  100.3 1.2 %copy-start.4 = (bf16[64,64,128]{2,1,0:T(8,128)(2,1)S(1)}, bf16[64,64,128]{2,1,0:T(8,128)(2,1)}, u32[]{:S(2)}) copy-start(bf16[64,64,128]{2,1,0:T(8,128)(2,1)} %copy-done.3) | copy-start | bytes 3145732

commit v2 on v1

--- a/solution.py
+++ b/solution.py
@@ -27,6 +27,10 @@
     return pltpu.CompilerParams(vmem_limit_bytes=mib * 1024 * 1024)
 
 
+def in_hbm(array):
+    return pltpu.with_memory_space_constraint(array, pltpu.HBM)
+
+
 def cost(flops, moved):
     return pl.CostEstimate(flops=flops, bytes_accessed=moved, transcendentals=0)
 
@@ -57,54 +61,77 @@
             face_ref[face * 32 : (face + 1) * 32, :] = jnp.where(left_lanes(32), upper, lower)
 
 
-def field_kernel(face_rows, right_ref, parts_ref, nodes_ref, *face_refs):
-    step = pl.program_id(0)
-    for chunk in range(STEP * BLOCK // LANES):
-        piece = right_ref[:, chunk * LANES : (chunk + 1) * LANES]
-        doubled = jnp.concatenate([piece, piece], axis=0).T
-        start = pl.multiple_of(step * STEP * BLOCK + chunk * LANES, LANES)
-        nodes_ref[pl.ds(start, LANES), :] = doubled
-        halves = two_parts(doubled)
-        parts_ref[step * STEP + 2 * chunk] = halves[:BLOCK]
-        parts_ref[step * STEP + 2 * chunk + 1] = halves[BLOCK:]
-
-    @pl.when(step == GRID - 1)
-    def _():
-        emit_faces(face_rows, nodes_ref, face_refs)
-
-
-def entries_kernel(raw_ref, mats_ref, rows_ref):
-    step = pl.program_id(0)
+def columns_of(step):
+    return pl.ds(pl.multiple_of(step * STEP * BLOCK, STEP * BLOCK), STEP * BLOCK)
+
+
+def field_kernel(
+    face_rows, right_hbm, parts_ref, turned_ref, nodes_ref, out0, out1, out2, out3, right_ref, sems
+):
+    copies = []
+    for step in range(GRID):
+        columns = pl.ds(step * STEP * BLOCK, STEP * BLOCK)
+        copies.append(
+            pltpu.make_async_copy(right_hbm.at[:, columns], right_ref.at[step], sems.at[step])
+        )
+        copies[step].start()
+    for step in range(GRID):
+        copies[step].wait()
+        lead, rest = halves_of(right_ref[step])
+        columns = slice(step * STEP * BLOCK, (step + 1) * STEP * BLOCK)
+        turned_ref[:RHS, columns] = lead
+        turned_ref[RHS:, columns] = rest
+        for chunk in range(STEP * BLOCK // LANES):
+            piece = right_ref[step, :, chunk * LANES : (chunk + 1) * LANES]
+            doubled = jnp.concatenate([piece, piece], axis=0).T
+            start = step * STEP * BLOCK + chunk * LANES
+            nodes_ref[start : start + LANES, :] = doubled
+            halves = two_parts(doubled)
+            parts_ref[step * STEP + 2 * chunk] = halves[:BLOCK]
+            parts_ref[step * STEP + 2 * chunk + 1] = halves[BLOCK:]
+    emit_faces(face_rows, nodes_ref, (out0, out1, out2, out3))
+
+
+def entries_kernel(raw_hbm, mats_ref, raw_ref, rows_ref, sems):
     half = left_lanes(32)
     lane = lax.broadcasted_iota(jnp.int32, (32, LANES), 1)
     twice = 2 * lax.broadcasted_iota(jnp.int32, (32, LANES), 0)
-    shift_even = jnp.where(lane == twice, SHIFT, 0.0)
-    shift_odd = jnp.where(lane == twice + 1, SHIFT, 0.0)
-    shift_odd = jnp.where(half, shift_odd, 0.0)
-    shift_even = jnp.where(half, shift_even, 0.0)
-    for k in range(COUPLED):
-        for pair in range(32):
-            rows_ref[pl.ds((k * 32 + pair) * STEP, STEP), :] = raw_ref[
-                k, :, pair * LANES : (pair + 1) * LANES
-            ]
-    for item in range(STEP):
-        for duo in range(4):
-            first = rows_ref[pl.ds(2 * duo * 256 + item, 32, stride=STEP), :]
-            if 2 * duo + 1 < COUPLED:
-                second = rows_ref[pl.ds((2 * duo + 1) * 256 + item, 32, stride=STEP), :]
-            else:
-                second = jnp.zeros_like(first)
-            even = jnp.where(half, first, pltpu.roll(second, RHS, 1))
-            odd = jnp.where(half, pltpu.roll(first, RHS, 1), second)
-            if duo == 0:
-                even = even - shift_even
-                odd = odd - shift_odd
-            stacked = jnp.concatenate([even, odd], axis=0)
-            lead = stacked.astype(BF16)
-            rest = (stacked - lead.astype(F32)).astype(BF16)
-            block = step * STEP + item
-            mats_ref[block, :BLOCK, duo * LANES : (duo + 1) * LANES] = lead
-            mats_ref[block, BLOCK:, duo * LANES : (duo + 1) * LANES] = rest
+    shift_even = jnp.where(jnp.logical_and(half, lane == twice), SHIFT, 0.0)
+    shift_odd = jnp.where(jnp.logical_and(half, lane == twice + 1), SHIFT, 0.0)
+
+    def fetch(step):
+        blocks = pl.ds(pl.multiple_of(step * STEP, STEP), STEP)
+        return pltpu.make_async_copy(raw_hbm.at[:, blocks], raw_ref.at[step], sems.at[step])
+
+    for step in range(GRID):
+        fetch(step).start()
+
+    def group(step, carry):
+        fetch(step).wait()
+        for k in range(COUPLED):
+            for pair in range(32):
+                rows_ref[pl.ds((k * 32 + pair) * STEP, STEP), :] = raw_ref[
+                    step, k, :, pair * LANES : (pair + 1) * LANES
+                ]
+        for item in range(STEP):
+            for duo in range(4):
+                first = rows_ref[pl.ds(2 * duo * 256 + item, 32, stride=STEP), :]
+                if 2 * duo + 1 < COUPLED:
+                    second = rows_ref[pl.ds((2 * duo + 1) * 256 + item, 32, stride=STEP), :]
+                else:
+                    second = jnp.zeros_like(first)
+                even = jnp.where(half, first, pltpu.roll(second, RHS, 1))
+                odd = jnp.where(half, pltpu.roll(first, RHS, 1), second)
+                if duo == 0:
+                    even = even - shift_even
+                    odd = odd - shift_odd
+                lead, rest = halves_of(jnp.concatenate([even, odd], axis=0))
+                block = step * STEP + item
+                mats_ref[block, :BLOCK, duo * LANES : (duo + 1) * LANES] = lead
+                mats_ref[block, BLOCK:, duo * LANES : (duo + 1) * LANES] = rest
+        return carry
+
+    lax.fori_loop(0, GRID, group, 0)
 
 
 def fill_extended(parts_ref, received, extended_ref):
@@ -124,10 +151,8 @@
     for k in range(COUPLED - 1):
         pieces.append(extended_ref[neighbours[k, block]])
     pieces.append(pieces[0])
-    product = jnp.dot(
-        mats_ref[block], jnp.concatenate(pieces, axis=0), preferred_element_type=F32
-    )
-    folded = product[:BLOCK] + product[BLOCK:]
+    grid = product(mats_ref[block], jnp.concatenate(pieces, axis=0))
+    folded = grid[:BLOCK] + grid[BLOCK:]
     doubled = folded + pltpu.roll(folded, RHS, 1)
     start = pl.multiple_of(block * BLOCK, BLOCK)
     nodes_ref[pl.ds(start, 32, stride=2), :] = doubled[:32]
@@ -154,10 +179,6 @@
     emit_faces(face_rows, nodes_ref, (out0, out1, out2, out3))
 
 
-def gram_of(left, right):
-    return lax.dot_general(left, right, (((0,), (0,)), ((), ())), preferred_element_type=F32)
-
-
 def quarter_sum(grid):
     tall = grid[:RHS] + grid[RHS:]
     return tall + pltpu.roll(tall, RHS, 1)
@@ -168,15 +189,23 @@
     return ref[pl.ds(first, STEP)].reshape(STEP * BLOCK, LANES)
 
 
-def gram_kernel(field_ref, image_ref, out_ref, wide_acc, acc_ref):
+def product(left, right):
+    return jnp.dot(left, right, preferred_element_type=F32)
+
+
+def gram_kernel(turned_ref, field_ref, image_ref, out_ref, image_turned_ref, wide_acc, acc_ref):
     wide_acc[...] = jnp.zeros_like(wide_acc)
     acc_ref[...] = jnp.zeros_like(acc_ref)
 
     def group(step, carry):
         field = rows_of(field_ref, step)
         image = rows_of(image_ref, step)
-        wide_acc[...] += gram_of(field, jnp.concatenate([field, image], axis=1))
-        acc_ref[...] += gram_of(image, image)
+        turned = image.T
+        image_turned_ref[:, columns_of(step)] = turned
+        wide_acc[...] += product(
+            turned_ref[:, columns_of(step)], jnp.concatenate([field, image], axis=1)
+        )
+        acc_ref[...] += product(turned, image)
         return carry
 
     lax.fori_loop(0, GRID, group, 0)
@@ -186,8 +215,8 @@
 
 
 def second_kernel(
-    neighbours, mats_ref, parts_ref, near, far, below, above, field_ref, gram_ref,
-    image_ref, sums_ref, extended_ref, nodes_ref, acc_ref,
+    neighbours, mats_ref, parts_ref, near, far, below, above, turned_ref, image_turned_ref,
+    gram_ref, outgoing_ref, image_ref, sums_ref, extended_ref, nodes_ref, acc_ref,
 ):
     fill_extended(parts_ref, (near, far, below, above), extended_ref)
     acc_ref[...] = jnp.zeros_like(acc_ref)
@@ -197,8 +226,9 @@
             block = step * STEP + item
             doubled = block_row(block, neighbours, mats_ref, extended_ref, nodes_ref)
             image_ref[block] = two_parts(doubled)
-        joined = jnp.concatenate([rows_of(field_ref, step), rows_of(parts_ref, step)], axis=1)
-        acc_ref[...] += gram_of(joined, rows_of(image_ref, step))
+        columns = columns_of(step)
+        both = jnp.concatenate([turned_ref[:, columns], image_turned_ref[:, columns]], axis=0)
+        acc_ref[...] += product(both, rows_of(image_ref, step))
         return carry
 
     lax.fori_loop(0, GRID, group, 0)
@@ -278,14 +308,47 @@
 
 
 def eliminate(systems):
-    row_id = lax.broadcasted_iota(jnp.int32, (RHS, 1), 0)
-    for k in range(RHS):
-        done = []
-        for system in systems:
-            pivot = system[k : k + 1, :] * (1.0 / system[k : k + 1, k : k + 1])
-            done.append(jnp.where(row_id == k, pivot, system - system[:, k : k + 1] * pivot))
-        systems = done
-    return [system[:, RHS:] for system in systems]
+    tall = 8
+    spread = (tall, LANES)
+    sub = lax.broadcasted_iota(jnp.int32, spread, 0)
+    grids = [[system[tall * r : tall * r + tall] for r in range(RHS // tall)] for system in systems]
+    for pivot in range(RHS // tall):
+        base = tall * pivot
+        for tiles in grids:
+            rows = tiles[pivot]
+            entry = {
+                (i, j): jnp.broadcast_to(rows[i : i + 1, base + j : base + j + 1], spread)
+                for i in range(tall)
+                for j in range(i + 1)
+            }
+            inverse, lower = [], {}
+            for r in range(tall):
+                inverse.append(1.0 / entry[r, r])
+                for i in range(r + 1, tall):
+                    lower[i, r] = entry[i, r] * inverse[r]
+                    for j in range(r + 1, i + 1):
+                        entry[i, j] = entry[i, j] - lower[i, r] * entry[j, r]
+            solved = [jnp.broadcast_to(rows[i : i + 1, :], spread) for i in range(tall)]
+            for i in range(tall):
+                for j in range(i):
+                    solved[i] = solved[i] - lower[i, j] * solved[j]
+            for i in reversed(range(tall)):
+                solved[i] = solved[i] * inverse[i]
+                for j in range(i + 1, tall):
+                    solved[i] = solved[i] - lower[j, i] * solved[j]
+            for r in range(RHS // tall):
+                if r == pivot:
+                    continue
+                old = tiles[r]
+                fresh = old
+                for i in range(tall):
+                    fresh = fresh - old[:, base + i : base + i + 1] * solved[i]
+                tiles[r] = fresh
+            merged = solved[0]
+            for i in range(1, tall):
+                merged = jnp.where(sub == i, solved[i], merged)
+            tiles[pivot] = merged
+    return [jnp.concatenate(tiles, axis=0)[:, RHS:] for tiles in grids]
 
 
 def wide(left, right):
@@ -322,7 +385,7 @@
 
 
 def final_kernel(
-    sums_ref, field_ref, image_ref, far_ref, solution_ref, residual_ref, coef_ref, weights_ref
+    sums_ref, turned_ref, image_turned_ref, far_ref, solution_ref, residual_ref, coef_ref, weights_ref
 ):
     step = pl.program_id(0)
 
@@ -339,11 +402,13 @@
         weights_ref[LANES:] = rest
         coef_ref[...] = jnp.concatenate([keep.T, -drop.T], axis=0)
 
-    basis = jnp.concatenate(
-        [rows_of(ref, step) for ref in (field_ref, image_ref, far_ref)], axis=1
-    )
-    mixed = lax.dot_general(
-        weights_ref[...], basis, (((1,), (1,)), ((), ())), preferred_element_type=F32
+    columns = columns_of(step)
+    both = jnp.concatenate([turned_ref[:, columns], image_turned_ref[:, columns]], axis=0)
+    mixed = product(weights_ref[:, : 2 * LANES], both) + lax.dot_general(
+        weights_ref[:, 2 * LANES :],
+        rows_of(far_ref, step),
+        (((1,), (1,)), ((), ())),
+        preferred_element_type=F32,
     )
     mixed = mixed[:LANES] + mixed[LANES:]
     solution_ref[...] = mixed[:RHS]
@@ -366,14 +431,12 @@
             )
         rows = jnp.concatenate(pieces, axis=0)
         lead, rest = halves_of(rows)
-        product = jnp.dot(
-            jnp.concatenate([lead, rest], axis=0), weights, preferred_element_type=F32
-        )
-        product = product[:LANES] + product[LANES:]
-        product = product[:, :LANES] + product[:, LANES:]
+        grid = product(jnp.concatenate([lead, rest], axis=0), weights)
+        grid = grid[:LANES] + grid[LANES:]
+        grid = grid[:, :LANES] + grid[:, LANES:]
         for at in range(8):
             pair = 8 * pack + at
-            out_ref[:, pair * LANES : (pair + 1) * LANES] = product[16 * at : 16 * at + 16]
+            out_ref[:, pair * LANES : (pair + 1) * LANES] = grid[16 * at : 16 * at + 16]
 
 
 def swap(shard, axis, bit):
@@ -401,6 +464,7 @@
     return lax.all_to_all(copies, "layer", 0, 0, tiled=True).reshape(LANES, LANES)
 
 
+TURNED = jax.ShapeDtypeStruct((LANES, NODES_DEV), BF16)
 PARTS = jax.ShapeDtypeStruct((BLK_DEV, BLOCK, LANES), BF16)
 NODE_ROWS = jax.ShapeDtypeStruct((NODES_DEV, LANES), F32)
 FACE = jax.ShapeDtypeStruct((FACES * 32, LANES), F32)
@@ -409,29 +473,38 @@
 
 
 def on_device(right_side, block_entries, neighbours, face_rows, die_owner, die_node):
-    owners = die_owner[:, 0]
-    neighbours = neighbours.T
-    entries = jnp.transpose(block_entries, (1, 0, 2))
+    owners = in_hbm(die_owner[:, 0])
+    die_node = in_hbm(die_node)
+    neighbours = in_hbm(neighbours.T)
+    face_rows = in_hbm(face_rows)
+    entries = in_hbm(jnp.transpose(block_entries, (1, 0, 2)))
+    right_side = in_hbm(right_side)
     outcome = pl.pallas_call(
         field_kernel,
-        grid=(GRID,),
-        in_specs=[smem(), FIELD_STEP],
-        out_specs=[resident()] * 6,
-        out_shape=[PARTS, NODE_ROWS] + [FACE] * 4,
+        in_specs=[smem(), pl.BlockSpec(memory_space=pl.ANY)],
+        out_specs=[resident()] * 7,
+        out_shape=[PARTS, TURNED, NODE_ROWS] + [FACE] * 4,
+        scratch_shapes=[
+            pltpu.VMEM((GRID, RHS, STEP * BLOCK), F32),
+            pltpu.SemaphoreType.DMA((GRID,)),
+        ],
         compiler_params=params(8),
         cost_estimate=cost(1_000_000, 5_000_000),
         name="field",
     )(face_rows, right_side)
-    field, own_rows, faces = outcome[0], outcome[1], outcome[2:]
+    field, turned, own_rows, faces = outcome[0], outcome[1], outcome[2], outcome[3:]
     received = exchange(faces)
     mats = pl.pallas_call(
         entries_kernel,
-        grid=(GRID,),
-        in_specs=[pl.BlockSpec((COUPLED, STEP, BLOCK * BLOCK), lambda i: (0, i, 0))],
+        in_specs=[pl.BlockSpec(memory_space=pl.ANY)],
         out_specs=resident(),
         out_shape=jax.ShapeDtypeStruct((BLK_DEV, 2 * BLOCK, 4 * LANES), BF16),
-        scratch_shapes=[pltpu.VMEM((COUPLED * 32 * STEP, LANES), F32)],
-        compiler_params=params(8),
+        scratch_shapes=[
+            pltpu.VMEM((GRID, COUPLED, STEP, BLOCK * BLOCK), F32),
+            pltpu.VMEM((COUPLED * 32 * STEP, LANES), F32),
+            pltpu.SemaphoreType.DMA((GRID,)),
+        ],
+        compiler_params=params(12),
         cost_estimate=cost(10_000_000, 16_000_000),
         name="entries",
     )(entries)
@@ -464,26 +537,26 @@
     relayed = lax.all_to_all(
         outgoing.reshape(16, SLOTS, LANES), "layer", 0, 0, tiled=True
     ).reshape(16 * SLOTS, LANES)
-    grams = pl.pallas_call(
+    grams, image_turned = pl.pallas_call(
         gram_kernel,
-        in_specs=[resident()] * 2,
-        out_specs=resident(),
-        out_shape=jax.ShapeDtypeStruct((3 * RHS, LANES), F32),
+        in_specs=[resident()] * 3,
+        out_specs=[resident()] * 2,
+        out_shape=[jax.ShapeDtypeStruct((3 * RHS, LANES), F32), TURNED],
         scratch_shapes=[pltpu.VMEM((LANES, 2 * LANES), F32), pltpu.VMEM((LANES, LANES), F32)],
         compiler_params=params(8),
         cost_estimate=cost(500_000_000, 2_000_000),
         name="near_grams",
-    )(field, image)
+    )(turned, field, image)
     far_image, sums = pl.pallas_call(
         second_kernel,
-        in_specs=[smem()] + [resident()] * 8,
+        in_specs=[smem()] + [resident()] * 9 + [pl.BlockSpec(memory_space=pl.ANY)],
         out_specs=[resident()] * 2,
         out_shape=[PARTS, jax.ShapeDtypeStruct((LANES, LANES), F32)],
         scratch_shapes=apply_scratch + [pltpu.VMEM((2 * LANES, LANES), F32)],
         compiler_params=params(8),
         cost_estimate=cost(1_000_000_000, 14_000_000),
         name="second_image",
-    )(neighbours, mats, image, *received, field, grams)
+    )(neighbours, mats, image, *received, turned, image_turned, grams, outgoing)
     sums = total(sums)
     solution_field, residual, coef = pl.pallas_call(
         final_kernel,
@@ -495,7 +568,7 @@
         compiler_params=params(8),
         cost_estimate=cost(500_000_000, 8_000_000),
         name="final",
-    )(sums, field, image, far_image)
+    )(sums, turned, image_turned, far_image)
     mech_temps = pl.pallas_call(
         owner_kernel,
         in_specs=[resident()] * 2,

time: 122 us -> 111 us (0.910)
  blocking collectives: 30.6 us -> 39.8 us
  local copies, waits for them, and re-layouts: 10.7 us -> 2.2 us
  starting transfers between devices: 30.4 us -> 25.4 us
  waiting for transfers between devices: 4.48 us -> 0.59 us
  Pallas kernels: 43.9 us -> 41.5 us
    all_to_all x0 -> x1, blocking collectives: none -> 10.9 us  [total(): lax.all_to_all(copies, 'layer', 0, 0, tiled=True).reshape(LANES, LANES)]
    unnamed x22 -> x4, local copies, waits for them, and re-layouts: 10.1 us -> 2.18 us
    all_to_all x1 -> x0, starting transfers between devices: 4.79 us -> none  [total(): lax.all_to_all(copies, 'layer', 0, 0, tiled=True).reshape(LANES, LANES)]
    pallas_call x1, Pallas kernels: 17.8 us -> 13.8 us  [on_device(): pl.pallas_call(final_kernel, grid=(GRID,), in_specs=[resident()] * 4, out...]
    ppermute x4, waiting for transfers between devices: 3.75 us -> 0.01 us  [swap(): lax.ppermute(shard, axis, [(i, i ^ bit) for i in range(lax.axis_size(axis...]
    all_to_all x1, blocking collectives: 15.9 us -> 14.2 us  [total(): mine = jnp.sum(lax.all_to_all(parts, 'layer', 0, 0, tiled=True), axis=0)]
    all_to_all x1, starting transfers between devices: 6.53 us -> 4.9 us  [on_device(): lax.all_to_all(outgoing.reshape(16, SLOTS, LANES), 'layer', 0, 0, tiled=T...]
    ppermute x4, starting transfers between devices: 7.42 us -> 8.79 us  [swap(): lax.ppermute(shard, axis, [(i, i ^ bit) for i in range(lax.axis_size(axis...]
  transfers between devices with their start and end apart: 10 -> 9, of which waited for: 2 -> 2; matrix products, arithmetic and copies ran while one was open for 0% -> 0% of each run, Pallas kernels for 23% -> 22%
where the time goes in v2:
time: 111 us; the launch traced here: 110 us
  Pallas kernels  41.5 us (37%)
  blocking collectives  39.8 us (36%)
  starting transfers between devices  25.4 us (23%)
  local copies, waits for them, and re-layouts  2.2 us (2%)
    all_to_all x1, blocking collectives, total(): mine = jnp.sum(lax.all_to_all(copies, 'region', 0, 0, tiled=True), axis=0)  14.7 us
    all_to_all x1, blocking collectives, total(): mine = jnp.sum(lax.all_to_all(parts, 'layer', 0, 0, tiled=True), axis=0)  14.2 us
    pallas_call x1, Pallas kernels, on_device(): pl.pallas_call(final_kernel, grid=(GRID,), in_specs=[resident()] * 4, out...  13.8 us
    all_to_all x1, blocking collectives, total(): lax.all_to_all(copies, 'layer', 0, 0, tiled=True).reshape(LANES, LANES)  10.9 us
    ppermute x4, starting transfers between devices, swap(): lax.ppermute(shard, axis, [(i, i ^ bit) for i in range(lax.axis_size(axis...  8.79 us
    pallas_call x1, Pallas kernels, on_device(): pl.pallas_call(second_kernel, in_specs=[smem()] + [resident()] * 9 + [pl....  7.07 us
    ppermute x2, starting transfers between devices, exchange(): lax.ppermute(faces[2], 'layer', [(i, i + 1) for i in range(count - 1)])  6.95 us
    pallas_call x1, Pallas kernels, on_device(): pl.pallas_call(first_kernel, in_specs=[smem(), smem()] + [resident()] * 7...  5.27 us
  transfers between devices with their start and end apart: 9, of which 2 were waited for; matrix products, arithmetic and copies ran while one was open for 0% of the time, Pallas kernels for 22%

profile of v2, /device:TPU:8, one launch (start us, length us, event | category | flops | bytes accessed | tf_op | source)
XLA Modules:
  0.0 110.2 jit_solution(4928234085289754107)
XLA Ops:
  0.6 2.9 %field.1 = (bf16[64,64,128]{2,1,0:T(8,128)(2,1)S(1)}, bf16[128,4096]{1,0:T(8,128)(2,1)S(1)}, f32[4096,128]{1,0:T(8,128)S(1)}, f32[256,128]{1,0:T(8,128)S(1)}, f3...) custom-call(s32[4,8]{1,0:T(4,128)} %face_rows.3, f32[64,4096]{1,0:T(8,128)} %right_hbm.1), custom_call_target="tpu_custom_call" | custom-call | flops 1000000 | bytes 5000000 | tf_op jit(solution)/shard_map/field/pallas_call | solution.py:482
  3.5 0.1 collective-permute-start
  3.6 7.3 %collective-permute-start.1 = (f32[256,128]{1,0:T(8,128)S(1)}, f32[256,128]{1,0:T(8,128)S(1)}, u32[]{:S(2)}, u32[]{:S(2)}) collective-permute-start(f32[256,128]{1,0:T(8,128)S(1)} %get-tuple-element.26), channel_id=1, source_target_pairs={{0,128},{16,144},{32,160},{48,176},{64,192},{80,208},{96,224},{112... | collective-permute-start | bytes 393224 | tf_op jit(solution)/shard_map/ppermute | solution.py:443
  10.9 3.5 %collective-permute-start.2 = (f32[256,128]{1,0:T(8,128)S(1)}, f32[256,128]{1,0:T(8,128)S(1)}, u32[]{:S(2)}, u32[]{:S(2)}) collective-permute-start(f32[256,128]{1,0:T(8,128)S(1)} %get-tuple-element.27), channel_id=1, source_target_pairs={{0,1},{1,2},{2,3},{3,4},{4,5},{5,6},{6,7},{7,8},{8,9},{9,10},{10,1... | collective-permute-start | bytes 393224 | tf_op jit(solution)/shard_map/ppermute | solution.py:451
  14.3 2.4 %collective-permute-start.3 = (f32[256,128]{1,0:T(8,128)S(1)}, f32[256,128]{1,0:T(8,128)S(1)}, u32[]{:S(2)}, u32[]{:S(2)}) collective-permute-start(f32[256,128]{1,0:T(8,128)S(1)} %get-tuple-element.28), channel_id=1, source_target_pairs={{1,0},{2,1},{3,2},{4,3},{5,4},{6,5},{7,6},{8,7},{9,8},{10,9},{11,1... | collective-permute-start | bytes 393224 | tf_op jit(solution)/shard_map/ppermute | solution.py:452
  16.7 4.6 %entries.1.mats_ref = bf16[64,128,512]{2,1,0:T(8,128)(2,1)S(1)} custom-call(f32[7,64,4096]{2,1,0:T(8,128)} %bitcast.10), custom_call_target="tpu_custom_call" | custom-call | flops 10000000 | bytes 16000000 | tf_op jit(solution)/shard_map/entries/pallas_call | solution.py:497
  21.3 0.0 collective-permute-done.near
  21.3 0.0 collective-permute-done.1.far
  21.3 0.0 collective-permute-done.2.below
  21.3 0.2 collective-permute-done.3.above
  21.5 5.3 %first_image.1 = (bf16[64,64,128]{2,1,0:T(8,128)(2,1)S(1)}, f32[4096,128]{1,0:T(8,128)S(1)}, f32[256,128]{1,0:T(8,128)S(1)}, f32[256,128]{1,0:T(8,128)S(1)}, f32...) custom-call(s32[6,64]{1,0:T(8,128)} %bitcast.11, s32[4,8]{1,0:T(4,128)} %face_rows.3, ...), custom_call_target="tpu_custom_call" | custom-call | flops 1000000000 | bytes 16000000 | tf_op jit(solution)/shard_map/first_image/pallas_call | solution.py:515
  26.8 0.1 collective-permute-start.4
  26.9 1.3 %collective-permute-start.5 = (f32[256,128]{1,0:T(8,128)S(1)}, f32[256,128]{1,0:T(8,128)S(1)}, u32[]{:S(2)}, u32[]{:S(2)}) collective-permute-start(f32[256,128]{1,0:T(8,128)S(1)} %get-tuple-element.31), channel_id=1, source_target_pairs={{0,128},{16,144},{32,160},{48,176},{64,192},{80,208},{96,224},{112... | collective-permute-start | bytes 393224 | tf_op jit(solution)/shard_map/ppermute | solution.py:443
  28.2 3.5 %collective-permute-start.6 = (f32[256,128]{1,0:T(8,128)S(1)}, f32[256,128]{1,0:T(8,128)S(1)}, u32[]{:S(2)}, u32[]{:S(2)}) collective-permute-start(f32[256,128]{1,0:T(8,128)S(1)} %get-tuple-element.32), channel_id=1, source_target_pairs={{0,1},{1,2},{2,3},{3,4},{4,5},{5,6},{6,7},{7,8},{8,9},{9,10},{10,1... | collective-permute-start | bytes 393224 | tf_op jit(solution)/shard_map/ppermute | solution.py:451
  31.7 2.4 %collective-permute-start.7 = (f32[256,128]{1,0:T(8,128)S(1)}, f32[256,128]{1,0:T(8,128)S(1)}, u32[]{:S(2)}, u32[]{:S(2)}) collective-permute-start(f32[256,128]{1,0:T(8,128)S(1)} %get-tuple-element.33), channel_id=1, source_target_pairs={{1,0},{2,1},{3,2},{4,3},{5,4},{6,5},{7,6},{8,7},{9,8},{10,9},{11,1... | collective-permute-start | bytes 393224 | tf_op jit(solution)/shard_map/ppermute | solution.py:452
  34.1 4.1 %relay_rows.1.outgoing_ref = f32[2048,128]{1,0:T(8,128)} custom-call(s32[512]{0:T(512)} %bitcast.13, s32[512]{0:T(512)} %die_node.1, f32[4096,128]{1,0:T(8,128)S(1)} %get-tuple-element.37.both_ref), custom_call_target="tpu_custom_call" | custom-call | flops 1000000 | bytes 10000000 | tf_op jit(solution)/shard_map/relay_rows/pallas_call | solution.py:527
  38.2 2.1 %near_grams.1 = (f32[192,128]{1,0:T(8,128)S(1)}, bf16[128,4096]{1,0:T(8,128)(2,1)S(1)}) custom-call(bf16[128,4096]{1,0:T(8,128)(2,1)S(1)} %get-tuple-element.34.turned_ref, bf16[64,64,128]{2,1,0:T(8,128)(2,1)S(1)} %get-tuple-element.23.parts_ref.field_ref, bf16[64,64,128]{2,1,0:T(8,128)(2,1)S(1)} %get-tuple-element.29.image_ref.parts_ref), custom_call_target="tpu_custom_call" | custom-call | flops 500000000 | bytes 2000000 | tf_op jit(solution)/shard_map/near_grams/pallas_call | solution.py:540
  40.3 0.0 collective-permute-done.4.near
  40.3 0.0 collective-permute-done.5.far
  40.3 0.0 collective-permute-done.6.below
  40.4 0.0 collective-permute-done.7.above
  40.4 7.1 %second_image.1 = (bf16[64,64,128]{2,1,0:T(8,128)(2,1)S(1)}, f32[128,128]{1,0:T(8,128)S(1)}) custom-call(s32[6,64]{1,0:T(8,128)} %bitcast.12, bf16[64,128,512]{2,1,0:T(8,128)(2,1)S(1)} %entries.1.mats_ref, bf16[64,64,128]{2,1,0:T(8,128)(2,1)S(1)} %get-tuple-element.29.image_ref.parts_ref, f32[256,128]{1,0:T(8,128)S(1)} %collective-permute-done.4.near, ...), custom_call_target="tpu_custom_call" | custom-call | flops 1000000000 | bytes 14000000 | tf_op jit(solution)/shard_map/second_image/pallas_call | solution.py:550
  47.4 0.0 copy-start
  47.4 1.0 copy-done
  48.4 14.2 %all_to_all.20 = f32[16,8,128]{2,1,0:T(8,128)S(1)} all-to-all(f32[16,8,128]{2,1,0:T(8,128)S(1)} %bitcast.9), channel_id=1, replica_groups=mesh['region'=16,'layer'=16] {'layer'}, dimensions={0} | all-to-all | bytes 131072 | tf_op jit(solution)/shard_map/all_to_all | solution.py:460
  62.6 14.7 %all_to_all.21 = f32[16,8,128]{2,1,0:T(8,128)S(1)} all-to-all(f32[16,8,128]{2,1,0:T(8,128)S(1)} %broadcast_in_dim.4), channel_id=1, replica_groups=mesh['region'=16,'layer'=16] {'region'}, dimensions={0} | all-to-all | bytes 131072 | tf_op jit(solution)/shard_map/all_to_all | solution.py:462
  77.3 10.9 %all_to_all.22 = f32[16,8,128]{2,1,0:T(8,128)S(1)} all-to-all(f32[16,8,128]{2,1,0:T(8,128)S(1)} %broadcast_in_dim.5), channel_id=1, replica_groups=mesh['region'=16,'layer'=16] {'layer'}, dimensions={0} | all-to-all | bytes 131072 | tf_op jit(solution)/shard_map/all_to_all | solution.py:464
  88.2 4.9 %all-to-all-start.3 = ((f32[16,128,128]{2,1,0:T(8,128)}), f32[16,128,128]{2,1,0:T(8,128)S(1)}, u32[]{:S(2)}, u32[]{:S(2)}) async-start(f32[16,128,128]{2,1,0:T(8,128)} %bitcast.5), calls=%async_computation.3 | async-start | bytes 2097152 | tf_op jit(solution)/shard_map/all_to_all | solution.py:537
  93.1 0.0 copy-start.1
  93.1 1.2 %copy-done.1 = bf16[64,64,128]{2,1,0:T(8,128)(2,1)S(1)} copy-done((bf16[64,64,128]{2,1,0:T(8,128)(2,1)S(1)}, bf16[64,64,128]{2,1,0:T(8,128)(2,1)}, u32[]{:S(2)}) %copy-start.1) | copy-done | bytes 1048600
  94.4 13.8 %final.1 = (f32[64,4096]{1,0:T(8,128)}, f32[64,4096]{1,0:T(8,128)}, f32[128,64]{1,0:T(8,128)S(1)}) custom-call(f32[128,128]{1,0:T(8,128)S(1)} %bitcast.8, bf16[128,4096]{1,0:T(8,128)(2,1)S(1)} %get-tuple-element.34.turned_ref, bf16[128,4096]{1,0:T(8,128)(2,1)S(1)} %get-tuple-element.35.image_turned_ref, bf16[64,64,128]{2,1,0:T(8,128)(2,1)S(1)} %copy-done.1), custom_call_target="tpu_custom_call" | custom-call | flops 500000000 | bytes 8000000 | tf_op jit(solution)/shard_map/final/pallas_call | solution.py:561
  108.2 0.4 all-to-all-done.3
  108.6 1.6 %owner_rows.1 = f32[16,8192]{1,0:T(8,128)} custom-call(f32[128,64]{1,0:T(8,128)S(1)} %get-tuple-element.42.coef_ref, f32[2048,128]{1,0:T(8,128)S(1)} %bitcast.7), custom_call_target="tpu_custom_call" | custom-call | flops 100000000 | bytes 2000000 | tf_op jit(solution)/shard_map/owner_rows/pallas_call | solution.py:572
  (4 shorter events, 0.1 us)
Async XLA Ops:
  3.5 17.8 %collective-permute-start = (f32[256,128]{1,0:T(8,128)S(1)}, f32[256,128]{1,0:T(8,128)S(1)}, u32[]{:S(2)}, u32[]{:S(2)}) collective-permute-start(f32[256,128]{1,0:T(8,128)S(1)} %get-tuple-element.25), channel_id=1, source_target_pairs={{0,16},{16,0},{32,48},{48,32},{64,80},{80,64},{96,112},{112,96},{1... | collective-permute-start | bytes 393224 | tf_op jit(solution)/shard_map/ppermute | solution.py:443
  3.6 17.7 %collective-permute-start.1 = (f32[256,128]{1,0:T(8,128)S(1)}, f32[256,128]{1,0:T(8,128)S(1)}, u32[]{:S(2)}, u32[]{:S(2)}) collective-permute-start(f32[256,128]{1,0:T(8,128)S(1)} %get-tuple-element.26), channel_id=1, source_target_pairs={{0,128},{16,144},{32,160},{48,176},{64,192},{80,208},{96,224},{112... | collective-permute-start | bytes 393224 | tf_op jit(solution)/shard_map/ppermute | solution.py:443
  10.9 10.5 %collective-permute-start.2 = (f32[256,128]{1,0:T(8,128)S(1)}, f32[256,128]{1,0:T(8,128)S(1)}, u32[]{:S(2)}, u32[]{:S(2)}) collective-permute-start(f32[256,128]{1,0:T(8,128)S(1)} %get-tuple-element.27), channel_id=1, source_target_pairs={{0,1},{1,2},{2,3},{3,4},{4,5},{5,6},{6,7},{7,8},{8,9},{9,10},{10,1... | collective-permute-start | bytes 393224 | tf_op jit(solution)/shard_map/ppermute | solution.py:451
  14.3 7.2 %collective-permute-start.3 = (f32[256,128]{1,0:T(8,128)S(1)}, f32[256,128]{1,0:T(8,128)S(1)}, u32[]{:S(2)}, u32[]{:S(2)}) collective-permute-start(f32[256,128]{1,0:T(8,128)S(1)} %get-tuple-element.28), channel_id=1, source_target_pairs={{1,0},{2,1},{3,2},{4,3},{5,4},{6,5},{7,6},{8,7},{9,8},{10,9},{11,1... | collective-permute-start | bytes 393224 | tf_op jit(solution)/shard_map/ppermute | solution.py:452
  26.8 13.5 %collective-permute-start.4 = (f32[256,128]{1,0:T(8,128)S(1)}, f32[256,128]{1,0:T(8,128)S(1)}, u32[]{:S(2)}, u32[]{:S(2)}) collective-permute-start(f32[256,128]{1,0:T(8,128)S(1)} %get-tuple-element.30), channel_id=1, source_target_pairs={{0,16},{16,0},{32,48},{48,32},{64,80},{80,64},{96,112},{112,96},{1... | collective-permute-start | bytes 393224 | tf_op jit(solution)/shard_map/ppermute | solution.py:443
  26.9 13.4 %collective-permute-start.5 = (f32[256,128]{1,0:T(8,128)S(1)}, f32[256,128]{1,0:T(8,128)S(1)}, u32[]{:S(2)}, u32[]{:S(2)}) collective-permute-start(f32[256,128]{1,0:T(8,128)S(1)} %get-tuple-element.31), channel_id=1, source_target_pairs={{0,128},{16,144},{32,160},{48,176},{64,192},{80,208},{96,224},{112... | collective-permute-start | bytes 393224 | tf_op jit(solution)/shard_map/ppermute | solution.py:443
  28.2 12.1 %collective-permute-start.6 = (f32[256,128]{1,0:T(8,128)S(1)}, f32[256,128]{1,0:T(8,128)S(1)}, u32[]{:S(2)}, u32[]{:S(2)}) collective-permute-start(f32[256,128]{1,0:T(8,128)S(1)} %get-tuple-element.32), channel_id=1, source_target_pairs={{0,1},{1,2},{2,3},{3,4},{4,5},{5,6},{6,7},{7,8},{8,9},{9,10},{10,1... | collective-permute-start | bytes 393224 | tf_op jit(solution)/shard_map/ppermute | solution.py:451
  31.7 8.7 %collective-permute-start.7 = (f32[256,128]{1,0:T(8,128)S(1)}, f32[256,128]{1,0:T(8,128)S(1)}, u32[]{:S(2)}, u32[]{:S(2)}) collective-permute-start(f32[256,128]{1,0:T(8,128)S(1)} %get-tuple-element.33), channel_id=1, source_target_pairs={{1,0},{2,1},{3,2},{4,3},{5,4},{6,5},{7,6},{8,7},{9,8},{10,9},{11,1... | collective-permute-start | bytes 393224 | tf_op jit(solution)/shard_map/ppermute | solution.py:452
  47.4 1.0 copy-start
  88.2 20.3 %all-to-all-start.3 = ((f32[16,128,128]{2,1,0:T(8,128)}), f32[16,128,128]{2,1,0:T(8,128)S(1)}, u32[]{:S(2)}, u32[]{:S(2)}) async-start(f32[16,128,128]{2,1,0:T(8,128)} %bitcast.5), calls=%async_computation.3 | async-start | bytes 2097152 | tf_op jit(solution)/shard_map/all_to_all | solution.py:537
  93.1 1.2 %copy-start.1 = (bf16[64,64,128]{2,1,0:T(8,128)(2,1)S(1)}, bf16[64,64,128]{2,1,0:T(8,128)(2,1)}, u32[]{:S(2)}) copy-start(bf16[64,64,128]{2,1,0:T(8,128)(2,1)} %copy-done) | copy-start | bytes 3145732

commit v3 on v2

--- a/solution.py
+++ b/solution.py
@@ -19,12 +19,17 @@
 STEP = 8
 GRID = BLK_DEV // STEP
 SHIFT = 1.5
+SAVE_ENDS = (47, 63)
 BF16 = jnp.bfloat16
 F32 = jnp.float32
 
 
 def params(mib):
     return pltpu.CompilerParams(vmem_limit_bytes=mib * 1024 * 1024)
+
+
+def far_memory():
+    return pl.BlockSpec(memory_space=pltpu.HBM)
 
 
 def in_hbm(array):
@@ -62,7 +67,7 @@
 
 
 def columns_of(step):
-    return pl.ds(pl.multiple_of(step * STEP * BLOCK, STEP * BLOCK), STEP * BLOCK)
+    return slice(step * STEP * BLOCK, (step + 1) * STEP * BLOCK)
 
 
 def field_kernel(
@@ -100,13 +105,13 @@
     shift_odd = jnp.where(jnp.logical_and(half, lane == twice + 1), SHIFT, 0.0)
 
     def fetch(step):
-        blocks = pl.ds(pl.multiple_of(step * STEP, STEP), STEP)
+        blocks = pl.ds(step * STEP, STEP)
         return pltpu.make_async_copy(raw_hbm.at[:, blocks], raw_ref.at[step], sems.at[step])
 
     for step in range(GRID):
         fetch(step).start()
 
-    def group(step, carry):
+    for step in range(GRID):
         fetch(step).wait()
         for k in range(COUPLED):
             for pair in range(32):
@@ -129,9 +134,6 @@
                 block = step * STEP + item
                 mats_ref[block, :BLOCK, duo * LANES : (duo + 1) * LANES] = lead
                 mats_ref[block, BLOCK:, duo * LANES : (duo + 1) * LANES] = rest
-        return carry
-
-    lax.fori_loop(0, GRID, group, 0)
 
 
 def fill_extended(parts_ref, received, extended_ref):
@@ -154,7 +156,7 @@
     grid = product(mats_ref[block], jnp.concatenate(pieces, axis=0))
     folded = grid[:BLOCK] + grid[BLOCK:]
     doubled = folded + pltpu.roll(folded, RHS, 1)
-    start = pl.multiple_of(block * BLOCK, BLOCK)
+    start = block * BLOCK
     nodes_ref[pl.ds(start, 32, stride=2), :] = doubled[:32]
     nodes_ref[pl.ds(start + 1, 32, stride=2), :] = doubled[32:]
     return nodes_ref[pl.ds(start, BLOCK), :]
@@ -162,21 +164,24 @@
 
 def first_kernel(
     neighbours, face_rows, mats_ref, parts_ref, own_ref, near, far, below, above,
-    image_ref, both_ref, out0, out1, out2, out3, extended_ref, nodes_ref,
+    image_ref, both_hbm, out0, out1, out2, out3, extended_ref, nodes_ref, both_ref, sem,
 ):
+    def save(at):
+        first = SAVE_ENDS[at - 1] + 1 if at else 0
+        part = pl.ds(first * BLOCK, (SAVE_ENDS[at] + 1 - first) * BLOCK)
+        return pltpu.make_async_copy(both_ref.at[part], both_hbm.at[part], sem.at[at])
+
     fill_extended(parts_ref, (near, far, below, above), extended_ref)
-
-    def group(step, carry):
-        for item in range(STEP):
-            block = step * STEP + item
-            doubled = block_row(block, neighbours, mats_ref, extended_ref, nodes_ref)
-            image_ref[block] = two_parts(doubled)
-            rows = pl.ds(pl.multiple_of(block * BLOCK, BLOCK), BLOCK)
-            both_ref[rows, :] = jnp.where(left_lanes(BLOCK), own_ref[rows, :], doubled)
-        return carry
-
-    lax.fori_loop(0, GRID, group, 0)
+    for block in range(BLK_DEV):
+        doubled = block_row(block, neighbours, mats_ref, extended_ref, nodes_ref)
+        image_ref[block] = two_parts(doubled)
+        rows = slice(block * BLOCK, (block + 1) * BLOCK)
+        both_ref[rows, :] = jnp.where(left_lanes(BLOCK), own_ref[rows, :], doubled)
+        if block in SAVE_ENDS:
+            save(SAVE_ENDS.index(block)).start()
     emit_faces(face_rows, nodes_ref, (out0, out1, out2, out3))
+    for at in range(len(SAVE_ENDS)):
+        save(at).wait()
 
 
 def quarter_sum(grid):
@@ -185,8 +190,7 @@
 
 
 def rows_of(ref, step):
-    first = pl.multiple_of(step * STEP, STEP)
-    return ref[pl.ds(first, STEP)].reshape(STEP * BLOCK, LANES)
+    return ref[step * STEP : (step + 1) * STEP].reshape(STEP * BLOCK, LANES)
 
 
 def product(left, right):
@@ -196,8 +200,7 @@
 def gram_kernel(turned_ref, field_ref, image_ref, out_ref, image_turned_ref, wide_acc, acc_ref):
     wide_acc[...] = jnp.zeros_like(wide_acc)
     acc_ref[...] = jnp.zeros_like(acc_ref)
-
-    def group(step, carry):
+    for step in range(GRID):
         field = rows_of(field_ref, step)
         image = rows_of(image_ref, step)
         turned = image.T
@@ -206,9 +209,6 @@
             turned_ref[:, columns_of(step)], jnp.concatenate([field, image], axis=1)
         )
         acc_ref[...] += product(turned, image)
-        return carry
-
-    lax.fori_loop(0, GRID, group, 0)
     out_ref[:RHS, :] = quarter_sum(wide_acc[:, :LANES])
     out_ref[RHS:LANES, :] = quarter_sum(wide_acc[:, LANES:])
     out_ref[LANES:, :] = quarter_sum(acc_ref[...])
@@ -216,22 +216,19 @@
 
 def second_kernel(
     neighbours, mats_ref, parts_ref, near, far, below, above, turned_ref, image_turned_ref,
-    gram_ref, outgoing_ref, image_ref, sums_ref, extended_ref, nodes_ref, acc_ref,
+    gram_ref, image_hbm, sums_ref, extended_ref, nodes_ref, image_ref, acc_ref, sem,
 ):
     fill_extended(parts_ref, (near, far, below, above), extended_ref)
     acc_ref[...] = jnp.zeros_like(acc_ref)
-
-    def group(step, carry):
-        for item in range(STEP):
-            block = step * STEP + item
-            doubled = block_row(block, neighbours, mats_ref, extended_ref, nodes_ref)
-            image_ref[block] = two_parts(doubled)
+    for block in range(BLK_DEV):
+        doubled = block_row(block, neighbours, mats_ref, extended_ref, nodes_ref)
+        image_ref[block] = two_parts(doubled)
+    saving = pltpu.make_async_copy(image_ref, image_hbm, sem)
+    saving.start()
+    for step in range(GRID):
         columns = columns_of(step)
         both = jnp.concatenate([turned_ref[:, columns], image_turned_ref[:, columns]], axis=0)
         acc_ref[...] += product(both, rows_of(image_ref, step))
-        return carry
-
-    lax.fori_loop(0, GRID, group, 0)
     pack_sums(
         gram_ref[:RHS, :],
         gram_ref[RHS:LANES, :],
@@ -240,6 +237,7 @@
         quarter_sum(acc_ref[LANES:]),
         sums_ref,
     )
+    saving.wait()
 
 
 def pack_sums(norm, curve, image_norm, far_field, far_image, sums_ref):
@@ -278,10 +276,13 @@
     return norm, curve, image_norm, far_field, far_image
 
 
-def relay_kernel(owners, die_node, both_ref, out_ref, counts):
+def relay_kernel(owners, die_node, both_hbm, sums_hbm, out_ref, counts, both_ref, sem):
+    fetch = pltpu.make_async_copy(both_hbm, both_ref, sem)
+    fetch.start()
     out_ref[...] = jnp.zeros_like(out_ref)
     for owner in range(16):
         counts[owner] = owner * SLOTS
+    fetch.wait()
 
     def move(row, carry):
         owner = owners[row]
@@ -385,34 +386,43 @@
 
 
 def final_kernel(
-    sums_ref, turned_ref, image_turned_ref, far_ref, solution_ref, residual_ref, coef_ref, weights_ref
+    sums_ref, turned_ref, image_turned_ref, far_hbm, solution_hbm, residual_hbm, coef_ref,
+    far_ref, solution_ref, residual_ref, far_sem, sems,
 ):
-    step = pl.program_id(0)
-
-    @pl.when(step == 0)
-    def _():
-        keep, drop, left_over, taken = solve_steps(sums_ref)
-        top = [wide(keep, keep), wide(-drop, -drop), jnp.zeros((RHS, LANES), F32)]
-        low = [wide(left_over, left_over), wide(-taken, -taken), wide(drop, drop)]
-        rows = jnp.concatenate(
-            [jnp.concatenate(top, axis=1), jnp.concatenate(low, axis=1)], axis=0
+    fetch = pltpu.make_async_copy(far_hbm, far_ref, far_sem)
+    fetch.start()
+    keep, drop, left_over, taken = solve_steps(sums_ref)
+    top = [wide(keep, keep), wide(-drop, -drop), jnp.zeros((RHS, LANES), F32)]
+    low = [wide(left_over, left_over), wide(-taken, -taken), wide(drop, drop)]
+    rows = jnp.concatenate(
+        [jnp.concatenate(top, axis=1), jnp.concatenate(low, axis=1)], axis=0
+    )
+    weights = jnp.concatenate(halves_of(rows), axis=0)
+    coef_ref[...] = jnp.concatenate([keep.T, -drop.T], axis=0)
+    fetch.wait()
+    copies = []
+    for step in range(GRID):
+        columns = columns_of(step)
+        both = jnp.concatenate([turned_ref[:, columns], image_turned_ref[:, columns]], axis=0)
+        mixed = product(weights[:, : 2 * LANES], both) + lax.dot_general(
+            weights[:, 2 * LANES :],
+            rows_of(far_ref, step),
+            (((1,), (1,)), ((), ())),
+            preferred_element_type=F32,
         )
-        lead, rest = halves_of(rows)
-        weights_ref[:LANES] = lead
-        weights_ref[LANES:] = rest
-        coef_ref[...] = jnp.concatenate([keep.T, -drop.T], axis=0)
-
-    columns = columns_of(step)
-    both = jnp.concatenate([turned_ref[:, columns], image_turned_ref[:, columns]], axis=0)
-    mixed = product(weights_ref[:, : 2 * LANES], both) + lax.dot_general(
-        weights_ref[:, 2 * LANES :],
-        rows_of(far_ref, step),
-        (((1,), (1,)), ((), ())),
-        preferred_element_type=F32,
-    )
-    mixed = mixed[:LANES] + mixed[LANES:]
-    solution_ref[...] = mixed[:RHS]
-    residual_ref[...] = mixed[RHS:]
+        mixed = mixed[:LANES] + mixed[LANES:]
+        solution_ref[:, columns] = mixed[:RHS]
+        residual_ref[:, columns] = mixed[RHS:]
+        part = pl.ds(step * STEP * BLOCK, STEP * BLOCK)
+        for at, (source, target) in enumerate(
+            ((solution_ref, solution_hbm), (residual_ref, residual_hbm))
+        ):
+            copies.append(
+                pltpu.make_async_copy(source.at[:, part], target.at[:, part], sems.at[at, step])
+            )
+            copies[-1].start()
+    for copy in copies:
+        copy.wait()
 
 
 def owner_kernel(coef_ref, got_ref, out_ref):
@@ -469,7 +479,6 @@
 NODE_ROWS = jax.ShapeDtypeStruct((NODES_DEV, LANES), F32)
 FACE = jax.ShapeDtypeStruct((FACES * 32, LANES), F32)
 FIELD = jax.ShapeDtypeStruct((RHS, NODES_DEV), F32)
-FIELD_STEP = pl.BlockSpec((RHS, STEP * BLOCK), lambda i: (0, i))
 
 
 def on_device(right_side, block_entries, neighbours, face_rows, die_owner, die_node):
@@ -515,28 +524,16 @@
     outcome = pl.pallas_call(
         first_kernel,
         in_specs=[smem(), smem()] + [resident()] * 7,
-        out_specs=[resident()] * 6,
-        out_shape=[PARTS, NODE_ROWS] + [FACE] * 4,
-        scratch_shapes=apply_scratch,
+        out_specs=[resident(), far_memory()] + [resident()] * 4,
+        out_shape=[PARTS, pltpu.HBM(NODE_ROWS.shape, F32)] + [FACE] * 4,
+        scratch_shapes=apply_scratch
+        + [pltpu.VMEM((NODES_DEV, LANES), F32), pltpu.SemaphoreType.DMA((len(SAVE_ENDS),))],
         compiler_params=params(8),
         cost_estimate=cost(1_000_000_000, 16_000_000),
         name="first_image",
     )(neighbours, face_rows, mats, field, own_rows, *received)
     image, both_rows, faces = outcome[0], outcome[1], outcome[2:]
     received = exchange(faces)
-    outgoing = pl.pallas_call(
-        relay_kernel,
-        in_specs=[smem(), smem(), resident()],
-        out_specs=resident(),
-        out_shape=jax.ShapeDtypeStruct((16 * SLOTS, LANES), F32),
-        scratch_shapes=[pltpu.SMEM((16,), jnp.int32)],
-        compiler_params=params(8),
-        cost_estimate=cost(1_000_000, 10_000_000),
-        name="relay_rows",
-    )(owners, die_node, both_rows)
-    relayed = lax.all_to_all(
-        outgoing.reshape(16, SLOTS, LANES), "layer", 0, 0, tiled=True
-    ).reshape(16 * SLOTS, LANES)
     grams, image_turned = pl.pallas_call(
         gram_kernel,
         in_specs=[resident()] * 3,
@@ -547,28 +544,58 @@
         cost_estimate=cost(500_000_000, 2_000_000),
         name="near_grams",
     )(turned, field, image)
-    far_image, sums = pl.pallas_call(
+    far_image, local_sums = pl.pallas_call(
         second_kernel,
-        in_specs=[smem()] + [resident()] * 9 + [pl.BlockSpec(memory_space=pl.ANY)],
-        out_specs=[resident()] * 2,
-        out_shape=[PARTS, jax.ShapeDtypeStruct((LANES, LANES), F32)],
-        scratch_shapes=apply_scratch + [pltpu.VMEM((2 * LANES, LANES), F32)],
+        in_specs=[smem()] + [resident()] * 9,
+        out_specs=[far_memory(), resident()],
+        out_shape=[
+            pltpu.HBM(PARTS.shape, BF16),
+            jax.ShapeDtypeStruct((LANES, LANES), F32),
+        ],
+        scratch_shapes=apply_scratch
+        + [
+            pltpu.VMEM(PARTS.shape, BF16),
+            pltpu.VMEM((2 * LANES, LANES), F32),
+            pltpu.SemaphoreType.DMA,
+        ],
         compiler_params=params(8),
         cost_estimate=cost(1_000_000_000, 14_000_000),
         name="second_image",
-    )(neighbours, mats, image, *received, turned, image_turned, grams, outgoing)
-    sums = total(sums)
+    )(neighbours, mats, image, *received, turned, image_turned, grams)
+    outgoing = pl.pallas_call(
+        relay_kernel,
+        in_specs=[smem(), smem(), far_memory(), pl.BlockSpec(memory_space=pl.ANY)],
+        out_specs=resident(),
+        out_shape=jax.ShapeDtypeStruct((16 * SLOTS, LANES), F32),
+        scratch_shapes=[
+            pltpu.SMEM((16,), jnp.int32),
+            pltpu.VMEM((NODES_DEV, LANES), F32),
+            pltpu.SemaphoreType.DMA,
+        ],
+        compiler_params=params(8),
+        cost_estimate=cost(1_000_000, 10_000_000),
+        name="relay_rows",
+    )(owners, die_node, in_hbm(both_rows), local_sums)
+    relayed = lax.all_to_all(
+        outgoing.reshape(16, SLOTS, LANES), "layer", 0, 0, tiled=True
+    ).reshape(16 * SLOTS, LANES)
+    sums = total(local_sums)
     solution_field, residual, coef = pl.pallas_call(
         final_kernel,
-        grid=(GRID,),
-        in_specs=[resident()] * 4,
-        out_specs=[FIELD_STEP, FIELD_STEP, resident()],
+        in_specs=[resident()] * 3 + [far_memory()],
+        out_specs=[far_memory()] * 2 + [resident()],
         out_shape=[FIELD, FIELD, jax.ShapeDtypeStruct((LANES, RHS), F32)],
-        scratch_shapes=[pltpu.VMEM((2 * LANES, 3 * LANES), BF16)],
+        scratch_shapes=[
+            pltpu.VMEM(PARTS.shape, BF16),
+            pltpu.VMEM(FIELD.shape, F32),
+            pltpu.VMEM(FIELD.shape, F32),
+            pltpu.SemaphoreType.DMA,
+            pltpu.SemaphoreType.DMA((2, GRID)),
+        ],
         compiler_params=params(8),
         cost_estimate=cost(500_000_000, 8_000_000),
         name="final",
-    )(sums, turned, image_turned, far_image)
+    )(sums, turned, image_turned, in_hbm(far_image))
     mech_temps = pl.pallas_call(
         owner_kernel,
         in_specs=[resident()] * 2,

time: 111 us -> 110 us (level)
  blocking collectives: 39.8 us -> 30 us
  waiting for transfers between devices: 0.59 us -> 8.95 us
  starting transfers between devices: 25.4 us -> 32 us
  Pallas kernels: 41.5 us -> 37.3 us
  local copies, waits for them, and re-layouts: 2.2 us -> 0.65 us
    all_to_all x1 -> x0, blocking collectives: 10.9 us -> none  [total(): lax.all_to_all(copies, 'layer', 0, 0, tiled=True).reshape(LANES, LANES)]
    all_to_all x0 -> x1, starting transfers between devices: none -> 4.79 us  [total(): lax.all_to_all(copies, 'layer', 0, 0, tiled=True).reshape(LANES, LANES)]
    all_to_all x1, waiting for transfers between devices: 0.4 us -> 3.91 us  [on_device(): lax.all_to_all(outgoing.reshape(16, SLOTS, LANES), 'layer', 0, 0, tiled=T...]
    unnamed x4 -> x0, local copies, waits for them, and re-layouts: 2.18 us -> none
    ppermute x2, waiting for transfers between devices: 0.18 us -> 2.28 us  [exchange(): lax.ppermute(faces[3], 'layer', [(i + 1, i) for i in range(count - 1)])]
    ppermute x4, waiting for transfers between devices: 0.01 us -> 2.08 us  [swap(): lax.ppermute(shard, axis, [(i, i ^ bit) for i in range(lax.axis_size(axis...]
    pallas_call x3, Pallas kernels: 25 us -> 23.1 us  [the longest x1 12.8 us: on_device(): pl.pallas_call(final_kernel, in_specs=[resident()] * 3 + [far_memory()],...]
    all_to_all x1, starting transfers between devices: 4.9 us -> 6.59 us  [on_device(): lax.all_to_all(outgoing.reshape(16, SLOTS, LANES), 'layer', 0, 0, tiled=T...]
  transfers between devices with their start and end apart: 9 -> 10, of which waited for: 2 -> 5; matrix products, arithmetic and copies ran while one was open for 0% -> 0% of each run, Pallas kernels for 22% -> 22%
where the time goes in v3:
time: 110 us
  Pallas kernels  37.3 us (34%)
  starting transfers between devices  32 us (29%)
  blocking collectives  30 us (27%)
  waiting for transfers between devices  8.95 us (8%)
    all_to_all x1, blocking collectives, total(): mine = jnp.sum(lax.all_to_all(parts, 'layer', 0, 0, tiled=True), axis=0)  15.3 us
    all_to_all x1, blocking collectives, total(): mine = jnp.sum(lax.all_to_all(copies, 'region', 0, 0, tiled=True), axis=0)  14.7 us
    pallas_call x1, Pallas kernels, on_device(): pl.pallas_call(final_kernel, in_specs=[resident()] * 3 + [far_memory()],...  12.8 us
    ppermute x4, starting transfers between devices, swap(): lax.ppermute(shard, axis, [(i, i ^ bit) for i in range(lax.axis_size(axis...  8.8 us
    ppermute x2, starting transfers between devices, exchange(): lax.ppermute(faces[2], 'layer', [(i, i + 1) for i in range(count - 1)])  6.94 us
    all_to_all x1, starting transfers between devices, on_device(): lax.all_to_all(outgoing.reshape(16, SLOTS, LANES), 'layer', 0, 0, tiled=T...  6.59 us
    pallas_call x1, Pallas kernels, on_device(): pl.pallas_call(relay_kernel, in_specs=[smem(), smem(), far_memory(), pl.B...  5.64 us
    ppermute x2, starting transfers between devices, exchange(): lax.ppermute(faces[3], 'layer', [(i + 1, i) for i in range(count - 1)])  4.9 us
  transfers between devices with their start and end apart: 10, of which 5 were waited for; matrix products, arithmetic and copies ran while one was open for 0% of the time, Pallas kernels for 22%

profile of v3, /device:TPU:8, one launch (start us, length us, event | category | flops | bytes accessed | tf_op | source)
XLA Modules:
  0.0 109.7 jit_solution(4032492901984722097)
XLA Ops:
  0.6 2.9 %field.1 = (bf16[64,64,128]{2,1,0:T(8,128)(2,1)S(1)}, bf16[128,4096]{1,0:T(8,128)(2,1)S(1)}, f32[4096,128]{1,0:T(8,128)S(1)}, f32[256,128]{1,0:T(8,128)S(1)}, f3...) custom-call(s32[4,8]{1,0:T(4,128)} %face_rows.3, f32[64,4096]{1,0:T(8,128)} %right_hbm.1), custom_call_target="tpu_custom_call" | custom-call | flops 1000000 | bytes 5000000 | tf_op jit(solution)/shard_map/field/pallas_call | solution.py:491
  3.5 0.1 collective-permute-start
  3.6 7.3 %collective-permute-start.1 = (f32[256,128]{1,0:T(8,128)S(1)}, f32[256,128]{1,0:T(8,128)S(1)}, u32[]{:S(2)}, u32[]{:S(2)}) collective-permute-start(f32[256,128]{1,0:T(8,128)S(1)} %get-tuple-element.26), channel_id=1, source_target_pairs={{0,128},{16,144},{32,160},{48,176},{64,192},{80,208},{96,224},{112... | collective-permute-start | bytes 393224 | tf_op jit(solution)/shard_map/ppermute | solution.py:453
  10.9 3.5 %collective-permute-start.2 = (f32[256,128]{1,0:T(8,128)S(1)}, f32[256,128]{1,0:T(8,128)S(1)}, u32[]{:S(2)}, u32[]{:S(2)}) collective-permute-start(f32[256,128]{1,0:T(8,128)S(1)} %get-tuple-element.27), channel_id=1, source_target_pairs={{0,1},{1,2},{2,3},{3,4},{4,5},{5,6},{6,7},{7,8},{8,9},{9,10},{10,1... | collective-permute-start | bytes 393224 | tf_op jit(solution)/shard_map/ppermute | solution.py:461
  14.3 2.4 %collective-permute-start.3 = (f32[256,128]{1,0:T(8,128)S(1)}, f32[256,128]{1,0:T(8,128)S(1)}, u32[]{:S(2)}, u32[]{:S(2)}) collective-permute-start(f32[256,128]{1,0:T(8,128)S(1)} %get-tuple-element.28), channel_id=1, source_target_pairs={{1,0},{2,1},{3,2},{4,3},{5,4},{6,5},{7,6},{8,7},{9,8},{10,9},{11,1... | collective-permute-start | bytes 393224 | tf_op jit(solution)/shard_map/ppermute | solution.py:462
  16.7 4.4 %entries.1.mats_ref = bf16[64,128,512]{2,1,0:T(8,128)(2,1)S(1)} custom-call(f32[7,64,4096]{2,1,0:T(8,128)} %bitcast.10), custom_call_target="tpu_custom_call" | custom-call | flops 10000000 | bytes 16000000 | tf_op jit(solution)/shard_map/entries/pallas_call | solution.py:506
  21.2 0.0 collective-permute-done.near
  21.2 0.0 collective-permute-done.1.far
  21.2 0.0 collective-permute-done.2.below
  21.2 0.3 collective-permute-done.3.above
  21.5 4.4 %first_image.1 = (bf16[64,64,128]{2,1,0:T(8,128)(2,1)S(1)}, f32[4096,128]{1,0:T(8,128)}, f32[256,128]{1,0:T(8,128)S(1)}, f32[256,128]{1,0:T(8,128)S(1)}, f32[256,128]{1,0:T(8,128)S(1)}, /*index=5*/f32[256,128]{1,0:T(8,128)S(1)}) custom-call(s32[6,64]{1,0:T(8,128)} %bitcast.11, s32[4,8]{1,0:T(4,128)} %face_rows.3, bf16[64,128,512]{2,1,0:T(8,128)(2,1)S(1)} %entries.1.mats_ref, ...), custom_call_target="tpu_custom_call" | custom-call | flops 1000000000 | bytes 16000000 | tf_op jit(solution)/shard_map/first_image/pallas_call | solution.py:524
  26.0 0.1 collective-permute-start.4
  26.1 1.3 %collective-permute-start.5 = (f32[256,128]{1,0:T(8,128)S(1)}, f32[256,128]{1,0:T(8,128)S(1)}, u32[]{:S(2)}, u32[]{:S(2)}) collective-permute-start(f32[256,128]{1,0:T(8,128)S(1)} %get-tuple-element.31), channel_id=1, source_target_pairs={{0,128},{16,144},{32,160},{48,176},{64,192},{80,208},{96,224},{112... | collective-permute-start | bytes 393224 | tf_op jit(solution)/shard_map/ppermute | solution.py:453
  27.4 3.5 %collective-permute-start.6 = (f32[256,128]{1,0:T(8,128)S(1)}, f32[256,128]{1,0:T(8,128)S(1)}, u32[]{:S(2)}, u32[]{:S(2)}) collective-permute-start(f32[256,128]{1,0:T(8,128)S(1)} %get-tuple-element.32), channel_id=1, source_target_pairs={{0,1},{1,2},{2,3},{3,4},{4,5},{5,6},{6,7},{7,8},{8,9},{9,10},{10,1... | collective-permute-start | bytes 393224 | tf_op jit(solution)/shard_map/ppermute | solution.py:461
  30.9 2.5 %collective-permute-start.7 = (f32[256,128]{1,0:T(8,128)S(1)}, f32[256,128]{1,0:T(8,128)S(1)}, u32[]{:S(2)}, u32[]{:S(2)}) collective-permute-start(f32[256,128]{1,0:T(8,128)S(1)} %get-tuple-element.33), channel_id=1, source_target_pairs={{1,0},{2,1},{3,2},{4,3},{5,4},{6,5},{7,6},{8,7},{9,8},{10,9},{11,1... | collective-permute-start | bytes 393224 | tf_op jit(solution)/shard_map/ppermute | solution.py:462
  33.4 0.8 near_grams.1
  34.2 0.0 collective-permute-done.4.near
  34.2 2.1 %collective-permute-done.5.far = f32[256,128]{1,0:T(8,128)S(1)} collective-permute-done((f32[256,128]{1,0:T(8,128)S(1)}, f32[256,128]{1,0:T(8,128)S(1)}, u32[]{:S(2)}, u32[]{:S(2)}) %collective-permute-start.5) | collective-permute-done | bytes 131104 | tf_op jit(solution)/shard_map/ppermute | solution.py:453
  36.3 0.0 collective-permute-done.6.below
  36.3 2.0 %collective-permute-done.7.above = f32[256,128]{1,0:T(8,128)S(1)} collective-permute-done((f32[256,128]{1,0:T(8,128)S(1)}, f32[256,128]{1,0:T(8,128)S(1)}, u32[]{:S(2)}, u32[]{:S(2)}) %collective-permute-start.7) | collective-permute-done | bytes 131104 | tf_op jit(solution)/shard_map/ppermute | solution.py:462
  38.3 4.7 %second_image.1 = (bf16[64,64,128]{2,1,0:T(8,128)(2,1)}, f32[128,128]{1,0:T(8,128)S(1)}) custom-call(s32[6,64]{1,0:T(8,128)} %bitcast.12, bf16[64,128,512]{2,1,0:T(8,128)(2,1)S(1)} %entries.1.mats_ref, bf16[64,64,128]{2,1,0:T(8,128)(2,1)S(1)} %get-tuple-element.29.image_ref.parts_ref, f32[256,128]{1,0:T(8,128)S(1)} %collective-permute-done.4.near, ...), custom_call_target="tpu_custom_call" | custom-call | flops 1000000000 | bytes 14000000 | tf_op jit(solution)/shard_map/second_image/pallas_call | solution.py:547
  43.0 15.3 %all_to_all.20 = f32[16,8,128]{2,1,0:T(8,128)S(1)} all-to-all(f32[16,8,128]{2,1,0:T(8,128)S(1)} %bitcast.8), channel_id=1, replica_groups=mesh['region'=16,'layer'=16] {'layer'}, dimensions={0} | all-to-all | bytes 131072 | tf_op jit(solution)/shard_map/all_to_all | solution.py:470
  58.3 14.7 %all_to_all.21 = f32[16,8,128]{2,1,0:T(8,128)S(1)} all-to-all(f32[16,8,128]{2,1,0:T(8,128)S(1)} %broadcast_in_dim.4), channel_id=1, replica_groups=mesh['region'=16,'layer'=16] {'region'}, dimensions={0} | all-to-all | bytes 131072 | tf_op jit(solution)/shard_map/all_to_all | solution.py:472
  73.0 0.6 broadcast_in_dim.5
  73.7 4.8 %all-to-all-start.2 = ((f32[16,8,128]{2,1,0:T(8,128)}), f32[16,8,128]{2,1,0:T(8,128)S(1)}, u32[]{:S(2)}, u32[]{:S(2)}) async-start(f32[16,8,128]{2,1,0:T(8,128)} %broadcast_in_dim.5), calls=%async_computation.2 | async-start | bytes 131072 | tf_op jit(solution)/shard_map/all_to_all | solution.py:474
  78.4 5.6 %relay_rows.1 = f32[2048,128]{1,0:T(8,128)} custom-call(s32[512]{0:T(512)} %bitcast.13, s32[512]{0:T(512)} %die_node.1, f32[4096,128]{1,0:T(8,128)} %get-tuple-element.42.both_hbm, f32[128,128]{1,0:T(8,128)S(1)} %get-tuple-element.37.sums_hbm), custom_call_target="tpu_custom_call" | custom-call | flops 1000000 | bytes 10000000 | tf_op jit(solution)/shard_map/relay_rows/pallas_call | solution.py:565
  84.1 0.7 all-to-all-done.2
  84.8 6.6 %all-to-all-start.3 = ((f32[16,128,128]{2,1,0:T(8,128)}), f32[16,128,128]{2,1,0:T(8,128)S(1)}, u32[]{:S(2)}, u32[]{:S(2)}) async-start(f32[16,128,128]{2,1,0:T(8,128)} %bitcast.5), calls=%async_computation.3 | async-start | bytes 2097152 | tf_op jit(solution)/shard_map/all_to_all | solution.py:579
  91.4 12.8 %final.1 = (f32[64,4096]{1,0:T(8,128)}, f32[64,4096]{1,0:T(8,128)}, f32[128,64]{1,0:T(8,128)S(1)}) custom-call(f32[128,128]{1,0:T(8,128)S(1)} %bitcast.9, bf16[128,4096]{1,0:T(8,128)(2,1)S(1)} %get-tuple-element.34.turned_ref, bf16[128,4096]{1,0:T(8,128)(2,1)S(1)} %get-tuple-element.35.image_turned_ref, bf16[64,64,128]{2,1,0:T(8,128)(2,1)} %get-tuple-element.38.far_hbm), custom_call_target="tpu_custom_call" | custom-call | flops 500000000 | bytes 8000000 | tf_op jit(solution)/shard_map/final/pallas_call | solution.py:583
  104.1 3.9 %all-to-all-done.3 = f32[16,128,128]{2,1,0:T(8,128)S(1)} async-done(((f32[16,128,128]{2,1,0:T(8,128)}), f32[16,128,128]{2,1,0:T(8,128)S(1)}, u32[]{:S(2)}, u32[]{:S(2)}) %all-to-all-start.3) | async-done | bytes 1048608 | tf_op jit(solution)/shard_map/all_to_all | solution.py:579
  108.0 1.6 %owner_rows.1 = f32[16,8192]{1,0:T(8,128)} custom-call(f32[128,64]{1,0:T(8,128)S(1)} %get-tuple-element.41.coef_ref, f32[2048,128]{1,0:T(8,128)S(1)} %bitcast.7), custom_call_target="tpu_custom_call" | custom-call | flops 100000000 | bytes 2000000 | tf_op jit(solution)/shard_map/owner_rows/pallas_call | solution.py:599
  (3 shorter events, 0.0 us)
Async XLA Ops:
  3.5 17.7 %collective-permute-start = (f32[256,128]{1,0:T(8,128)S(1)}, f32[256,128]{1,0:T(8,128)S(1)}, u32[]{:S(2)}, u32[]{:S(2)}) collective-permute-start(f32[256,128]{1,0:T(8,128)S(1)} %get-tuple-element.25), channel_id=1, source_target_pairs={{0,16},{16,0},{32,48},{48,32},{64,80},{80,64},{96,112},{112,96},{1... | collective-permute-start | bytes 393224 | tf_op jit(solution)/shard_map/ppermute | solution.py:453
  3.6 17.6 %collective-permute-start.1 = (f32[256,128]{1,0:T(8,128)S(1)}, f32[256,128]{1,0:T(8,128)S(1)}, u32[]{:S(2)}, u32[]{:S(2)}) collective-permute-start(f32[256,128]{1,0:T(8,128)S(1)} %get-tuple-element.26), channel_id=1, source_target_pairs={{0,128},{16,144},{32,160},{48,176},{64,192},{80,208},{96,224},{112... | collective-permute-start | bytes 393224 | tf_op jit(solution)/shard_map/ppermute | solution.py:453
  10.9 10.3 %collective-permute-start.2 = (f32[256,128]{1,0:T(8,128)S(1)}, f32[256,128]{1,0:T(8,128)S(1)}, u32[]{:S(2)}, u32[]{:S(2)}) collective-permute-start(f32[256,128]{1,0:T(8,128)S(1)} %get-tuple-element.27), channel_id=1, source_target_pairs={{0,1},{1,2},{2,3},{3,4},{4,5},{5,6},{6,7},{7,8},{8,9},{9,10},{10,1... | collective-permute-start | bytes 393224 | tf_op jit(solution)/shard_map/ppermute | solution.py:461
  14.3 7.2 %collective-permute-start.3 = (f32[256,128]{1,0:T(8,128)S(1)}, f32[256,128]{1,0:T(8,128)S(1)}, u32[]{:S(2)}, u32[]{:S(2)}) collective-permute-start(f32[256,128]{1,0:T(8,128)S(1)} %get-tuple-element.28), channel_id=1, source_target_pairs={{1,0},{2,1},{3,2},{4,3},{5,4},{6,5},{7,6},{8,7},{9,8},{10,9},{11,1... | collective-permute-start | bytes 393224 | tf_op jit(solution)/shard_map/ppermute | solution.py:462
  26.0 8.3 %collective-permute-start.4 = (f32[256,128]{1,0:T(8,128)S(1)}, f32[256,128]{1,0:T(8,128)S(1)}, u32[]{:S(2)}, u32[]{:S(2)}) collective-permute-start(f32[256,128]{1,0:T(8,128)S(1)} %get-tuple-element.30), channel_id=1, source_target_pairs={{0,16},{16,0},{32,48},{48,32},{64,80},{80,64},{96,112},{112,96},{1... | collective-permute-start | bytes 393224 | tf_op jit(solution)/shard_map/ppermute | solution.py:453
  26.1 10.3 %collective-permute-start.5 = (f32[256,128]{1,0:T(8,128)S(1)}, f32[256,128]{1,0:T(8,128)S(1)}, u32[]{:S(2)}, u32[]{:S(2)}) collective-permute-start(f32[256,128]{1,0:T(8,128)S(1)} %get-tuple-element.31), channel_id=1, source_target_pairs={{0,128},{16,144},{32,160},{48,176},{64,192},{80,208},{96,224},{112... | collective-permute-start | bytes 393224 | tf_op jit(solution)/shard_map/ppermute | solution.py:453
  27.4 8.9 %collective-permute-start.6 = (f32[256,128]{1,0:T(8,128)S(1)}, f32[256,128]{1,0:T(8,128)S(1)}, u32[]{:S(2)}, u32[]{:S(2)}) collective-permute-start(f32[256,128]{1,0:T(8,128)S(1)} %get-tuple-element.32), channel_id=1, source_target_pairs={{0,1},{1,2},{2,3},{3,4},{4,5},{5,6},{6,7},{7,8},{8,9},{9,10},{10,1... | collective-permute-start | bytes 393224 | tf_op jit(solution)/shard_map/ppermute | solution.py:461
  30.9 7.4 %collective-permute-start.7 = (f32[256,128]{1,0:T(8,128)S(1)}, f32[256,128]{1,0:T(8,128)S(1)}, u32[]{:S(2)}, u32[]{:S(2)}) collective-permute-start(f32[256,128]{1,0:T(8,128)S(1)} %get-tuple-element.33), channel_id=1, source_target_pairs={{1,0},{2,1},{3,2},{4,3},{5,4},{6,5},{7,6},{8,7},{9,8},{10,9},{11,1... | collective-permute-start | bytes 393224 | tf_op jit(solution)/shard_map/ppermute | solution.py:462
  73.7 11.1 %all-to-all-start.2 = ((f32[16,8,128]{2,1,0:T(8,128)}), f32[16,8,128]{2,1,0:T(8,128)S(1)}, u32[]{:S(2)}, u32[]{:S(2)}) async-start(f32[16,8,128]{2,1,0:T(8,128)} %broadcast_in_dim.5), calls=%async_computation.2 | async-start | bytes 131072 | tf_op jit(solution)/shard_map/all_to_all | solution.py:474
  84.8 23.3 %all-to-all-start.3 = ((f32[16,128,128]{2,1,0:T(8,128)}), f32[16,128,128]{2,1,0:T(8,128)S(1)}, u32[]{:S(2)}, u32[]{:S(2)}) async-start(f32[16,128,128]{2,1,0:T(8,128)} %bitcast.5), calls=%async_computation.3 | async-start | bytes 2097152 | tf_op jit(solution)/shard_map/all_to_all | solution.py:579

commit v4 on v3

--- a/solution.py
+++ b/solution.py
@@ -19,7 +19,6 @@
 STEP = 8
 GRID = BLK_DEV // STEP
 SHIFT = 1.5
-SAVE_ENDS = (47, 63)
 BF16 = jnp.bfloat16
 F32 = jnp.float32
 
@@ -57,8 +56,8 @@
     return jnp.where(left_lanes(doubled.shape[0]), lead, doubled - lead).astype(BF16)
 
 
-def emit_faces(face_rows, nodes_ref, face_refs):
-    for side, face_ref in enumerate(face_refs):
+def emit_faces(face_rows, odd, nodes_ref, face_refs):
+    for side, face_ref in zip((0, 1, 2 + odd[0], 3 - odd[0]), face_refs):
         for face in range(FACES):
             start = pl.multiple_of(face_rows[side, face] * BLOCK, BLOCK)
             upper = nodes_ref[pl.ds(start, 32), :]
@@ -71,7 +70,7 @@
 
 
 def field_kernel(
-    face_rows, right_hbm, parts_ref, turned_ref, nodes_ref, out0, out1, out2, out3, right_ref, sems
+    face_rows, odd, right_hbm, parts_ref, turned_ref, nodes_ref, out0, out1, out2, out3, right_ref, sems
 ):
     copies = []
     for step in range(GRID):
@@ -94,7 +93,7 @@
             halves = two_parts(doubled)
             parts_ref[step * STEP + 2 * chunk] = halves[:BLOCK]
             parts_ref[step * STEP + 2 * chunk + 1] = halves[BLOCK:]
-    emit_faces(face_rows, nodes_ref, (out0, out1, out2, out3))
+    emit_faces(face_rows, odd, nodes_ref, (out0, out1, out2, out3))
 
 
 def entries_kernel(raw_hbm, mats_ref, raw_ref, rows_ref, sems):
@@ -136,10 +135,10 @@
                 mats_ref[block, BLOCK:, duo * LANES : (duo + 1) * LANES] = rest
 
 
-def fill_extended(parts_ref, received, extended_ref):
+def fill_extended(odd, parts_ref, received, extended_ref):
     extended_ref[:BLK_DEV] = parts_ref[...]
     half = left_lanes(32)
-    for side, got_ref in enumerate(received):
+    for side, got_ref in zip((0, 1, 3 - odd[0], 2 + odd[0]), received):
         for face in range(FACES):
             packed = got_ref[face * 32 : (face + 1) * 32, :]
             turned = pltpu.roll(packed, RHS, 1)
@@ -163,25 +162,16 @@
 
 
 def first_kernel(
-    neighbours, face_rows, mats_ref, parts_ref, own_ref, near, far, below, above,
-    image_ref, both_hbm, out0, out1, out2, out3, extended_ref, nodes_ref, both_ref, sem,
+    neighbours, face_rows, odd, mats_ref, parts_ref, own_ref, near, far, inner, outer,
+    image_ref, both_ref, out0, out1, out2, out3, extended_ref, nodes_ref,
 ):
-    def save(at):
-        first = SAVE_ENDS[at - 1] + 1 if at else 0
-        part = pl.ds(first * BLOCK, (SAVE_ENDS[at] + 1 - first) * BLOCK)
-        return pltpu.make_async_copy(both_ref.at[part], both_hbm.at[part], sem.at[at])
-
-    fill_extended(parts_ref, (near, far, below, above), extended_ref)
+    fill_extended(odd, parts_ref, (near, far, inner, outer), extended_ref)
     for block in range(BLK_DEV):
         doubled = block_row(block, neighbours, mats_ref, extended_ref, nodes_ref)
         image_ref[block] = two_parts(doubled)
         rows = slice(block * BLOCK, (block + 1) * BLOCK)
         both_ref[rows, :] = jnp.where(left_lanes(BLOCK), own_ref[rows, :], doubled)
-        if block in SAVE_ENDS:
-            save(SAVE_ENDS.index(block)).start()
-    emit_faces(face_rows, nodes_ref, (out0, out1, out2, out3))
-    for at in range(len(SAVE_ENDS)):
-        save(at).wait()
+    emit_faces(face_rows, odd, nodes_ref, (out0, out1, out2, out3))
 
 
 def quarter_sum(grid):
@@ -215,10 +205,10 @@
 
 
 def second_kernel(
-    neighbours, mats_ref, parts_ref, near, far, below, above, turned_ref, image_turned_ref,
-    gram_ref, image_hbm, sums_ref, extended_ref, nodes_ref, image_ref, acc_ref, sem,
+    neighbours, odd, mats_ref, parts_ref, near, far, inner, outer, turned_ref, image_turned_ref,
+    gram_ref, outgoing_ref, image_hbm, sums_ref, extended_ref, nodes_ref, image_ref, acc_ref, sem,
 ):
-    fill_extended(parts_ref, (near, far, below, above), extended_ref)
+    fill_extended(odd, parts_ref, (near, far, inner, outer), extended_ref)
     acc_ref[...] = jnp.zeros_like(acc_ref)
     for block in range(BLK_DEV):
         doubled = block_row(block, neighbours, mats_ref, extended_ref, nodes_ref)
@@ -276,13 +266,10 @@
     return norm, curve, image_norm, far_field, far_image
 
 
-def relay_kernel(owners, die_node, both_hbm, sums_hbm, out_ref, counts, both_ref, sem):
-    fetch = pltpu.make_async_copy(both_hbm, both_ref, sem)
-    fetch.start()
+def relay_kernel(owners, die_node, both_ref, out_ref, counts):
     out_ref[...] = jnp.zeros_like(out_ref)
     for owner in range(16):
         counts[owner] = owner * SLOTS
-    fetch.wait()
 
     def move(row, carry):
         owner = owners[row]
@@ -458,9 +445,10 @@
     top = lax.axis_size("region") // 2
     near = swap(faces[0], "region", 1)
     far = swap(faces[1], "region", top)
-    below = lax.ppermute(faces[2], "layer", [(i, i + 1) for i in range(count - 1)])
-    above = lax.ppermute(faces[3], "layer", [(i + 1, i) for i in range(count - 1)])
-    return near, far, below, above
+    inner = swap(faces[2], "layer", 1)
+    pairs = [(i, i + 1) for i in range(1, count - 1, 2)]
+    outer = lax.ppermute(faces[3], "layer", pairs + [(b, a) for a, b in pairs])
+    return near, far, inner, outer
 
 
 def total(local):
@@ -486,11 +474,12 @@
     die_node = in_hbm(die_node)
     neighbours = in_hbm(neighbours.T)
     face_rows = in_hbm(face_rows)
+    odd = (lax.axis_index("layer") % 2).astype(jnp.int32).reshape(1)
     entries = in_hbm(jnp.transpose(block_entries, (1, 0, 2)))
     right_side = in_hbm(right_side)
     outcome = pl.pallas_call(
         field_kernel,
-        in_specs=[smem(), pl.BlockSpec(memory_space=pl.ANY)],
+        in_specs=[smem(), smem(), pl.BlockSpec(memory_space=pl.ANY)],
         out_specs=[resident()] * 7,
         out_shape=[PARTS, TURNED, NODE_ROWS] + [FACE] * 4,
         scratch_shapes=[
@@ -500,7 +489,7 @@
         compiler_params=params(8),
         cost_estimate=cost(1_000_000, 5_000_000),
         name="field",
-    )(face_rows, right_side)
+    )(face_rows, odd, right_side)
     field, turned, own_rows, faces = outcome[0], outcome[1], outcome[2], outcome[3:]
     received = exchange(faces)
     mats = pl.pallas_call(
@@ -523,15 +512,14 @@
     ]
     outcome = pl.pallas_call(
         first_kernel,
-        in_specs=[smem(), smem()] + [resident()] * 7,
-        out_specs=[resident(), far_memory()] + [resident()] * 4,
-        out_shape=[PARTS, pltpu.HBM(NODE_ROWS.shape, F32)] + [FACE] * 4,
-        scratch_shapes=apply_scratch
-        + [pltpu.VMEM((NODES_DEV, LANES), F32), pltpu.SemaphoreType.DMA((len(SAVE_ENDS),))],
+        in_specs=[smem(), smem(), smem()] + [resident()] * 7,
+        out_specs=[resident()] * 6,
+        out_shape=[PARTS, NODE_ROWS] + [FACE] * 4,
+        scratch_shapes=apply_scratch,
         compiler_params=params(8),
         cost_estimate=cost(1_000_000_000, 16_000_000),
         name="first_image",
-    )(neighbours, face_rows, mats, field, own_rows, *received)
+    )(neighbours, face_rows, odd, mats, field, own_rows, *received)
     image, both_rows, faces = outcome[0], outcome[1], outcome[2:]
     received = exchange(faces)
     grams, image_turned = pl.pallas_call(
@@ -544,9 +532,22 @@
         cost_estimate=cost(500_000_000, 2_000_000),
         name="near_grams",
     )(turned, field, image)
+    outgoing = pl.pallas_call(
+        relay_kernel,
+        in_specs=[smem(), smem(), resident()],
+        out_specs=resident(),
+        out_shape=jax.ShapeDtypeStruct((16 * SLOTS, LANES), F32),
+        scratch_shapes=[pltpu.SMEM((16,), jnp.int32)],
+        compiler_params=params(8),
+        cost_estimate=cost(1_000_000, 10_000_000),
+        name="relay_rows",
+    )(owners, die_node, both_rows)
+    relayed = lax.all_to_all(
+        outgoing.reshape(16, SLOTS, LANES), "layer", 0, 0, tiled=True
+    ).reshape(16 * SLOTS, LANES)
     far_image, local_sums = pl.pallas_call(
         second_kernel,
-        in_specs=[smem()] + [resident()] * 9,
+        in_specs=[smem(), smem()] + [resident()] * 9 + [pl.BlockSpec(memory_space=pl.ANY)],
         out_specs=[far_memory(), resident()],
         out_shape=[
             pltpu.HBM(PARTS.shape, BF16),
@@ -561,24 +562,7 @@
         compiler_params=params(8),
         cost_estimate=cost(1_000_000_000, 14_000_000),
         name="second_image",
-    )(neighbours, mats, image, *received, turned, image_turned, grams)
-    outgoing = pl.pallas_call(
-        relay_kernel,
-        in_specs=[smem(), smem(), far_memory(), pl.BlockSpec(memory_space=pl.ANY)],
-        out_specs=resident(),
-        out_shape=jax.ShapeDtypeStruct((16 * SLOTS, LANES), F32),
-        scratch_shapes=[
-            pltpu.SMEM((16,), jnp.int32),
-            pltpu.VMEM((NODES_DEV, LANES), F32),
-            pltpu.SemaphoreType.DMA,
-        ],
-        compiler_params=params(8),
-        cost_estimate=cost(1_000_000, 10_000_000),
-        name="relay_rows",
-    )(owners, die_node, in_hbm(both_rows), local_sums)
-    relayed = lax.all_to_all(
-        outgoing.reshape(16, SLOTS, LANES), "layer", 0, 0, tiled=True
-    ).reshape(16 * SLOTS, LANES)
+    )(neighbours, odd, mats, image, *received, turned, image_turned, grams, outgoing)
     sums = total(local_sums)
     solution_field, residual, coef = pl.pallas_call(
         final_kernel,

time: 110 us -> 101 us (0.918)
  starting transfers between devices: 32 us -> 24.8 us
  blocking collectives: 30 us -> 36.9 us
  waiting for transfers between devices: 8.95 us -> 2.69 us
  Pallas kernels: 37.3 us -> 35.5 us
    all_to_all x0 -> x1, blocking collectives: none -> 10.9 us  [total(): lax.all_to_all(copies, 'layer', 0, 0, tiled=True).reshape(LANES, LANES)]
    all_to_all x1 -> x0, starting transfers between devices: 4.79 us -> none  [total(): lax.all_to_all(copies, 'layer', 0, 0, tiled=True).reshape(LANES, LANES)]
    ppermute x4 -> x2, starting transfers between devices: 11.8 us -> 9.24 us  [exchange(): outer = lax.ppermute(faces[3], 'layer', pairs + [(b, a) for a, b in pairs])]
    ppermute x4 -> x2, waiting for transfers between devices: 2.29 us -> 0.01 us  [exchange(): outer = lax.ppermute(faces[3], 'layer', pairs + [(b, a) for a, b in pairs])]
    all_to_all x1, blocking collectives: 14.7 us -> 12.6 us  [total(): mine = jnp.sum(lax.all_to_all(copies, 'region', 0, 0, tiled=True), axis=0)]
    ppermute x4 -> x6, waiting for transfers between devices: 2.08 us -> 0.02 us  [swap(): lax.ppermute(shard, axis, [(i, i ^ bit) for i in range(lax.axis_size(axis...]
    all_to_all x1, blocking collectives: 15.3 us -> 13.4 us  [total(): mine = jnp.sum(lax.all_to_all(parts, 'layer', 0, 0, tiled=True), axis=0)]
    ppermute x4 -> x6, starting transfers between devices: 8.8 us -> 10.6 us  [swap(): lax.ppermute(shard, axis, [(i, i ^ bit) for i in range(lax.axis_size(axis...]
  transfers between devices with their start and end apart: 10 -> 9, of which waited for: 5 -> 1; matrix products, arithmetic and copies ran while one was open for 0% -> 0% of each run, Pallas kernels for 22% -> 22%
where the time goes in v4:
time: 101 us
  blocking collectives  36.9 us (37%)
  Pallas kernels  35.5 us (35%)
  starting transfers between devices  24.8 us (25%)
  waiting for transfers between devices  2.69 us (3%)
    all_to_all x1, blocking collectives, total(): mine = jnp.sum(lax.all_to_all(parts, 'layer', 0, 0, tiled=True), axis=0)  13.4 us
    pallas_call x1, Pallas kernels, on_device(): pl.pallas_call(final_kernel, in_specs=[resident()] * 3 + [far_memory()],...  12.8 us
    all_to_all x1, blocking collectives, total(): mine = jnp.sum(lax.all_to_all(copies, 'region', 0, 0, tiled=True), axis=0)  12.6 us
    all_to_all x1, blocking collectives, total(): lax.all_to_all(copies, 'layer', 0, 0, tiled=True).reshape(LANES, LANES)  10.9 us
    ppermute x6, starting transfers between devices, swap(): lax.ppermute(shard, axis, [(i, i ^ bit) for i in range(lax.axis_size(axis...  10.6 us
    ppermute x2, starting transfers between devices, exchange(): outer = lax.ppermute(faces[3], 'layer', pairs + [(b, a) for a, b in pairs])  9.24 us
    pallas_call x1, Pallas kernels, on_device(): pl.pallas_call(second_kernel, in_specs=[smem(), smem()] + [resident()] *...  4.93 us
    all_to_all x1, starting transfers between devices, on_device(): lax.all_to_all(outgoing.reshape(16, SLOTS, LANES), 'layer', 0, 0, tiled=T...  4.9 us
  transfers between devices with their start and end apart: 9, of which 1 were waited for; matrix products, arithmetic and copies ran while one was open for 0% of the time, Pallas kernels for 22%

profile of v4, /device:TPU:8, one launch (start us, length us, event | category | flops | bytes accessed | tf_op | source)
XLA Modules:
  0.0 100.7 jit_solution(3781816450994839371)
XLA Ops:
  0.6 2.9 %field.1 = (bf16[64,64,128]{2,1,0:T(8,128)(2,1)S(1)}, bf16[128,4096]{1,0:T(8,128)(2,1)S(1)}, f32[4096,128]{1,0:T(8,128)S(1)}, f32[256,128]{1,0:T(8,128)S(1)}, f3...) custom-call(s32[4,8]{1,0:T(4,128)} %face_rows.3, s32[1]{0:T(128)} %bitcast.1.odd, ...), custom_call_target="tpu_custom_call" | custom-call | flops 1000000 | bytes 5000000 | tf_op jit(solution)/shard_map/field/pallas_call | solution.py:480
  3.5 0.1 collective-permute-start
  3.6 7.3 %collective-permute-start.1 = (f32[256,128]{1,0:T(8,128)S(1)}, f32[256,128]{1,0:T(8,128)S(1)}, u32[]{:S(2)}, u32[]{:S(2)}) collective-permute-start(f32[256,128]{1,0:T(8,128)S(1)} %get-tuple-element.26), channel_id=1, source_target_pairs={{0,128},{16,144},{32,160},{48,176},{64,192},{80,208},{96,224},{112... | collective-permute-start | bytes 393224 | tf_op jit(solution)/shard_map/ppermute | solution.py:440
  10.9 0.4 collective-permute-start.2
  11.3 4.3 %collective-permute-start.3 = (f32[256,128]{1,0:T(8,128)S(1)}, f32[256,128]{1,0:T(8,128)S(1)}, u32[]{:S(2)}, u32[]{:S(2)}) collective-permute-start(f32[256,128]{1,0:T(8,128)S(1)} %get-tuple-element.28), channel_id=1, source_target_pairs={{1,2},{3,4},{5,6},{7,8},{9,10},{11,12},{13,14},{2,1},{4,3},{6,5},{... | collective-permute-start | bytes 393224 | tf_op jit(solution)/shard_map/ppermute | solution.py:450
  15.6 4.4 %entries.1.mats_ref = bf16[64,128,512]{2,1,0:T(8,128)(2,1)S(1)} custom-call(f32[7,64,4096]{2,1,0:T(8,128)} %bitcast.11), custom_call_target="tpu_custom_call" | custom-call | flops 10000000 | bytes 16000000 | tf_op jit(solution)/shard_map/entries/pallas_call | solution.py:495
  20.1 0.0 collective-permute-done.near
  20.1 0.0 collective-permute-done.1.far
  20.1 0.0 collective-permute-done.2.inner
  20.1 0.0 collective-permute-done.3.outer
  20.1 3.9 %first_image.1 = (bf16[64,64,128]{2,1,0:T(8,128)(2,1)S(1)}, f32[4096,128]{1,0:T(8,128)S(1)}, f32[256,128]{1,0:T(8,128)S(1)}, f32[256,128]{1,0:T(8,128)S(1)}, f32...) custom-call(s32[6,64]{1,0:T(8,128)} %bitcast.12, s32[4,8]{1,0:T(4,128)} %face_rows.3, s32[1]{0:T(128)} %bitcast.1.odd, ...), custom_call_target="tpu_custom_call" | custom-call | flops 1000000000 | bytes 16000000 | tf_op jit(solution)/shard_map/first_image/pallas_call | solution.py:513
  24.1 0.1 collective-permute-start.4
  24.2 2.7 %collective-permute-start.5 = (f32[256,128]{1,0:T(8,128)S(1)}, f32[256,128]{1,0:T(8,128)S(1)}, u32[]{:S(2)}, u32[]{:S(2)}) collective-permute-start(f32[256,128]{1,0:T(8,128)S(1)} %get-tuple-element.31), channel_id=1, source_target_pairs={{0,128},{16,144},{32,160},{48,176},{64,192},{80,208},{96,224},{112... | collective-permute-start | bytes 393224 | tf_op jit(solution)/shard_map/ppermute | solution.py:440
  26.9 0.0 collective-permute-start.6
  26.9 4.9 %collective-permute-start.7 = (f32[256,128]{1,0:T(8,128)S(1)}, f32[256,128]{1,0:T(8,128)S(1)}, u32[]{:S(2)}, u32[]{:S(2)}) collective-permute-start(f32[256,128]{1,0:T(8,128)S(1)} %get-tuple-element.33), channel_id=1, source_target_pairs={{1,2},{3,4},{5,6},{7,8},{9,10},{11,12},{13,14},{2,1},{4,3},{6,5},{... | collective-permute-start | bytes 393224 | tf_op jit(solution)/shard_map/ppermute | solution.py:450
  31.8 4.1 %relay_rows.1.outgoing_ref = f32[2048,128]{1,0:T(8,128)} custom-call(s32[512]{0:T(512)} %bitcast.14, s32[512]{0:T(512)} %die_node.1, f32[4096,128]{1,0:T(8,128)S(1)} %get-tuple-element.37.both_ref), custom_call_target="tpu_custom_call" | custom-call | flops 1000000 | bytes 10000000 | tf_op jit(solution)/shard_map/relay_rows/pallas_call | solution.py:535
  35.9 0.8 near_grams.1
  36.8 0.0 collective-permute-done.4.near
  36.8 0.0 collective-permute-done.5.far
  36.8 0.0 collective-permute-done.6.inner
  36.8 0.0 collective-permute-done.7.outer
  36.8 4.9 %second_image.1 = (bf16[64,64,128]{2,1,0:T(8,128)(2,1)}, f32[128,128]{1,0:T(8,128)S(1)}) custom-call(s32[6,64]{1,0:T(8,128)} %bitcast.13, s32[1]{0:T(128)} %bitcast.1.odd, bf16[64,128,512]{2,1,0:T(8,128)(2,1)S(1)} %entries.1.mats_ref, bf16[64,64,128]{2,1,0:T(8,128)(2,1)S(1)} %get-tuple-element.29.image_ref.parts_ref, ...), custom_call_target="tpu_custom_call" | custom-call | flops 1000000000 | bytes 14000000 | tf_op jit(solution)/shard_map/second_image/pallas_call | solution.py:548
  41.7 13.4 %all_to_all.20 = f32[16,8,128]{2,1,0:T(8,128)S(1)} all-to-all(f32[16,8,128]{2,1,0:T(8,128)S(1)} %bitcast.10), channel_id=1, replica_groups=mesh['region'=16,'layer'=16] {'layer'}, dimensions={0} | all-to-all | bytes 131072 | tf_op jit(solution)/shard_map/all_to_all | solution.py:458
  55.2 12.6 %all_to_all.21 = f32[16,8,128]{2,1,0:T(8,128)S(1)} all-to-all(f32[16,8,128]{2,1,0:T(8,128)S(1)} %broadcast_in_dim.4), channel_id=1, replica_groups=mesh['region'=16,'layer'=16] {'region'}, dimensions={0} | all-to-all | bytes 131072 | tf_op jit(solution)/shard_map/all_to_all | solution.py:460
  67.8 10.9 %all_to_all.22 = f32[16,8,128]{2,1,0:T(8,128)S(1)} all-to-all(f32[16,8,128]{2,1,0:T(8,128)S(1)} %broadcast_in_dim.5), channel_id=1, replica_groups=mesh['region'=16,'layer'=16] {'layer'}, dimensions={0} | all-to-all | bytes 131072 | tf_op jit(solution)/shard_map/all_to_all | solution.py:462
  78.7 4.9 %all-to-all-start.3 = ((f32[16,128,128]{2,1,0:T(8,128)}), f32[16,128,128]{2,1,0:T(8,128)S(1)}, u32[]{:S(2)}, u32[]{:S(2)}) async-start(f32[16,128,128]{2,1,0:T(8,128)} %bitcast.6), calls=%async_computation.3 | async-start | bytes 2097152 | tf_op jit(solution)/shard_map/all_to_all | solution.py:545
  83.6 12.8 %final.1 = (f32[64,4096]{1,0:T(8,128)}, f32[64,4096]{1,0:T(8,128)}, f32[128,64]{1,0:T(8,128)S(1)}) custom-call(f32[128,128]{1,0:T(8,128)S(1)} %bitcast.9, bf16[128,4096]{1,0:T(8,128)(2,1)S(1)} %get-tuple-element.34.turned_ref, bf16[128,4096]{1,0:T(8,128)(2,1)S(1)} %get-tuple-element.35.image_turned_ref, bf16[64,64,128]{2,1,0:T(8,128)(2,1)} %get-tuple-element.39.far_hbm), custom_call_target="tpu_custom_call" | custom-call | flops 500000000 | bytes 8000000 | tf_op jit(solution)/shard_map/final/pallas_call | solution.py:567
  96.4 2.7 %all-to-all-done.3 = f32[16,128,128]{2,1,0:T(8,128)S(1)} async-done(((f32[16,128,128]{2,1,0:T(8,128)}), f32[16,128,128]{2,1,0:T(8,128)S(1)}, u32[]{:S(2)}, u32[]{:S(2)}) %all-to-all-start.3) | async-done | bytes 1048608 | tf_op jit(solution)/shard_map/all_to_all | solution.py:545
  99.1 1.6 %owner_rows.1 = f32[16,8192]{1,0:T(8,128)} custom-call(f32[128,64]{1,0:T(8,128)S(1)} %get-tuple-element.42.coef_ref, f32[2048,128]{1,0:T(8,128)S(1)} %bitcast.8), custom_call_target="tpu_custom_call" | custom-call | flops 100000000 | bytes 2000000 | tf_op jit(solution)/shard_map/owner_rows/pallas_call | solution.py:583
  (4 shorter events, 0.1 us)
Async XLA Ops:
  3.5 16.6 %collective-permute-start = (f32[256,128]{1,0:T(8,128)S(1)}, f32[256,128]{1,0:T(8,128)S(1)}, u32[]{:S(2)}, u32[]{:S(2)}) collective-permute-start(f32[256,128]{1,0:T(8,128)S(1)} %get-tuple-element.25), channel_id=1, source_target_pairs={{0,16},{16,0},{32,48},{48,32},{64,80},{80,64},{96,112},{112,96},{1... | collective-permute-start | bytes 393224 | tf_op jit(solution)/shard_map/ppermute | solution.py:440
  3.6 16.5 %collective-permute-start.1 = (f32[256,128]{1,0:T(8,128)S(1)}, f32[256,128]{1,0:T(8,128)S(1)}, u32[]{:S(2)}, u32[]{:S(2)}) collective-permute-start(f32[256,128]{1,0:T(8,128)S(1)} %get-tuple-element.26), channel_id=1, source_target_pairs={{0,128},{16,144},{32,160},{48,176},{64,192},{80,208},{96,224},{112... | collective-permute-start | bytes 393224 | tf_op jit(solution)/shard_map/ppermute | solution.py:440
  10.9 9.2 %collective-permute-start.2 = (f32[256,128]{1,0:T(8,128)S(1)}, f32[256,128]{1,0:T(8,128)S(1)}, u32[]{:S(2)}, u32[]{:S(2)}) collective-permute-start(f32[256,128]{1,0:T(8,128)S(1)} %get-tuple-element.27), channel_id=1, source_target_pairs={{0,1},{1,0},{2,3},{3,2},{4,5},{5,4},{6,7},{7,6},{8,9},{9,8},{10,11... | collective-permute-start | bytes 393224 | tf_op jit(solution)/shard_map/ppermute | solution.py:440
  11.3 8.8 %collective-permute-start.3 = (f32[256,128]{1,0:T(8,128)S(1)}, f32[256,128]{1,0:T(8,128)S(1)}, u32[]{:S(2)}, u32[]{:S(2)}) collective-permute-start(f32[256,128]{1,0:T(8,128)S(1)} %get-tuple-element.28), channel_id=1, source_target_pairs={{1,2},{3,4},{5,6},{7,8},{9,10},{11,12},{13,14},{2,1},{4,3},{6,5},{... | collective-permute-start | bytes 393224 | tf_op jit(solution)/shard_map/ppermute | solution.py:450
  24.1 12.7 %collective-permute-start.4 = (f32[256,128]{1,0:T(8,128)S(1)}, f32[256,128]{1,0:T(8,128)S(1)}, u32[]{:S(2)}, u32[]{:S(2)}) collective-permute-start(f32[256,128]{1,0:T(8,128)S(1)} %get-tuple-element.30), channel_id=1, source_target_pairs={{0,16},{16,0},{32,48},{48,32},{64,80},{80,64},{96,112},{112,96},{1... | collective-permute-start | bytes 393224 | tf_op jit(solution)/shard_map/ppermute | solution.py:440
  24.2 12.6 %collective-permute-start.5 = (f32[256,128]{1,0:T(8,128)S(1)}, f32[256,128]{1,0:T(8,128)S(1)}, u32[]{:S(2)}, u32[]{:S(2)}) collective-permute-start(f32[256,128]{1,0:T(8,128)S(1)} %get-tuple-element.31), channel_id=1, source_target_pairs={{0,128},{16,144},{32,160},{48,176},{64,192},{80,208},{96,224},{112... | collective-permute-start | bytes 393224 | tf_op jit(solution)/shard_map/ppermute | solution.py:440
  26.9 9.9 %collective-permute-start.6 = (f32[256,128]{1,0:T(8,128)S(1)}, f32[256,128]{1,0:T(8,128)S(1)}, u32[]{:S(2)}, u32[]{:S(2)}) collective-permute-start(f32[256,128]{1,0:T(8,128)S(1)} %get-tuple-element.32), channel_id=1, source_target_pairs={{0,1},{1,0},{2,3},{3,2},{4,5},{5,4},{6,7},{7,6},{8,9},{9,8},{10,11... | collective-permute-start | bytes 393224 | tf_op jit(solution)/shard_map/ppermute | solution.py:440
  26.9 9.9 %collective-permute-start.7 = (f32[256,128]{1,0:T(8,128)S(1)}, f32[256,128]{1,0:T(8,128)S(1)}, u32[]{:S(2)}, u32[]{:S(2)}) collective-permute-start(f32[256,128]{1,0:T(8,128)S(1)} %get-tuple-element.33), channel_id=1, source_target_pairs={{1,2},{3,4},{5,6},{7,8},{9,10},{11,12},{13,14},{2,1},{4,3},{6,5},{... | collective-permute-start | bytes 393224 | tf_op jit(solution)/shard_map/ppermute | solution.py:450
  78.7 20.3 %all-to-all-start.3 = ((f32[16,128,128]{2,1,0:T(8,128)}), f32[16,128,128]{2,1,0:T(8,128)S(1)}, u32[]{:S(2)}, u32[]{:S(2)}) async-start(f32[16,128,128]{2,1,0:T(8,128)} %bitcast.6), calls=%async_computation.3 | async-start | bytes 2097152 | tf_op jit(solution)/shard_map/all_to_all | solution.py:545

commit v5 on v4

--- a/solution.py
+++ b/solution.py
@@ -43,8 +43,20 @@
     return pl.BlockSpec(memory_space=pltpu.VMEM)
 
 
-def smem():
-    return pl.BlockSpec(memory_space=pltpu.SMEM)
+def fetch_tables(sources, targets, sems):
+    copies = [
+        pltpu.make_async_copy(source, target, sems.at[at])
+        for at, (source, target) in enumerate(zip(sources, targets))
+    ]
+    for copy in copies:
+        copy.start()
+    return copies
+
+
+def tables(*shapes):
+    return [pltpu.SMEM(shape, jnp.int32) for shape in shapes] + [
+        pltpu.SemaphoreType.DMA((len(shapes),))
+    ]
 
 
 def left_lanes(rows):
@@ -70,33 +82,33 @@
 
 
 def field_kernel(
-    face_rows, odd, right_hbm, parts_ref, turned_ref, nodes_ref, out0, out1, out2, out3, right_ref, sems
+    face_hbm, odd_hbm, right_hbm, right_ref, nodes_ref, out0, out1, out2, out3, sems,
+    face_rows, odd, table_sems,
 ):
+    waits = fetch_tables((face_hbm, odd_hbm), (face_rows, odd), table_sems)
     copies = []
     for step in range(GRID):
         columns = pl.ds(step * STEP * BLOCK, STEP * BLOCK)
         copies.append(
-            pltpu.make_async_copy(right_hbm.at[:, columns], right_ref.at[step], sems.at[step])
+            pltpu.make_async_copy(
+                right_hbm.at[:, columns], right_ref.at[:, columns], sems.at[step]
+            )
         )
         copies[step].start()
     for step in range(GRID):
         copies[step].wait()
-        lead, rest = halves_of(right_ref[step])
-        columns = slice(step * STEP * BLOCK, (step + 1) * STEP * BLOCK)
-        turned_ref[:RHS, columns] = lead
-        turned_ref[RHS:, columns] = rest
         for chunk in range(STEP * BLOCK // LANES):
-            piece = right_ref[step, :, chunk * LANES : (chunk + 1) * LANES]
-            doubled = jnp.concatenate([piece, piece], axis=0).T
             start = step * STEP * BLOCK + chunk * LANES
-            nodes_ref[start : start + LANES, :] = doubled
-            halves = two_parts(doubled)
-            parts_ref[step * STEP + 2 * chunk] = halves[:BLOCK]
-            parts_ref[step * STEP + 2 * chunk + 1] = halves[BLOCK:]
+            piece = right_ref[:, start : start + LANES]
+            nodes_ref[start : start + LANES, :] = jnp.concatenate([piece, piece], axis=0).T
+    for wait in waits:
+        wait.wait()
     emit_faces(face_rows, odd, nodes_ref, (out0, out1, out2, out3))
 
 
-def entries_kernel(raw_hbm, mats_ref, raw_ref, rows_ref, sems):
+def entries_kernel(
+    raw_hbm, right_ref, nodes_ref, mats_ref, parts_ref, turned_ref, raw_ref, rows_ref, sems
+):
     half = left_lanes(32)
     lane = lax.broadcasted_iota(jnp.int32, (32, LANES), 1)
     twice = 2 * lax.broadcasted_iota(jnp.int32, (32, LANES), 0)
@@ -109,7 +121,13 @@
 
     for step in range(GRID):
         fetch(step).start()
-
+    for step in range(GRID):
+        columns = columns_of(step)
+        lead, rest = halves_of(right_ref[:, columns])
+        turned_ref[:RHS, columns] = lead
+        turned_ref[RHS:, columns] = rest
+    for block in range(BLK_DEV):
+        parts_ref[block] = two_parts(nodes_ref[block * BLOCK : (block + 1) * BLOCK, :])
     for step in range(GRID):
         fetch(step).wait()
         for k in range(COUPLED):
@@ -135,8 +153,11 @@
                 mats_ref[block, BLOCK:, duo * LANES : (duo + 1) * LANES] = rest
 
 
-def fill_extended(odd, parts_ref, received, extended_ref):
+def own_extended(parts_ref, extended_ref):
     extended_ref[:BLK_DEV] = parts_ref[...]
+
+
+def fill_extended(odd, received, extended_ref):
     half = left_lanes(32)
     for side, got_ref in zip((0, 1, 3 - odd[0], 2 + odd[0]), received):
         for face in range(FACES):
@@ -162,10 +183,17 @@
 
 
 def first_kernel(
-    neighbours, face_rows, odd, mats_ref, parts_ref, own_ref, near, far, inner, outer,
+    neighbours_hbm, face_hbm, odd_hbm, mats_ref, parts_ref, own_ref, near, far, inner, outer,
     image_ref, both_ref, out0, out1, out2, out3, extended_ref, nodes_ref,
+    neighbours, face_rows, odd, table_sems,
 ):
-    fill_extended(odd, parts_ref, (near, far, inner, outer), extended_ref)
+    waits = fetch_tables(
+        (neighbours_hbm, face_hbm, odd_hbm), (neighbours, face_rows, odd), table_sems
+    )
+    own_extended(parts_ref, extended_ref)
+    for wait in waits:
+        wait.wait()
+    fill_extended(odd, (near, far, inner, outer), extended_ref)
     for block in range(BLK_DEV):
         doubled = block_row(block, neighbours, mats_ref, extended_ref, nodes_ref)
         image_ref[block] = two_parts(doubled)
@@ -205,10 +233,15 @@
 
 
 def second_kernel(
-    neighbours, odd, mats_ref, parts_ref, near, far, inner, outer, turned_ref, image_turned_ref,
+    neighbours_hbm, odd_hbm, mats_ref, parts_ref, near, far, inner, outer, turned_ref, image_turned_ref,
     gram_ref, outgoing_ref, image_hbm, sums_ref, extended_ref, nodes_ref, image_ref, acc_ref, sem,
+    neighbours, odd, table_sems,
 ):
-    fill_extended(odd, parts_ref, (near, far, inner, outer), extended_ref)
+    waits = fetch_tables((neighbours_hbm, odd_hbm), (neighbours, odd), table_sems)
+    own_extended(parts_ref, extended_ref)
+    for wait in waits:
+        wait.wait()
+    fill_extended(odd, (near, far, inner, outer), extended_ref)
     acc_ref[...] = jnp.zeros_like(acc_ref)
     for block in range(BLK_DEV):
         doubled = block_row(block, neighbours, mats_ref, extended_ref, nodes_ref)
@@ -266,10 +299,15 @@
     return norm, curve, image_norm, far_field, far_image
 
 
-def relay_kernel(owners, die_node, both_ref, out_ref, counts):
+def relay_kernel(
+    owners_hbm, node_hbm, both_ref, out_ref, counts, owners, die_node, table_sems
+):
+    waits = fetch_tables((owners_hbm, node_hbm), (owners, die_node), table_sems)
     out_ref[...] = jnp.zeros_like(out_ref)
     for owner in range(16):
         counts[owner] = owner * SLOTS
+    for wait in waits:
+        wait.wait()
 
     def move(row, carry):
         owner = owners[row]
@@ -412,11 +450,16 @@
         copy.wait()
 
 
-def owner_kernel(coef_ref, got_ref, out_ref):
+def owner_kernel(coef_ref, got_ref, out_hbm, out_ref, sems):
     coef = coef_ref[...]
     none = jnp.zeros_like(coef)
     square = jnp.concatenate([wide(coef, none), wide(none, coef)], axis=0)
     weights = jnp.concatenate(halves_of(square), axis=1)
+
+    def save(at):
+        part = pl.ds(at * 32 * LANES, 32 * LANES)
+        return pltpu.make_async_copy(out_ref.at[:, part], out_hbm.at[:, part], sems.at[at])
+
     for pack in range(8):
         pieces = []
         for pair in range(8 * pack, 8 * pack + 8):
@@ -434,6 +477,10 @@
         for at in range(8):
             pair = 8 * pack + at
             out_ref[:, pair * LANES : (pair + 1) * LANES] = grid[16 * at : 16 * at + 16]
+        if pack % 4 == 3:
+            save(pack // 4).start()
+    for at in range(2):
+        save(at).wait()
 
 
 def swap(shard, axis, bit):
@@ -479,24 +526,25 @@
     right_side = in_hbm(right_side)
     outcome = pl.pallas_call(
         field_kernel,
-        in_specs=[smem(), smem(), pl.BlockSpec(memory_space=pl.ANY)],
-        out_specs=[resident()] * 7,
-        out_shape=[PARTS, TURNED, NODE_ROWS] + [FACE] * 4,
-        scratch_shapes=[
-            pltpu.VMEM((GRID, RHS, STEP * BLOCK), F32),
-            pltpu.SemaphoreType.DMA((GRID,)),
-        ],
+        in_specs=[pl.BlockSpec(memory_space=pl.ANY)] * 3,
+        out_specs=[resident()] * 6,
+        out_shape=[FIELD, NODE_ROWS] + [FACE] * 4,
+        scratch_shapes=[pltpu.SemaphoreType.DMA((GRID,))] + tables((4, FACES), (1,)),
         compiler_params=params(8),
         cost_estimate=cost(1_000_000, 5_000_000),
         name="field",
     )(face_rows, odd, right_side)
-    field, turned, own_rows, faces = outcome[0], outcome[1], outcome[2], outcome[3:]
+    right_rows, own_rows, faces = outcome[0], outcome[1], outcome[2:]
     received = exchange(faces)
-    mats = pl.pallas_call(
+    mats, field, turned = pl.pallas_call(
         entries_kernel,
-        in_specs=[pl.BlockSpec(memory_space=pl.ANY)],
-        out_specs=resident(),
-        out_shape=jax.ShapeDtypeStruct((BLK_DEV, 2 * BLOCK, 4 * LANES), BF16),
+        in_specs=[pl.BlockSpec(memory_space=pl.ANY)] + [resident()] * 2,
+        out_specs=[resident()] * 3,
+        out_shape=[
+            jax.ShapeDtypeStruct((BLK_DEV, 2 * BLOCK, 4 * LANES), BF16),
+            PARTS,
+            TURNED,
+        ],
         scratch_shapes=[
             pltpu.VMEM((GRID, COUPLED, STEP, BLOCK * BLOCK), F32),
             pltpu.VMEM((COUPLED * 32 * STEP, LANES), F32),
@@ -505,17 +553,17 @@
         compiler_params=params(12),
         cost_estimate=cost(10_000_000, 16_000_000),
         name="entries",
-    )(entries)
+    )(entries, right_rows, own_rows)
     apply_scratch = [
         pltpu.VMEM((BLK_DEV + 4 * FACES, BLOCK, LANES), BF16),
         pltpu.VMEM((NODES_DEV, LANES), F32),
     ]
     outcome = pl.pallas_call(
         first_kernel,
-        in_specs=[smem(), smem(), smem()] + [resident()] * 7,
+        in_specs=[pl.BlockSpec(memory_space=pl.ANY)] * 3 + [resident()] * 7,
         out_specs=[resident()] * 6,
         out_shape=[PARTS, NODE_ROWS] + [FACE] * 4,
-        scratch_shapes=apply_scratch,
+        scratch_shapes=apply_scratch + tables((COUPLED - 1, BLK_DEV), (4, FACES), (1,)),
         compiler_params=params(8),
         cost_estimate=cost(1_000_000_000, 16_000_000),
         name="first_image",
@@ -534,10 +582,10 @@
     )(turned, field, image)
     outgoing = pl.pallas_call(
         relay_kernel,
-        in_specs=[smem(), smem(), resident()],
+        in_specs=[pl.BlockSpec(memory_space=pl.ANY)] * 2 + [resident()],
         out_specs=resident(),
         out_shape=jax.ShapeDtypeStruct((16 * SLOTS, LANES), F32),
-        scratch_shapes=[pltpu.SMEM((16,), jnp.int32)],
+        scratch_shapes=[pltpu.SMEM((16,), jnp.int32)] + tables((DIE_ROWS,), (DIE_ROWS,)),
         compiler_params=params(8),
         cost_estimate=cost(1_000_000, 10_000_000),
         name="relay_rows",
@@ -547,7 +595,9 @@
     ).reshape(16 * SLOTS, LANES)
     far_image, local_sums = pl.pallas_call(
         second_kernel,
-        in_specs=[smem(), smem()] + [resident()] * 9 + [pl.BlockSpec(memory_space=pl.ANY)],
+        in_specs=[pl.BlockSpec(memory_space=pl.ANY)] * 2
+        + [resident()] * 9
+        + [pl.BlockSpec(memory_space=pl.ANY)],
         out_specs=[far_memory(), resident()],
         out_shape=[
             pltpu.HBM(PARTS.shape, BF16),
@@ -558,7 +608,8 @@
             pltpu.VMEM(PARTS.shape, BF16),
             pltpu.VMEM((2 * LANES, LANES), F32),
             pltpu.SemaphoreType.DMA,
-        ],
+        ]
+        + tables((COUPLED - 1, BLK_DEV), (1,)),
         compiler_params=params(8),
         cost_estimate=cost(1_000_000_000, 14_000_000),
         name="second_image",
@@ -583,8 +634,12 @@
     mech_temps = pl.pallas_call(
         owner_kernel,
         in_specs=[resident()] * 2,
-        out_specs=resident(),
+        out_specs=far_memory(),
         out_shape=jax.ShapeDtypeStruct((16, SLOTS * RHS), F32),
+        scratch_shapes=[
+            pltpu.VMEM((16, SLOTS * RHS), F32),
+            pltpu.SemaphoreType.DMA((2,)),
+        ],
         compiler_params=params(8),
         cost_estimate=cost(100_000_000, 2_000_000),
         name="owner_rows",

time: 101 us -> 100 us (0.990)
  Pallas kernels: 35.5 us -> 34.2 us
    pallas_call x5, Pallas kernels: 17.5 us -> 16.2 us  [the longest x1 4.69 us: on_device(): pl.pallas_call(second_kernel, in_specs=[pl.BlockSpec(memory_space=pl.ANY)...]
where the time goes in v5:
time: 100 us; the launch traced here: 99.6 us
  blocking collectives  36.9 us (37%)
  Pallas kernels  34.2 us (34%)
  starting transfers between devices  24.8 us (25%)
  waiting for transfers between devices  2.69 us (3%)
    all_to_all x1, blocking collectives, total(): mine = jnp.sum(lax.all_to_all(parts, 'layer', 0, 0, tiled=True), axis=0)  13.4 us
    pallas_call x1, Pallas kernels, on_device(): pl.pallas_call(final_kernel, in_specs=[resident()] * 3 + [far_memory()],...  12.8 us
    all_to_all x1, blocking collectives, total(): mine = jnp.sum(lax.all_to_all(copies, 'region', 0, 0, tiled=True), axis=0)  12.6 us
    all_to_all x1, blocking collectives, total(): lax.all_to_all(copies, 'layer', 0, 0, tiled=True).reshape(LANES, LANES)  10.9 us
    ppermute x6, starting transfers between devices, swap(): lax.ppermute(shard, axis, [(i, i ^ bit) for i in range(lax.axis_size(axis...  10.6 us
    ppermute x2, starting transfers between devices, exchange(): outer = lax.ppermute(faces[3], 'layer', pairs + [(b, a) for a, b in pairs])  9.24 us
    all_to_all x1, starting transfers between devices, on_device(): lax.all_to_all(outgoing.reshape(16, SLOTS, LANES), 'layer', 0, 0, tiled=T...  4.9 us
    pallas_call x1, Pallas kernels, on_device(): pl.pallas_call(second_kernel, in_specs=[pl.BlockSpec(memory_space=pl.ANY)...  4.69 us
  transfers between devices with their start and end apart: 9, of which 1 were waited for; matrix products, arithmetic and copies ran while one was open for 0% of the time, Pallas kernels for 22%

profile of v5, /device:TPU:8, one launch (start us, length us, event | category | flops | bytes accessed | tf_op | source)
XLA Modules:
  0.0 99.6 jit_solution(9161346045514349100)
XLA Ops:
  0.6 2.1 %field.1 = (f32[64,4096]{1,0:T(8,128)S(1)}, f32[4096,128]{1,0:T(8,128)S(1)}, f32[256,128]{1,0:T(8,128)S(1)}, f32[256,128]{1,0:T(8,128)S(1)}, f32[256,128]{1,0:T(8,128)S(1)}, /*index=5*/f32[256,128]{1,0:T(8,128)S(1)}) custom-call(s32[4,8]{1,0:T(4,128)} %face_hbm.3, s32[1]{0:T(128)} %bitcast.1.odd_hbm, f32[64,4096]{1,0:T(8,128)} %right_hbm.1), custom_call_target="tpu_custom_call" | custom-call | flops 1000000 | bytes 5000000 | tf_op jit(solution)/shard_map/field/pallas_call | solution.py:527
  2.8 0.1 collective-permute-start
  2.9 7.3 %collective-permute-start.1 = (f32[256,128]{1,0:T(8,128)S(1)}, f32[256,128]{1,0:T(8,128)S(1)}, u32[]{:S(2)}, u32[]{:S(2)}) collective-permute-start(f32[256,128]{1,0:T(8,128)S(1)} %get-tuple-element.30), channel_id=1, source_target_pairs={{0,128},{16,144},{32,160},{48,176},{64,192},{80,208},{96,224},{112... | collective-permute-start | bytes 393224 | tf_op jit(solution)/shard_map/ppermute | solution.py:487
  10.2 0.4 collective-permute-start.2
  10.6 4.3 %collective-permute-start.3 = (f32[256,128]{1,0:T(8,128)S(1)}, f32[256,128]{1,0:T(8,128)S(1)}, u32[]{:S(2)}, u32[]{:S(2)}) collective-permute-start(f32[256,128]{1,0:T(8,128)S(1)} %get-tuple-element.32), channel_id=1, source_target_pairs={{1,2},{3,4},{5,6},{7,8},{9,10},{11,12},{13,14},{2,1},{4,3},{6,5},{... | collective-permute-start | bytes 393224 | tf_op jit(solution)/shard_map/ppermute | solution.py:497
  14.9 4.4 %entries.1 = (bf16[64,128,512]{2,1,0:T(8,128)(2,1)S(1)}, bf16[64,64,128]{2,1,0:T(8,128)(2,1)S(1)}, bf16[128,4096]{1,0:T(8,128)(2,1)S(1)}) custom-call(f32[7,64,4096]{2,1,0:T(8,128)} %bitcast.11, f32[64,4096]{1,0:T(8,128)S(1)} %get-tuple-element.25.right_ref, f32[4096,128]{1,0:T(8,128)S(1)} %get-tuple-element.26.nodes_ref.own_ref), custom_call_target="tpu_custom_call" | custom-call | flops 10000000 | bytes 16000000 | tf_op jit(solution)/shard_map/entries/pallas_call | solution.py:539
  19.4 0.0 collective-permute-done.near
  19.4 0.0 collective-permute-done.1.far
  19.4 0.0 collective-permute-done.2.inner
  19.4 0.0 collective-permute-done.3.outer
  19.4 3.7 %first_image.1 = (bf16[64,64,128]{2,1,0:T(8,128)(2,1)S(1)}, f32[4096,128]{1,0:T(8,128)S(1)}, f32[256,128]{1,0:T(8,128)S(1)}, f32[256,128]{1,0:T(8,128)S(1)}, f32...) custom-call(s32[6,64]{1,0:T(8,128)} %bitcast.12, s32[4,8]{1,0:T(4,128)} %face_hbm.3, s32[1]{0:T(128)} %bitcast.1.odd_hbm, ...), custom_call_target="tpu_custom_call" | custom-call | flops 1000000000 | bytes 16000000 | tf_op jit(solution)/shard_map/first_image/pallas_call | solution.py:561
  23.1 0.1 collective-permute-start.4
  23.2 2.7 %collective-permute-start.5 = (f32[256,128]{1,0:T(8,128)S(1)}, f32[256,128]{1,0:T(8,128)S(1)}, u32[]{:S(2)}, u32[]{:S(2)}) collective-permute-start(f32[256,128]{1,0:T(8,128)S(1)} %get-tuple-element.35), channel_id=1, source_target_pairs={{0,128},{16,144},{32,160},{48,176},{64,192},{80,208},{96,224},{112... | collective-permute-start | bytes 393224 | tf_op jit(solution)/shard_map/ppermute | solution.py:487
  25.9 0.0 collective-permute-start.6
  25.9 4.9 %collective-permute-start.7 = (f32[256,128]{1,0:T(8,128)S(1)}, f32[256,128]{1,0:T(8,128)S(1)}, u32[]{:S(2)}, u32[]{:S(2)}) collective-permute-start(f32[256,128]{1,0:T(8,128)S(1)} %get-tuple-element.37), channel_id=1, source_target_pairs={{1,2},{3,4},{5,6},{7,8},{9,10},{11,12},{13,14},{2,1},{4,3},{6,5},{... | collective-permute-start | bytes 393224 | tf_op jit(solution)/shard_map/ppermute | solution.py:497
  30.9 4.1 %relay_rows.1.outgoing_ref = f32[2048,128]{1,0:T(8,128)} custom-call(s32[512]{0:T(512)} %bitcast.14, s32[512]{0:T(512)} %node_hbm.1, f32[4096,128]{1,0:T(8,128)S(1)} %get-tuple-element.41.both_ref), custom_call_target="tpu_custom_call" | custom-call | flops 1000000 | bytes 10000000 | tf_op jit(solution)/shard_map/relay_rows/pallas_call | solution.py:583
  35.0 0.8 near_grams.1
  35.8 0.0 collective-permute-done.4.near
  35.8 0.0 collective-permute-done.5.far
  35.8 0.0 collective-permute-done.6.inner
  35.8 0.0 collective-permute-done.7.outer
  35.8 4.7 %second_image.1 = (bf16[64,64,128]{2,1,0:T(8,128)(2,1)}, f32[128,128]{1,0:T(8,128)S(1)}) custom-call(s32[6,64]{1,0:T(8,128)} %bitcast.13, s32[1]{0:T(128)} %bitcast.1.odd_hbm, bf16[64,128,512]{2,1,0:T(8,128)(2,1)S(1)} %get-tuple-element.27.mats_ref, bf16[64,64,128]{2,1,0:T(8,128)(2,1)S(1)} %get-tuple-element.33.image_ref.parts_ref, ...), custom_call_target="tpu_custom_call" | custom-call | flops 1000000000 | bytes 14000000 | tf_op jit(solution)/shard_map/second_image/pallas_call | solution.py:596
  40.5 13.4 %all_to_all.20 = f32[16,8,128]{2,1,0:T(8,128)S(1)} all-to-all(f32[16,8,128]{2,1,0:T(8,128)S(1)} %bitcast.10), channel_id=1, replica_groups=mesh['region'=16,'layer'=16] {'layer'}, dimensions={0} | all-to-all | bytes 131072 | tf_op jit(solution)/shard_map/all_to_all | solution.py:505
  54.0 12.6 %all_to_all.21 = f32[16,8,128]{2,1,0:T(8,128)S(1)} all-to-all(f32[16,8,128]{2,1,0:T(8,128)S(1)} %broadcast_in_dim.4), channel_id=1, replica_groups=mesh['region'=16,'layer'=16] {'region'}, dimensions={0} | all-to-all | bytes 131072 | tf_op jit(solution)/shard_map/all_to_all | solution.py:507
  66.6 10.9 %all_to_all.22 = f32[16,8,128]{2,1,0:T(8,128)S(1)} all-to-all(f32[16,8,128]{2,1,0:T(8,128)S(1)} %broadcast_in_dim.5), channel_id=1, replica_groups=mesh['region'=16,'layer'=16] {'layer'}, dimensions={0} | all-to-all | bytes 131072 | tf_op jit(solution)/shard_map/all_to_all | solution.py:509
  77.5 4.9 %all-to-all-start.3 = ((f32[16,128,128]{2,1,0:T(8,128)}), f32[16,128,128]{2,1,0:T(8,128)S(1)}, u32[]{:S(2)}, u32[]{:S(2)}) async-start(f32[16,128,128]{2,1,0:T(8,128)} %bitcast.6), calls=%async_computation.3 | async-start | bytes 2097152 | tf_op jit(solution)/shard_map/all_to_all | solution.py:593
  82.4 12.8 %final.1 = (f32[64,4096]{1,0:T(8,128)}, f32[64,4096]{1,0:T(8,128)}, f32[128,64]{1,0:T(8,128)S(1)}) custom-call(f32[128,128]{1,0:T(8,128)S(1)} %bitcast.9, bf16[128,4096]{1,0:T(8,128)(2,1)S(1)} %get-tuple-element.38.turned_ref, bf16[128,4096]{1,0:T(8,128)(2,1)S(1)} %get-tuple-element.39.image_turned_ref, bf16[64,64,128]{2,1,0:T(8,128)(2,1)} %get-tuple-element.43.far_hbm), custom_call_target="tpu_custom_call" | custom-call | flops 500000000 | bytes 8000000 | tf_op jit(solution)/shard_map/final/pallas_call | solution.py:618
  95.2 2.7 %all-to-all-done.3 = f32[16,128,128]{2,1,0:T(8,128)S(1)} async-done(((f32[16,128,128]{2,1,0:T(8,128)}), f32[16,128,128]{2,1,0:T(8,128)S(1)}, u32[]{:S(2)}, u32[]{:S(2)}) %all-to-all-start.3) | async-done | bytes 1048608 | tf_op jit(solution)/shard_map/all_to_all | solution.py:593
  97.9 1.6 %owner_rows.1 = f32[16,8192]{1,0:T(8,128)} custom-call(f32[128,64]{1,0:T(8,128)S(1)} %get-tuple-element.46.coef_ref, f32[2048,128]{1,0:T(8,128)S(1)} %bitcast.8), custom_call_target="tpu_custom_call" | custom-call | flops 100000000 | bytes 2000000 | tf_op jit(solution)/shard_map/owner_rows/pallas_call | solution.py:634
  (4 shorter events, 0.1 us)
Async XLA Ops:
  2.8 16.6 %collective-permute-start = (f32[256,128]{1,0:T(8,128)S(1)}, f32[256,128]{1,0:T(8,128)S(1)}, u32[]{:S(2)}, u32[]{:S(2)}) collective-permute-start(f32[256,128]{1,0:T(8,128)S(1)} %get-tuple-element.29), channel_id=1, source_target_pairs={{0,16},{16,0},{32,48},{48,32},{64,80},{80,64},{96,112},{112,96},{1... | collective-permute-start | bytes 393224 | tf_op jit(solution)/shard_map/ppermute | solution.py:487
  2.9 16.5 %collective-permute-start.1 = (f32[256,128]{1,0:T(8,128)S(1)}, f32[256,128]{1,0:T(8,128)S(1)}, u32[]{:S(2)}, u32[]{:S(2)}) collective-permute-start(f32[256,128]{1,0:T(8,128)S(1)} %get-tuple-element.30), channel_id=1, source_target_pairs={{0,128},{16,144},{32,160},{48,176},{64,192},{80,208},{96,224},{112... | collective-permute-start | bytes 393224 | tf_op jit(solution)/shard_map/ppermute | solution.py:487
  10.2 9.2 %collective-permute-start.2 = (f32[256,128]{1,0:T(8,128)S(1)}, f32[256,128]{1,0:T(8,128)S(1)}, u32[]{:S(2)}, u32[]{:S(2)}) collective-permute-start(f32[256,128]{1,0:T(8,128)S(1)} %get-tuple-element.31), channel_id=1, source_target_pairs={{0,1},{1,0},{2,3},{3,2},{4,5},{5,4},{6,7},{7,6},{8,9},{9,8},{10,11... | collective-permute-start | bytes 393224 | tf_op jit(solution)/shard_map/ppermute | solution.py:487
  10.6 8.8 %collective-permute-start.3 = (f32[256,128]{1,0:T(8,128)S(1)}, f32[256,128]{1,0:T(8,128)S(1)}, u32[]{:S(2)}, u32[]{:S(2)}) collective-permute-start(f32[256,128]{1,0:T(8,128)S(1)} %get-tuple-element.32), channel_id=1, source_target_pairs={{1,2},{3,4},{5,6},{7,8},{9,10},{11,12},{13,14},{2,1},{4,3},{6,5},{... | collective-permute-start | bytes 393224 | tf_op jit(solution)/shard_map/ppermute | solution.py:497
  23.1 12.7 %collective-permute-start.4 = (f32[256,128]{1,0:T(8,128)S(1)}, f32[256,128]{1,0:T(8,128)S(1)}, u32[]{:S(2)}, u32[]{:S(2)}) collective-permute-start(f32[256,128]{1,0:T(8,128)S(1)} %get-tuple-element.34), channel_id=1, source_target_pairs={{0,16},{16,0},{32,48},{48,32},{64,80},{80,64},{96,112},{112,96},{1... | collective-permute-start | bytes 393224 | tf_op jit(solution)/shard_map/ppermute | solution.py:487
  23.2 12.6 %collective-permute-start.5 = (f32[256,128]{1,0:T(8,128)S(1)}, f32[256,128]{1,0:T(8,128)S(1)}, u32[]{:S(2)}, u32[]{:S(2)}) collective-permute-start(f32[256,128]{1,0:T(8,128)S(1)} %get-tuple-element.35), channel_id=1, source_target_pairs={{0,128},{16,144},{32,160},{48,176},{64,192},{80,208},{96,224},{112... | collective-permute-start | bytes 393224 | tf_op jit(solution)/shard_map/ppermute | solution.py:487
  25.9 9.9 %collective-permute-start.6 = (f32[256,128]{1,0:T(8,128)S(1)}, f32[256,128]{1,0:T(8,128)S(1)}, u32[]{:S(2)}, u32[]{:S(2)}) collective-permute-start(f32[256,128]{1,0:T(8,128)S(1)} %get-tuple-element.36), channel_id=1, source_target_pairs={{0,1},{1,0},{2,3},{3,2},{4,5},{5,4},{6,7},{7,6},{8,9},{9,8},{10,11... | collective-permute-start | bytes 393224 | tf_op jit(solution)/shard_map/ppermute | solution.py:487
  25.9 9.9 %collective-permute-start.7 = (f32[256,128]{1,0:T(8,128)S(1)}, f32[256,128]{1,0:T(8,128)S(1)}, u32[]{:S(2)}, u32[]{:S(2)}) collective-permute-start(f32[256,128]{1,0:T(8,128)S(1)} %get-tuple-element.37), channel_id=1, source_target_pairs={{1,2},{3,4},{5,6},{7,8},{9,10},{11,12},{13,14},{2,1},{4,3},{6,5},{... | collective-permute-start | bytes 393224 | tf_op jit(solution)/shard_map/ppermute | solution.py:497
  77.5 20.3 %all-to-all-start.3 = ((f32[16,128,128]{2,1,0:T(8,128)}), f32[16,128,128]{2,1,0:T(8,128)S(1)}, u32[]{:S(2)}, u32[]{:S(2)}) async-start(f32[16,128,128]{2,1,0:T(8,128)} %bitcast.6), calls=%async_computation.3 | async-start | bytes 2097152 | tf_op jit(solution)/shard_map/all_to_all | solution.py:593

commit v6 on v5

--- a/solution.py
+++ b/solution.py
@@ -69,7 +69,7 @@
 
 
 def emit_faces(face_rows, odd, nodes_ref, face_refs):
-    for side, face_ref in zip((0, 1, 2 + odd[0], 3 - odd[0]), face_refs):
+    for side, face_ref in zip((1, 0, 2 + odd[0], 3 - odd[0]), face_refs):
         for face in range(FACES):
             start = pl.multiple_of(face_rows[side, face] * BLOCK, BLOCK)
             upper = nodes_ref[pl.ds(start, 32), :]
@@ -159,7 +159,7 @@
 
 def fill_extended(odd, received, extended_ref):
     half = left_lanes(32)
-    for side, got_ref in zip((0, 1, 3 - odd[0], 2 + odd[0]), received):
+    for side, got_ref in zip((1, 0, 3 - odd[0], 2 + odd[0]), received):
         for face in range(FACES):
             packed = got_ref[face * 32 : (face + 1) * 32, :]
             turned = pltpu.roll(packed, RHS, 1)
@@ -183,7 +183,7 @@
 
 
 def first_kernel(
-    neighbours_hbm, face_hbm, odd_hbm, mats_ref, parts_ref, own_ref, near, far, inner, outer,
+    neighbours_hbm, face_hbm, odd_hbm, mats_ref, parts_ref, own_ref, far, near, inner, outer,
     image_ref, both_ref, out0, out1, out2, out3, extended_ref, nodes_ref,
     neighbours, face_rows, odd, table_sems,
 ):
@@ -193,7 +193,7 @@
     own_extended(parts_ref, extended_ref)
     for wait in waits:
         wait.wait()
-    fill_extended(odd, (near, far, inner, outer), extended_ref)
+    fill_extended(odd, (far, near, inner, outer), extended_ref)
     for block in range(BLK_DEV):
         doubled = block_row(block, neighbours, mats_ref, extended_ref, nodes_ref)
         image_ref[block] = two_parts(doubled)
@@ -233,7 +233,7 @@
 
 
 def second_kernel(
-    neighbours_hbm, odd_hbm, mats_ref, parts_ref, near, far, inner, outer, turned_ref, image_turned_ref,
+    neighbours_hbm, odd_hbm, mats_ref, parts_ref, far, near, inner, outer, turned_ref, image_turned_ref,
     gram_ref, outgoing_ref, image_hbm, sums_ref, extended_ref, nodes_ref, image_ref, acc_ref, sem,
     neighbours, odd, table_sems,
 ):
@@ -241,17 +241,15 @@
     own_extended(parts_ref, extended_ref)
     for wait in waits:
         wait.wait()
-    fill_extended(odd, (near, far, inner, outer), extended_ref)
-    acc_ref[...] = jnp.zeros_like(acc_ref)
+    fill_extended(odd, (far, near, inner, outer), extended_ref)
     for block in range(BLK_DEV):
         doubled = block_row(block, neighbours, mats_ref, extended_ref, nodes_ref)
         image_ref[block] = two_parts(doubled)
     saving = pltpu.make_async_copy(image_ref, image_hbm, sem)
     saving.start()
-    for step in range(GRID):
-        columns = columns_of(step)
-        both = jnp.concatenate([turned_ref[:, columns], image_turned_ref[:, columns]], axis=0)
-        acc_ref[...] += product(both, rows_of(image_ref, step))
+    far_rows = image_ref[...].reshape(NODES_DEV, LANES)
+    acc_ref[:LANES] = product(turned_ref[...], far_rows)
+    acc_ref[LANES:] = product(image_turned_ref[...], far_rows)
     pack_sums(
         gram_ref[:RHS, :],
         gram_ref[RHS:LANES, :],
@@ -490,12 +488,12 @@
 def exchange(faces):
     count = lax.axis_size("layer")
     top = lax.axis_size("region") // 2
-    near = swap(faces[0], "region", 1)
-    far = swap(faces[1], "region", top)
+    far = swap(faces[0], "region", top)
+    near = swap(faces[1], "region", 1)
     inner = swap(faces[2], "layer", 1)
     pairs = [(i, i + 1) for i in range(1, count - 1, 2)]
     outer = lax.ppermute(faces[3], "layer", pairs + [(b, a) for a, b in pairs])
-    return near, far, inner, outer
+    return far, near, inner, outer
 
 
 def total(local):

time: 100 us -> 100 us (level)
  blocking collectives: 36.9 us -> 38.1 us
  transfers between devices with their start and end apart: 9 -> 9, of which waited for: 1 -> 2; matrix products, arithmetic and copies ran while one was open for 0% -> 0% of each run, Pallas kernels for 22% -> 22%
where the time goes in v6:
time: 100 us
  blocking collectives  38.1 us (38%)
  Pallas kernels  34 us (34%)
  starting transfers between devices  24 us (24%)
  waiting for transfers between devices  2.94 us (3%)
    all_to_all x1, blocking collectives, total(): mine = jnp.sum(lax.all_to_all(parts, 'layer', 0, 0, tiled=True), axis=0)  13.8 us
    all_to_all x1, blocking collectives, total(): mine = jnp.sum(lax.all_to_all(copies, 'region', 0, 0, tiled=True), axis=0)  13.3 us
    pallas_call x1, Pallas kernels, on_device(): pl.pallas_call(final_kernel, in_specs=[resident()] * 3 + [far_memory()],...  12.8 us
    all_to_all x1, blocking collectives, total(): lax.all_to_all(copies, 'layer', 0, 0, tiled=True).reshape(LANES, LANES)  10.9 us
    ppermute x6, starting transfers between devices, swap(): lax.ppermute(shard, axis, [(i, i ^ bit) for i in range(lax.axis_size(axis...  10.3 us
    ppermute x2, starting transfers between devices, exchange(): outer = lax.ppermute(faces[3], 'layer', pairs + [(b, a) for a, b in pairs])  8.79 us
    all_to_all x1, starting transfers between devices, on_device(): lax.all_to_all(outgoing.reshape(16, SLOTS, LANES), 'layer', 0, 0, tiled=T...  4.9 us
    pallas_call x1, Pallas kernels, on_device(): pl.pallas_call(second_kernel, in_specs=[pl.BlockSpec(memory_space=pl.ANY)...  4.54 us
  transfers between devices with their start and end apart: 9, of which 2 were waited for; matrix products, arithmetic and copies ran while one was open for 0% of the time, Pallas kernels for 22%

profile of v6, /device:TPU:8, one launch (start us, length us, event | category | flops | bytes accessed | tf_op | source)
XLA Modules:
  0.0 100.0 jit_solution(16666994946547778468)
XLA Ops:
  0.6 2.1 %field.1 = (f32[64,4096]{1,0:T(8,128)S(1)}, f32[4096,128]{1,0:T(8,128)S(1)}, f32[256,128]{1,0:T(8,128)S(1)}, f32[256,128]{1,0:T(8,128)S(1)}, f32[256,128]{1,0:T(8,128)S(1)}, /*index=5*/f32[256,128]{1,0:T(8,128)S(1)}) custom-call(s32[4,8]{1,0:T(4,128)} %face_hbm.3, s32[1]{0:T(128)} %bitcast.1.odd_hbm, f32[64,4096]{1,0:T(8,128)} %right_hbm.1), custom_call_target="tpu_custom_call" | custom-call | flops 1000000 | bytes 5000000 | tf_op jit(solution)/shard_map/field/pallas_call | solution.py:525
  2.8 7.3 %collective-permute-start = (f32[256,128]{1,0:T(8,128)S(1)}, f32[256,128]{1,0:T(8,128)S(1)}, u32[]{:S(2)}, u32[]{:S(2)}) collective-permute-start(f32[256,128]{1,0:T(8,128)S(1)} %get-tuple-element.29), channel_id=1, source_target_pairs={{0,128},{16,144},{32,160},{48,176},{64,192},{80,208},{96,224},{112... | collective-permute-start | bytes 393224 | tf_op jit(solution)/shard_map/ppermute | solution.py:485
  10.1 0.0 collective-permute-start.1
  10.1 0.4 collective-permute-start.2
  10.5 4.3 %collective-permute-start.3 = (f32[256,128]{1,0:T(8,128)S(1)}, f32[256,128]{1,0:T(8,128)S(1)}, u32[]{:S(2)}, u32[]{:S(2)}) collective-permute-start(f32[256,128]{1,0:T(8,128)S(1)} %get-tuple-element.32), channel_id=1, source_target_pairs={{1,2},{3,4},{5,6},{7,8},{9,10},{11,12},{13,14},{2,1},{4,3},{6,5},{... | collective-permute-start | bytes 393224 | tf_op jit(solution)/shard_map/ppermute | solution.py:495
  14.8 4.4 %entries.1 = (bf16[64,128,512]{2,1,0:T(8,128)(2,1)S(1)}, bf16[64,64,128]{2,1,0:T(8,128)(2,1)S(1)}, bf16[128,4096]{1,0:T(8,128)(2,1)S(1)}) custom-call(f32[7,64,4096]{2,1,0:T(8,128)} %bitcast.11, f32[64,4096]{1,0:T(8,128)S(1)} %get-tuple-element.25.right_ref, f32[4096,128]{1,0:T(8,128)S(1)} %get-tuple-element.26.nodes_ref.own_ref), custom_call_target="tpu_custom_call" | custom-call | flops 10000000 | bytes 16000000 | tf_op jit(solution)/shard_map/entries/pallas_call | solution.py:537
  19.3 0.0 collective-permute-done.far
  19.3 0.0 collective-permute-done.1.near
  19.3 0.0 collective-permute-done.2.inner
  19.3 0.0 collective-permute-done.3.outer
  19.3 3.7 %first_image.1 = (bf16[64,64,128]{2,1,0:T(8,128)(2,1)S(1)}, f32[4096,128]{1,0:T(8,128)S(1)}, f32[256,128]{1,0:T(8,128)S(1)}, f32[256,128]{1,0:T(8,128)S(1)}, f32...) custom-call(s32[6,64]{1,0:T(8,128)} %bitcast.12, s32[4,8]{1,0:T(4,128)} %face_hbm.3, s32[1]{0:T(128)} %bitcast.1.odd_hbm, ...), custom_call_target="tpu_custom_call" | custom-call | flops 1000000000 | bytes 16000000 | tf_op jit(solution)/shard_map/first_image/pallas_call | solution.py:559
  23.0 2.1 %collective-permute-start.4 = (f32[256,128]{1,0:T(8,128)S(1)}, f32[256,128]{1,0:T(8,128)S(1)}, u32[]{:S(2)}, u32[]{:S(2)}) collective-permute-start(f32[256,128]{1,0:T(8,128)S(1)} %get-tuple-element.34), channel_id=1, source_target_pairs={{0,128},{16,144},{32,160},{48,176},{64,192},{80,208},{96,224},{112... | collective-permute-start | bytes 393224 | tf_op jit(solution)/shard_map/ppermute | solution.py:485
  25.1 0.0 collective-permute-start.5
  25.1 0.4 collective-permute-start.6
  25.6 4.5 %collective-permute-start.7 = (f32[256,128]{1,0:T(8,128)S(1)}, f32[256,128]{1,0:T(8,128)S(1)}, u32[]{:S(2)}, u32[]{:S(2)}) collective-permute-start(f32[256,128]{1,0:T(8,128)S(1)} %get-tuple-element.37), channel_id=1, source_target_pairs={{1,2},{3,4},{5,6},{7,8},{9,10},{11,12},{13,14},{2,1},{4,3},{6,5},{... | collective-permute-start | bytes 393224 | tf_op jit(solution)/shard_map/ppermute | solution.py:495
  30.1 4.1 %relay_rows.1.outgoing_ref = f32[2048,128]{1,0:T(8,128)} custom-call(s32[512]{0:T(512)} %bitcast.14, s32[512]{0:T(512)} %node_hbm.1, f32[4096,128]{1,0:T(8,128)S(1)} %get-tuple-element.41.both_ref), custom_call_target="tpu_custom_call" | custom-call | flops 1000000 | bytes 10000000 | tf_op jit(solution)/shard_map/relay_rows/pallas_call | solution.py:581
  34.1 0.8 near_grams.1
  35.0 0.3 collective-permute-done.4.far
  35.2 0.0 collective-permute-done.5.near
  35.2 0.0 collective-permute-done.6.inner
  35.2 0.0 collective-permute-done.7.outer
  35.2 4.5 %second_image.1 = (bf16[64,64,128]{2,1,0:T(8,128)(2,1)}, f32[128,128]{1,0:T(8,128)S(1)}) custom-call(s32[6,64]{1,0:T(8,128)} %bitcast.13, s32[1]{0:T(128)} %bitcast.1.odd_hbm, bf16[64,128,512]{2,1,0:T(8,128)(2,1)S(1)} %get-tuple-element.27.mats_ref, bf16[64,64,128]{2,1,0:T(8,128)(2,1)S(1)} %get-tuple-element.33.image_ref.parts_ref, ...), custom_call_target="tpu_custom_call" | custom-call | flops 1000000000 | bytes 14000000 | tf_op jit(solution)/shard_map/second_image/pallas_call | solution.py:594
  39.8 13.8 %all_to_all.20 = f32[16,8,128]{2,1,0:T(8,128)S(1)} all-to-all(f32[16,8,128]{2,1,0:T(8,128)S(1)} %bitcast.10), channel_id=1, replica_groups=mesh['region'=16,'layer'=16] {'layer'}, dimensions={0} | all-to-all | bytes 131072 | tf_op jit(solution)/shard_map/all_to_all | solution.py:503
  53.7 13.3 %all_to_all.21 = f32[16,8,128]{2,1,0:T(8,128)S(1)} all-to-all(f32[16,8,128]{2,1,0:T(8,128)S(1)} %broadcast_in_dim.4), channel_id=1, replica_groups=mesh['region'=16,'layer'=16] {'region'}, dimensions={0} | all-to-all | bytes 131072 | tf_op jit(solution)/shard_map/all_to_all | solution.py:505
  67.0 10.9 %all_to_all.22 = f32[16,8,128]{2,1,0:T(8,128)S(1)} all-to-all(f32[16,8,128]{2,1,0:T(8,128)S(1)} %broadcast_in_dim.5), channel_id=1, replica_groups=mesh['region'=16,'layer'=16] {'layer'}, dimensions={0} | all-to-all | bytes 131072 | tf_op jit(solution)/shard_map/all_to_all | solution.py:507
  77.9 4.9 %all-to-all-start.3 = ((f32[16,128,128]{2,1,0:T(8,128)}), f32[16,128,128]{2,1,0:T(8,128)S(1)}, u32[]{:S(2)}, u32[]{:S(2)}) async-start(f32[16,128,128]{2,1,0:T(8,128)} %bitcast.6), calls=%async_computation.3 | async-start | bytes 2097152 | tf_op jit(solution)/shard_map/all_to_all | solution.py:591
  82.8 12.8 %final.1 = (f32[64,4096]{1,0:T(8,128)}, f32[64,4096]{1,0:T(8,128)}, f32[128,64]{1,0:T(8,128)S(1)}) custom-call(f32[128,128]{1,0:T(8,128)S(1)} %bitcast.9, bf16[128,4096]{1,0:T(8,128)(2,1)S(1)} %get-tuple-element.38.turned_ref, bf16[128,4096]{1,0:T(8,128)(2,1)S(1)} %get-tuple-element.39.image_turned_ref, bf16[64,64,128]{2,1,0:T(8,128)(2,1)} %get-tuple-element.43.far_hbm), custom_call_target="tpu_custom_call" | custom-call | flops 500000000 | bytes 8000000 | tf_op jit(solution)/shard_map/final/pallas_call | solution.py:616
  95.6 2.7 %all-to-all-done.3 = f32[16,128,128]{2,1,0:T(8,128)S(1)} async-done(((f32[16,128,128]{2,1,0:T(8,128)}), f32[16,128,128]{2,1,0:T(8,128)S(1)}, u32[]{:S(2)}, u32[]{:S(2)}) %all-to-all-start.3) | async-done | bytes 1048608 | tf_op jit(solution)/shard_map/all_to_all | solution.py:591
  98.2 1.6 %owner_rows.1 = f32[16,8192]{1,0:T(8,128)} custom-call(f32[128,64]{1,0:T(8,128)S(1)} %get-tuple-element.46.coef_ref, f32[2048,128]{1,0:T(8,128)S(1)} %bitcast.8), custom_call_target="tpu_custom_call" | custom-call | flops 100000000 | bytes 2000000 | tf_op jit(solution)/shard_map/owner_rows/pallas_call | solution.py:632
  (4 shorter events, 0.1 us)
Async XLA Ops:
  2.8 16.5 %collective-permute-start = (f32[256,128]{1,0:T(8,128)S(1)}, f32[256,128]{1,0:T(8,128)S(1)}, u32[]{:S(2)}, u32[]{:S(2)}) collective-permute-start(f32[256,128]{1,0:T(8,128)S(1)} %get-tuple-element.29), channel_id=1, source_target_pairs={{0,128},{16,144},{32,160},{48,176},{64,192},{80,208},{96,224},{112... | collective-permute-start | bytes 393224 | tf_op jit(solution)/shard_map/ppermute | solution.py:485
  10.1 9.2 %collective-permute-start.1 = (f32[256,128]{1,0:T(8,128)S(1)}, f32[256,128]{1,0:T(8,128)S(1)}, u32[]{:S(2)}, u32[]{:S(2)}) collective-permute-start(f32[256,128]{1,0:T(8,128)S(1)} %get-tuple-element.30), channel_id=1, source_target_pairs={{0,16},{16,0},{32,48},{48,32},{64,80},{80,64},{96,112},{112,96},{1... | collective-permute-start | bytes 393224 | tf_op jit(solution)/shard_map/ppermute | solution.py:485
  10.1 9.2 %collective-permute-start.2 = (f32[256,128]{1,0:T(8,128)S(1)}, f32[256,128]{1,0:T(8,128)S(1)}, u32[]{:S(2)}, u32[]{:S(2)}) collective-permute-start(f32[256,128]{1,0:T(8,128)S(1)} %get-tuple-element.31), channel_id=1, source_target_pairs={{0,1},{1,0},{2,3},{3,2},{4,5},{5,4},{6,7},{7,6},{8,9},{9,8},{10,11... | collective-permute-start | bytes 393224 | tf_op jit(solution)/shard_map/ppermute | solution.py:485
  10.5 8.8 %collective-permute-start.3 = (f32[256,128]{1,0:T(8,128)S(1)}, f32[256,128]{1,0:T(8,128)S(1)}, u32[]{:S(2)}, u32[]{:S(2)}) collective-permute-start(f32[256,128]{1,0:T(8,128)S(1)} %get-tuple-element.32), channel_id=1, source_target_pairs={{1,2},{3,4},{5,6},{7,8},{9,10},{11,12},{13,14},{2,1},{4,3},{6,5},{... | collective-permute-start | bytes 393224 | tf_op jit(solution)/shard_map/ppermute | solution.py:495
  23.0 12.2 %collective-permute-start.4 = (f32[256,128]{1,0:T(8,128)S(1)}, f32[256,128]{1,0:T(8,128)S(1)}, u32[]{:S(2)}, u32[]{:S(2)}) collective-permute-start(f32[256,128]{1,0:T(8,128)S(1)} %get-tuple-element.34), channel_id=1, source_target_pairs={{0,128},{16,144},{32,160},{48,176},{64,192},{80,208},{96,224},{112... | collective-permute-start | bytes 393224 | tf_op jit(solution)/shard_map/ppermute | solution.py:485
  25.1 10.1 %collective-permute-start.5 = (f32[256,128]{1,0:T(8,128)S(1)}, f32[256,128]{1,0:T(8,128)S(1)}, u32[]{:S(2)}, u32[]{:S(2)}) collective-permute-start(f32[256,128]{1,0:T(8,128)S(1)} %get-tuple-element.35), channel_id=1, source_target_pairs={{0,16},{16,0},{32,48},{48,32},{64,80},{80,64},{96,112},{112,96},{1... | collective-permute-start | bytes 393224 | tf_op jit(solution)/shard_map/ppermute | solution.py:485
  25.1 10.1 %collective-permute-start.6 = (f32[256,128]{1,0:T(8,128)S(1)}, f32[256,128]{1,0:T(8,128)S(1)}, u32[]{:S(2)}, u32[]{:S(2)}) collective-permute-start(f32[256,128]{1,0:T(8,128)S(1)} %get-tuple-element.36), channel_id=1, source_target_pairs={{0,1},{1,0},{2,3},{3,2},{4,5},{5,4},{6,7},{7,6},{8,9},{9,8},{10,11... | collective-permute-start | bytes 393224 | tf_op jit(solution)/shard_map/ppermute | solution.py:485
  25.6 9.7 %collective-permute-start.7 = (f32[256,128]{1,0:T(8,128)S(1)}, f32[256,128]{1,0:T(8,128)S(1)}, u32[]{:S(2)}, u32[]{:S(2)}) collective-permute-start(f32[256,128]{1,0:T(8,128)S(1)} %get-tuple-element.37), channel_id=1, source_target_pairs={{1,2},{3,4},{5,6},{7,8},{9,10},{11,12},{13,14},{2,1},{4,3},{6,5},{... | collective-permute-start | bytes 393224 | tf_op jit(solution)/shard_map/ppermute | solution.py:495
  77.9 20.3 %all-to-all-start.3 = ((f32[16,128,128]{2,1,0:T(8,128)}), f32[16,128,128]{2,1,0:T(8,128)S(1)}, u32[]{:S(2)}, u32[]{:S(2)}) async-start(f32[16,128,128]{2,1,0:T(8,128)} %bitcast.6), calls=%async_computation.3 | async-start | bytes 2097152 | tf_op jit(solution)/shard_map/all_to_all | solution.py:591
